TPU v7x, 512 devices: a whole 4x8x8 slice. The times are simulated.
512 devices in a mesh: clus: 64 (over x, z, core), samp: 8 (over y).
Axes of the slice: x: 4, y: 8, z: 8, core: 2. Of those that a mesh axis runs over, the one named last changes fastest.
Arguments:
- currents: bfloat16 [2048, 128, 128], P('clus'), may hold values from -6 to 6
- radiate: bfloat16 [2048, 2, 256, 128], P(('clus', 'samp')), may hold values from -0.375 to 0.375
- near_blocks: bfloat16 [2048, 10, 2, 128, 128], P(('clus', 'samp')), may hold values from -0.125 to 0.125
- near_cols: int32 [2048, 10], P(('clus', 'samp')), may hold values from 0 to 2047, as said below
- child_slot: int32 [2048], P('clus'), may hold values from 0 to 31, as said below
- interp: bfloat16 [2048, 256], P('samp'), may hold values from -0.375 to 0.375
- shift_angle: float32 [8, 2048], replicated, may hold values from -3.140625 to 3.140625
- far_dev: int32 [256, 16], P('clus'), may hold values from 0 to 63, all different within a row; in each aligned block of 4 rows (0 to 3, 4 to 7, ...) at most 2 rows name the same one
- far_loc: int32 [256, 16], P('clus'), may hold values from 0 to 3
- far_type: int32 [256, 16], P('clus'), may hold values from 0 to 63
- transl: bfloat16 [64, 2, 2048], P(None, None, 'samp'), may hold values from -0.25 to 0.25
Outputs:
- field: bfloat16 [2048, 128, 128], P(('clus', 'samp'))
Inputs may be any that keep to these rules, and one draw needn't show every extreme that they name: `near_cols`: row c holds 10 different clusters, the first being c itself; all lie between g * 32 - 8 and (g + 1) * 32 + 7 for g = c // 32. `child_slot`: each aligned block of 32 entries is a permutation of 0 to 31, so every coarser cluster has eight children, one in each octant. `far_dev`: A row names 16 different values; among the 4 rows of one index of clus no value is named by more than 2 rows, a bound that some block reaches.
All inputs are finite; a program needn't handle non-finite values.
Results may differ from a plain program's by a relative error of at most 0.0071.
Values may be sent and summed in bfloat16 or wider, within the bound.
No kernel may reach another device: no remote copies, remote signals or barrier semaphores. Data moves between devices by JAX's collectives and lax.ppermute only.
A program may use at most 128 MiB of HBM per device.

v0:
```python
import jax
import jax.numpy as jnp
from jax import lax
from jax.sharding import PartitionSpec as P

CAP = 2


def padded(block, sides, width):
    for axis, dim in sides:
        count = lax.axis_size(axis)
        forward = [(i, i + 1) for i in range(count - 1)]
        backward = [(target, source) for source, target in forward]
        low = lax.ppermute(
            lax.slice_in_dim(block, block.shape[dim] - width, None, axis=dim), axis, forward
        )
        high = lax.ppermute(lax.slice_in_dim(block, 0, width, axis=dim), axis, backward)
        block = jnp.concatenate([low, block, high], axis=dim)
    return block


def combine_parts(with_real, with_imag, sign):
    half_width = with_real.shape[-1] // 2
    real_part = with_real[..., :half_width] - sign * with_imag[..., half_width:]
    imag_part = with_real[..., half_width:] + sign * with_imag[..., :half_width]
    return jnp.concatenate([real_part, imag_part], axis=-1)


def rotate_parts(values, cosine, sine_part):
    half_width = values.shape[-1] // 2
    real_in = values[..., :half_width]
    imag_in = values[..., half_width:]
    cosine = cosine[..., None]
    sine_part = sine_part[..., None]
    return jnp.concatenate(
        [real_in * cosine - imag_in * sine_part, real_in * sine_part + imag_in * cosine], axis=-1
    )


def octant_rows(slot_ids, lookup_table):
    onehot = (slot_ids[:, None] % 8 == jnp.arange(8, dtype=jnp.int32)[None, :]).astype(jnp.float32)
    return jnp.dot(onehot, lookup_table, precision=lax.Precision.HIGHEST)


def slot_ranks(source_ids, clus_count):
    onehot = (source_ids[..., None] == jnp.arange(clus_count, dtype=jnp.int32)).astype(jnp.int32)
    before = jnp.cumsum(onehot, axis=-2) - onehot
    return jnp.sum(before * onehot, axis=-1)


def body(
    currents,
    radiate,
    near_blocks,
    near_cols,
    child_slot,
    interp,
    shift_angle,
    far_dev,
    far_loc,
    far_type,
    transl,
):
    group_size = currents.shape[0]
    own_count = radiate.shape[0]
    width_pair = currents.shape[2]
    half_pair = width_pair // 2
    samp_index = lax.axis_index("samp")
    clus_index = lax.axis_index("clus")
    clus_count = lax.axis_size("clus")
    own_start = samp_index * own_count
    own_currents = lax.dynamic_slice_in_dim(currents, own_start, own_count, 0)
    parents_here = far_dev.shape[0]
    list_len = far_dev.shape[1]
    slice_len = interp.shape[0]
    sample_start = samp_index * slice_len
    cosine_all = jnp.cos(shift_angle)
    sine_all = jnp.sin(shift_angle)
    cosine_own = lax.dynamic_slice_in_dim(cosine_all, sample_start, slice_len, 1)
    sine_own = lax.dynamic_slice_in_dim(sine_all, sample_start, slice_len, 1)
    with_real = jnp.einsum(
        "ckb,cbr->ckr", radiate[:, 0], own_currents, preferred_element_type=jnp.float32
    )
    with_imag = jnp.einsum(
        "ckb,cbr->ckr", radiate[:, 1], own_currents, preferred_element_type=jnp.float32
    )
    rad_child = combine_parts(with_real, with_imag, 1.0).astype(jnp.bfloat16)
    slot_ids = child_slot
    lifted = jnp.einsum(
        "kj,cjr->ckr",
        interp,
        lax.all_gather(rad_child, "samp", axis=0, tiled=True),
        preferred_element_type=jnp.float32,
    )
    rotated = rotate_parts(
        lifted, octant_rows(slot_ids, cosine_own), octant_rows(slot_ids, sine_own)
    )
    owners = (slot_ids[:, None] // 8 == jnp.arange(parents_here, dtype=jnp.int32)[None, :]).astype(
        jnp.float32
    )
    rad_parent = jnp.einsum("cp,ckr->pkr", owners, rotated, precision=lax.Precision.HIGHEST).astype(
        jnp.bfloat16
    )
    entries = parents_here * list_len
    sources = far_dev.reshape(entries)
    local_ids = far_loc.reshape(entries)
    rank_ids = slot_ranks(sources, clus_count)
    flat_slot = sources * CAP + rank_ids
    requests = (
        jnp.zeros((clus_count * CAP,), jnp.int32)
        .at[flat_slot]
        .set(local_ids)
        .reshape(clus_count, CAP)
    )
    asked_ids = lax.all_to_all(requests, "clus", split_axis=0, concat_axis=0, tiled=True)
    outgoing = rad_parent[asked_ids]
    arrived = lax.all_to_all(outgoing, "clus", split_axis=0, concat_axis=0, tiled=True)
    picked = arrived.reshape(clus_count * CAP, slice_len, width_pair)[sources * CAP + rank_ids]
    picked = picked.reshape(parents_here, list_len, slice_len, width_pair)
    type_count = transl.shape[0]
    type_onehot = (
        far_type.reshape(entries)[:, None] == jnp.arange(type_count, dtype=jnp.int32)[None, :]
    ).astype(jnp.float32)
    operators = jnp.dot(
        type_onehot,
        transl.reshape(type_count, 2 * slice_len).astype(jnp.float32),
        precision=lax.Precision.HIGHEST,
    )
    operators = operators.reshape(parents_here, list_len, 2, slice_len)
    cosine_op = operators[:, :, 0][..., None]
    sine_op = operators[:, :, 1][..., None]
    real_in = picked[..., :half_pair].astype(jnp.float32)
    imag_in = picked[..., half_pair:].astype(jnp.float32)
    real_sum = jnp.sum(real_in * cosine_op - imag_in * sine_op, axis=1)
    imag_sum = jnp.sum(real_in * sine_op + imag_in * cosine_op, axis=1)
    incoming = jnp.concatenate([real_sum, imag_sum], axis=-1).astype(jnp.bfloat16)
    slot_ids = child_slot
    chosen = incoming[slot_ids // 8].astype(jnp.float32)
    phased = rotate_parts(
        chosen, octant_rows(slot_ids, cosine_own), -octant_rows(slot_ids, sine_own)
    ).astype(jnp.bfloat16)
    child_in = lax.psum_scatter(
        jnp.einsum("kj,ckr->cjr", interp, phased, preferred_element_type=jnp.float32),
        "samp",
        scatter_dimension=0,
        tiled=True,
    ).astype(jnp.bfloat16)
    back_real = jnp.einsum(
        "ckb,ckr->cbr", radiate[:, 0], child_in, preferred_element_type=jnp.float32
    )
    back_imag = jnp.einsum(
        "ckb,ckr->cbr", radiate[:, 1], child_in, preferred_element_type=jnp.float32
    )
    far_part = combine_parts(back_real, back_imag, -1.0)
    margin = group_size // 4
    window = padded(currents, (("clus", 0),), margin)
    local_cols = near_cols - (clus_index * group_size - margin)
    neighbours = window[local_cols]
    near_real = jnp.einsum(
        "cjab,cjbr->car", near_blocks[:, :, 0], neighbours, preferred_element_type=jnp.float32
    )
    near_imag = jnp.einsum(
        "cjab,cjbr->car", near_blocks[:, :, 1], neighbours, preferred_element_type=jnp.float32
    )
    near_part = combine_parts(near_real, near_imag, 1.0)
    return (near_part + far_part).astype(jnp.bfloat16)


def solution(mesh):
    in_specs = (
        P("clus", None, None),
        P(("clus", "samp"), None, None, None),
        P(("clus", "samp"), None, None, None, None),
        P(("clus", "samp"), None),
        P("clus"),
        P("samp", None),
        P(),
        P("clus", None),
        P("clus", None),
        P("clus", None),
        P(None, None, "samp"),
    )
    out_specs = P(("clus", "samp"), None, None)
    return jax.shard_map(body, mesh=mesh, in_specs=in_specs, out_specs=out_specs, check_vma=False)
```

profile of v0, /device:TPU:1, one launch (start us, length us, event | category | flops | bytes accessed | tf_op | source)
XLA Modules:
  0.0 363.7 jit_solution(14303523392793757161)
XLA Ops:
  6.5 1.3 convolution_bitcast_fusion.2
  7.9 1.3 convolution_bitcast_fusion.3
  9.2 0.1 fusion.20
  9.3 0.8 copy.46
  10.2 0.1 eq.102
  10.3 0.1 reduce_window_sum.11
  10.6 0.2 select_reduce_fusion
  10.8 0.8 scatter_custom_fusion
  11.6 0.8 all_to_all.11
  12.4 14.8 %all-to-all-start = ((s32[64,1,2]{2,1,0:T(1,128)}), s32[64,1,2]{2,1,0:T(1,128)S(1)}, u32[]{:S(2)}, u32[]{:S(2)}) async-start(s32[64,1,2]{2,1,0:T(1,128)} %bitcast.20), calls=%async_computation | async-start | bytes 65536 | tf_op jit(solution)/shard_map/all_to_all | solution.py:115
  27.2 0.9 fusion.64
  28.1 0.9 fusion.45
  29.0 7.4 %all-to-all-done = s32[64,1,2]{2,1,0:T(1,128)S(1)} async-done(((s32[64,1,2]{2,1,0:T(1,128)}), s32[64,1,2]{2,1,0:T(1,128)S(1)}, u32[]{:S(2)}, u32[]{:S(2)}) %all-to-all-start) | async-done | bytes 544 | tf_op jit(solution)/shard_map/all_to_all | solution.py:115
  36.5 0.1 copy.51
  36.6 0.1 reshape.143
  36.8 18.3 %all-gather.2.cloned.1.call-done = bf16[32,256,128]{2,1,0:T(8,128)(2,1)} async-done(((bf16[4,256,128]{2,1,0:T(8,128)(2,1)}), bf16[32,256,128]{2,1,0:T(8,128)(2,1)}) %all-gather.2.cloned.1.call-update) | async-done | bytes 2097168 | tf_op jit(solution)/shard_map/all_gather | solution.py:92
  55.0 2.3 convolution_bitcast_fusion.1
  57.4 0.6 multiply_subtract_fusion
  58.0 2.2 pad_maximum_fusion
  60.2 5.5 %copy.48 = f32[32,256,128]{2,0,1:T(8,128)} copy(f32[32,256,128]{1,2,0:T(8,128)} %pad_maximum_fusion) | data formatting | bytes 8388608 | tf_op jit(solution)/shard_map/concatenate | solution.py:35
  65.8 3.6 convolution_convert_fusion
  69.4 6.4 %gather_fusion.1 = bf16[128,256,128]{2,1,0:T(8,128)(2,1)} fusion(bf16[4,256,128]{2,1,0:T(8,128)(2,1)S(1)} %copy.52, s32[1024]{0:T(1024)S(1)} %pad_clamp_fusion.2), kind=kCustom, calls=%fused_computation.1 | custom fusion | bytes 16777728 | tf_op jit(solution)/shard_map/gather | solution.py:116
  75.8 15.6 %all-to-all-start.1 = ((bf16[64,2,256,128]{3,2,1,0:T(8,128)(2,1)}), bf16[64,2,256,128]{3,2,1,0:T(8,128)(2,1)}, u32[]{:S(2)}, u32[]{:S(2)}) async-start(bf16[64,2,256,128]{3,2,1,0:T(8,128)(2,1)} %bitcast.102), calls=%async_computation.1 | async-start | bytes 16777216 | tf_op jit(solution)/shard_map/all_to_all | solution.py:117
  91.4 0.2 reduce-scatter.2.cloned.1.call-start
  91.7 0.2 fusion.38
  91.9 185.2 %all-to-all-done.1 = bf16[64,2,256,128]{3,2,1,0:T(8,128)(2,1)} async-done(((bf16[64,2,256,128]{3,2,1,0:T(8,128)(2,1)}), bf16[64,2,256,128]{3,2,1,0:T(8,128)(2,1)}, u32[]{:S(2)}, u32[]{:S(2)}) %all-to-all-start.1) | async-done | bytes 8388640 | tf_op jit(solution)/shard_map/all_to_all | solution.py:117
  277.1 6.4 %gather_fusion.2 = bf16[64,256,128]{2,1,0:T(8,128)(2,1)} fusion(bf16[128,256,128]{2,1,0:T(8,128)(2,1)} %bitcast.23, s32[1024]{0:T(1024)S(1)} %pad_clamp_fusion.1), kind=kCustom, calls=%fused_computation.2 | custom fusion | bytes 8388864 | tf_op jit(solution)/shard_map/gather | solution.py:118
  283.6 9.0 %fusion.1 = (bf16[4,256,64]{2,1,0:T(8,128)(2,1)S(1)}, bf16[4,256,64]{2,1,0:T(8,128)(2,1)S(1)}) fusion(f32[4,16,256]{2,1,0:T(8,128)S(1)} %get-tuple-element.22, f32[4,16,256]{2,1,0:T(8,128)S(1)} %get-tuple-element.21, bf16[4,16,256,128]{3,2,1,0:T(8,128)(2,1)} %bitcast.101), kind=kLoop, calls=%fused_computation.10 | loop fusion | flops 10354688 | bytes 4587520 | tf_op jit(solution)/shard_map/reduce_sum | solution.py:134
  292.6 0.1 pad_maximum_fusion.3
  292.7 2.1 gather_fusion.3
  294.9 3.3 copy.54
  298.1 0.5 convert_element_type.35
  298.7 0.8 subtract_convert_fusion
  299.5 2.7 convolution_bitcast_fusion
  302.2 1.2 copy-done.1
  303.4 1.9 collective-permute-start
  305.4 2.4 collective-permute-start.1
  307.9 0.7 collective-permute-done
  308.7 4.8 %collective-permute-done.1 = bf16[8,128,128]{2,1,0:T(8,128)(2,1)S(1)} collective-permute-done((bf16[8,128,128]{2,1,0:T(8,128)(2,1)S(1)}, bf16[8,128,128]{2,1,0:T(8,128)(2,1)S(1)}, u32[]{:S(2)}, u32[]{:S(2)}) %collective-permute-start.1) | collective-permute-done | bytes 262176 | tf_op jit(solution)/shard_map/ppermute | solution.py:17
  313.5 0.2 pad_maximum_fusion.1
  313.7 0.8 gather_fusion
  314.5 2.1 fusion.13
  316.5 0.1 copy-done.9
  316.7 0.6 fusion.16
  317.3 36.2 %reduce-scatter.2.cloned.1.call-done = f32[4,256,128]{1,2,0:T(8,128)} async-done(((f32[32,256,128]{1,2,0:T(8,128)}), f32[4,256,128]{1,2,0:T(8,128)}) %reduce-scatter.2.cloned.1.call-update) | async-done | bytes 524304 | tf_op jit(solution)/shard_map/reduce_scatter | solution.py:142
  353.5 1.3 convolution_bitcast_fusion.4
  354.8 1.3 convolution_bitcast_fusion.5
  356.1 0.8 copy.55
  (42 shorter events, 0.7 us)
Async XLA Ops:
  6.5 48.5 %copy-start = (bf16[256,256]{1,0:T(8,128)(2,1)S(1)}, bf16[256,256]{1,0:T(8,128)(2,1)}, u32[]{:S(2)}) copy-start(bf16[256,256]{1,0:T(8,128)(2,1)} %param.16) | copy-start | bytes 393220
  6.5 48.5 %all-gather.2.cloned.1.call-start = ((), (), s32[]{:S(2)}) async-start(), calls=%async_computation.3 | async-start | bytes 2359296 | tf_op jit(solution)/shard_map/all_gather | solution.py:92
  6.5 3.6 %copy-start.4 = (s32[4,16]{1,0:T(4,128)S(1)}, s32[4,16]{1,0:T(4,128)}, u32[]{:S(2)}) copy-start(s32[4,16]{1,0:T(4,128)} %param.18) | copy-start | bytes 772
  6.5 4.0 %copy-start.6 = (s32[4,16]{1,0:T(4,128)S(1)}, s32[4,16]{1,0:T(4,128)}, u32[]{:S(2)}) copy-start(s32[4,16]{1,0:T(4,128)} %param.19) | copy-start | bytes 772
  7.9 19.3 %copy-start.8 = (s32[32]{0:T(128)S(1)}, s32[32]{0:T(128)}, u32[]{:S(2)}) copy-start(s32[32]{0:T(128)} %param.15) | copy-start | bytes 388
  12.4 24.1 %all-to-all-start = ((s32[64,1,2]{2,1,0:T(1,128)}), s32[64,1,2]{2,1,0:T(1,128)S(1)}, u32[]{:S(2)}, u32[]{:S(2)}) async-start(s32[64,1,2]{2,1,0:T(1,128)} %bitcast.20), calls=%async_computation | async-start | bytes 65536 | tf_op jit(solution)/shard_map/all_to_all | solution.py:115
  75.8 15.8 %copy-start.3 = (bf16[64,2,256]{2,1,0:T(2,128)(2,1)S(1)}, bf16[64,2,256]{2,1,0:T(2,128)(2,1)}, u32[]{:S(2)}) copy-start(bf16[64,2,256]{2,1,0:T(2,128)(2,1)} %param.21) | copy-start | bytes 196612
  75.8 15.8 %copy-start.5 = (s32[4,16]{1,0:T(4,128)S(1)}, s32[4,16]{1,0:T(4,128)}, u32[]{:S(2)}) copy-start(s32[4,16]{1,0:T(4,128)} %param.20) | copy-start | bytes 772
  75.8 201.3 %all-to-all-start.1 = ((bf16[64,2,256,128]{3,2,1,0:T(8,128)(2,1)}), bf16[64,2,256,128]{3,2,1,0:T(8,128)(2,1)}, u32[]{:S(2)}, u32[]{:S(2)}) async-start(bf16[64,2,256,128]{3,2,1,0:T(8,128)(2,1)} %bitcast.102), calls=%async_computation.1 | async-start | bytes 16777216 | tf_op jit(solution)/shard_map/all_to_all | solution.py:117
  91.4 262.1 %reduce-scatter.2.cloned.1.call-start = ((), (), s32[]{:S(2)}) async-start(), calls=%async_computation.4 | async-start | bytes 4718592 | tf_op jit(solution)/shard_map/reduce_scatter | solution.py:142
  302.2 1.2 copy-start.1
  302.2 5.6 %copy-start.7 = (s32[4,10]{1,0:T(4,128)S(1)}, s32[4,10]{1,0:T(4,128)}, u32[]{:S(2)}) copy-start(s32[4,10]{1,0:T(4,128)} %param.14) | copy-start | bytes 484
  303.4 5.2 %collective-permute-start = (bf16[8,128,128]{2,1,0:T(8,128)(2,1)S(1)}, bf16[8,128,128]{2,1,0:T(8,128)(2,1)S(1)}, u32[]{:S(2)}, u32[]{:S(2)}) collective-permute-start(bf16[8,128,128]{2,1,0:T(8,128)(2,1)S(1)} %get-tuple-element.15), channel_id=1, source_target_pairs={{0,8},{8,16},{16,24},{24,32},{32,40},{40,48},{48,56},{56,64},{64,7... | collective-permute-start | bytes 786440 | tf_op jit(solution)/shard_map/ppermute | solution.py:14
  305.4 8.1 %collective-permute-start.1 = (bf16[8,128,128]{2,1,0:T(8,128)(2,1)S(1)}, bf16[8,128,128]{2,1,0:T(8,128)(2,1)S(1)}, u32[]{:S(2)}, u32[]{:S(2)}) collective-permute-start(bf16[8,128,128]{2,1,0:T(8,128)(2,1)S(1)} %get-tuple-element.16), channel_id=1, source_target_pairs={{8,0},{16,8},{24,16},{32,24},{40,32},{48,40},{56,48},{64,56},{72,6... | collective-permute-start | bytes 786440 | tf_op jit(solution)/shard_map/ppermute | solution.py:17
  314.5 2.2 copy-start.9
  316.7 36.9 %copy-start.2 = (bf16[4,2,256,128]{3,2,1,0:T(8,128)(2,1)S(1)}, bf16[4,2,256,128]{3,2,1,0:T(8,128)(2,1)}, u32[]{:S(2)}) copy-start(bf16[4,2,256,128]{3,2,1,0:T(8,128)(2,1)} %param.12) | copy-start | bytes 1572868
Sparse Core Ops, SparseCore 0:
  10.3 44.6 all-gather.1
  302.3 51.1 reduce-scatter.1
where the time goes:
time: 365 us; the launch traced here: 364 us
  waiting for transfers between devices  253 us (69%)
  starting transfers between devices  34.9 us (10%)
  local copies, waits for them, and re-layouts  29.8 us (8%)
  matrix products  18.4 us (5%)
  other arithmetic  14.1 us (4%)
  between operations  13.8 us (4%)
    all_to_all x1, waiting for transfers between devices, body(): lax.all_to_all(outgoing, 'clus', split_axis=0, concat_axis=0, tiled=True)  185 us
    reduce_scatter x1, waiting for transfers between devices, body(): lax.psum_scatter(jnp.einsum('kj,ckr->cjr', interp, phased, preferred_elem...  36.2 us
    all_gather x1, waiting for transfers between devices, body(): lax.all_gather(rad_child, 'samp', axis=0, tiled=True)  18.3 us
    all_to_all x1, starting transfers between devices, body(): lax.all_to_all(outgoing, 'clus', split_axis=0, concat_axis=0, tiled=True)  15.6 us
    all_to_all x1, starting transfers between devices, body(): lax.all_to_all(requests, 'clus', split_axis=0, concat_axis=0, tiled=True)  14.8 us
    reduce_sum x1, other arithmetic, body(): real_sum = jnp.sum(real_in * cosine_op - imag_in * sine_op, axis=1)  9 us
    all_to_all x1, waiting for transfers between devices, body(): lax.all_to_all(requests, 'clus', split_axis=0, concat_axis=0, tiled=True)  7.39 us
  transfers between devices with their start and end apart: 6, of which 6 were waited for; matrix products, arithmetic and copies ran while one was open for 2% of the time, Pallas kernels for 0%

commit v1 on v0

v1 whole, which is shorter than its diff:
```python
import jax
import jax.numpy as jnp
from jax import lax
from jax.experimental import pallas as pl
from jax.experimental.pallas import tpu as pltpu
from jax.sharding import PartitionSpec as P

BF = jnp.bfloat16
F32 = jnp.float32
VMEM_LIMIT = 60 * 1024 * 1024
VM = pl.BlockSpec(memory_space=pltpu.VMEM)
SM = pl.BlockSpec(memory_space=pltpu.SMEM)


def nt_dot(a, b):
    return lax.dot_general(a, b, (((1,), (1,)), ((), ())), preferred_element_type=F32)


def nn_dot(a, b):
    return lax.dot_general(a, b, (((1,), (0,)), ((), ())), preferred_element_type=F32)


def tn_dot(a, b):
    return lax.dot_general(a, b, (((0,), (0,)), ((), ())), preferred_element_type=F32)


def rows_of(shape, dim):
    return lax.broadcasted_iota(jnp.int32, shape, dim)


def radiate_kernel(ids, cur, rad, itp, tra, lists, out):
    trow = tra[0].astype(F32)
    row = rows_of((8, 256), 0)
    extra = jnp.where(row == 0, trow[0:1], jnp.where(row == 1, trow[1:2], lists[...]))
    extra = extra.astype(BF)
    for s in range(8):
        out[s, 64:192, :] = itp[...]
        out[s, 192:200, :] = extra
    for c in range(4):
        values = cur[c].astype(F32).T.astype(BF)
        with_real = nt_dot(values, rad[c, 0])
        with_imag = nt_dot(values, rad[c, 1])
        real = with_real[:64] - with_imag[64:]
        imag = with_real[64:] + with_imag[:64]
        for s in range(8):
            both = jnp.concatenate([real[8 * s : 8 * s + 8], imag[8 * s : 8 * s + 8]], axis=0)
            out[s, 16 * c : 16 * c + 16, :] = both.astype(BF)


def lift_kernel(slots, ids, got, other, cosine, sine, out, whole, lhs, inverse):
    core = ids[0]

    def note(c, carry):
        inverse[slots[c]] = c
        return carry

    lax.fori_loop(0, 32, note, 0)

    def collect(n, carry):
        c = inverse[n]
        src = pl.multiple_of(lax.rem(c, 4) * 16, 16)
        dst = pl.multiple_of(n * 16, 16)
        lhs[pl.ds(dst, 16), :] = got[lax.div(c, 4), pl.ds(src, 16), :]
        return carry

    lax.fori_loop(0, 32, collect, 0)
    mine = pl.multiple_of(core * 128, 128)
    theirs = pl.multiple_of((1 - core) * 128, 128)
    for s in range(8):
        whole[s, pl.ds(mine, 128), :] = got[s, 64:192, :]
        whole[s, pl.ds(theirs, 128), :] = other[s]

    def step(k, carry):
        lanes = pl.ds(pl.multiple_of(k * 256, 256), 256)
        cos = cosine[:, lanes]
        sin = sine[:, lanes]
        for p in range(4):
            lifted = nt_dot(lhs[128 * p : 128 * p + 128, :], whole[k])
            real_sum = imag_sum = None
            for o in range(8):
                re = lifted[16 * o : 16 * o + 8]
                im = lifted[16 * o + 8 : 16 * o + 16]
                co, si = cos[o : o + 1], sin[o : o + 1]
                real = re * co - im * si
                imag = re * si + im * co
                real_sum = real if real_sum is None else real_sum + real
                imag_sum = imag if imag_sum is None else imag_sum + imag
            parts = (real_sum, imag_sum)
            if p == 0:
                reals, imags = [], []
            reals.append(parts[0])
            imags.append(parts[1])
        block = jnp.stack(reals + imags, axis=0)
        block = jnp.swapaxes(block, 0, 1)
        extra = got[k, 192:208, :].astype(F32)[0:8]
        extra = jnp.broadcast_to(extra[None], (8, 8, 256))
        both = jnp.concatenate([block, extra], axis=1).astype(BF)
        for r in range(8):
            out[r // 2, k, r % 2] = both[r]
        return carry

    lax.fori_loop(0, 8, step, 0)


def translate_kernel(got, out, table, tran, codes, real_acc, imag_acc):
    table[...] = got[:, 0:8, :].reshape(512, 256)
    tran[...] = got[:, 8:16, :].reshape(512, 256)
    row = rows_of((256, 512), 0)
    col = rows_of((256, 512), 1)
    pick = (col == (lax.shift_right_logical(row, 2) * 8 + 2 + (row & 3))).astype(F32).astype(BF)
    listed = nn_dot(pick, tran[:, 0:128])
    codes[...] = listed.astype(jnp.int32)
    real_acc[...] = jnp.zeros_like(real_acc)
    imag_acc[...] = jnp.zeros_like(imag_acc)
    for f in range(16):
        code = codes[:, f : f + 1]
        src = code + lax.shift_right_logical(code, 2) * 4
        kind = codes[:, 16 + f : 17 + f] * 8
        one = lambda target: (col == target).astype(F32).astype(BF)
        re = nn_dot(one(src), table[...])
        im = nn_dot(one(src + 4), table[...])
        tre = nn_dot(one(kind), tran[...])
        tim = nn_dot(one(kind + 1), tran[...])
        real_acc[...] += re * tre - im * tim
        imag_acc[...] += re * tim + im * tre
    re = real_acc[...].reshape(32, 8, 256)
    im = imag_acc[...].reshape(32, 8, 256)
    low = rows_of((32, 8, 256), 1) < 4
    out[:, 0] = jnp.where(low, re, pltpu.roll(im, 4, 1)).astype(BF)
    out[:, 1] = jnp.where(low, pltpu.roll(re, 4, 1), im).astype(BF)


def descend_kernel(slots, got, cosine, sine, whole, out, lhs, acc):
    acc[...] = jnp.zeros_like(acc)

    def step(k, carry):
        lanes = pl.ds(pl.multiple_of(k * 256, 256), 256)
        cos = cosine[:, lanes]
        sin = sine[:, lanes]
        block = jnp.stack([got[r // 2, k, r % 2].astype(F32) for r in range(8)], axis=0)
        block = jnp.swapaxes(block, 0, 1)
        for p in range(4):
            re, im = block[p], block[4 + p]
            for o in range(8):
                co, si = cos[o : o + 1], sin[o : o + 1]
                both = jnp.concatenate([re * co + im * si, im * co - re * si], axis=0)
                n = 8 * p + o
                lhs[16 * n : 16 * n + 16, :] = both.astype(BF)
        acc[...] += nn_dot(lhs[...], whole[k])
        return carry

    lax.fori_loop(0, 8, step, 0)

    def place(c, carry):
        src = pl.multiple_of(slots[c] * 16, 16)
        dst = pl.multiple_of(lax.rem(c, 4) * 16, 16)
        out[lax.div(c, 4), pl.ds(dst, 16), :] = acc[pl.ds(src, 16), :].astype(BF)
        return carry

    lax.fori_loop(0, 32, place, 0)


def finish_kernel(got, rad, near, out):
    for c in range(4):
        pieces = [got[s, 16 * c : 16 * c + 16, :].astype(F32) for s in range(8)]
        rows = jnp.concatenate([q[:8] for q in pieces] + [q[8:] for q in pieces], axis=0)
        received = rows.T.astype(BF)
        with_real = tn_dot(rad[c, 0], received)
        with_imag = tn_dot(rad[c, 1], received)
        turned = pltpu.roll(with_imag, 64, 1)
        lane = rows_of((128, 128), 1)
        far = with_real + jnp.where(lane < 64, turned, -turned)
        out[c] = (near[c] + far).astype(BF)


def params():
    return pltpu.CompilerParams(vmem_limit_bytes=VMEM_LIMIT)


def combine_parts(with_real, with_imag, sign):
    half_width = with_real.shape[-1] // 2
    real_part = with_real[..., :half_width] - sign * with_imag[..., half_width:]
    imag_part = with_real[..., half_width:] + sign * with_imag[..., :half_width]
    return jnp.concatenate([real_part, imag_part], axis=-1)


def near_field(currents, near_blocks, near_cols):
    group = currents.shape[0]
    margin = group // 4
    count = lax.axis_size("clus")
    up = [(i, i + 1) for i in range(count - 1)]
    down = [(b, a) for a, b in up]
    low = lax.ppermute(currents[group - margin :], "clus", up)
    high = lax.ppermute(currents[:margin], "clus", down)
    window = jnp.concatenate([low, currents, high], axis=0)
    local = near_cols - (lax.axis_index("clus") * group - margin)
    neighbours = window[local]
    near_real = jnp.einsum(
        "cjab,cjbr->car", near_blocks[:, :, 0], neighbours, preferred_element_type=F32
    )
    near_imag = jnp.einsum(
        "cjab,cjbr->car", near_blocks[:, :, 1], neighbours, preferred_element_type=F32
    )
    return combine_parts(near_real, near_imag, 1.0)


def body(
    currents,
    radiate,
    near_blocks,
    near_cols,
    child_slot,
    interp,
    shift_angle,
    far_dev,
    far_loc,
    far_type,
    transl,
):
    samp = lax.axis_index("samp")
    clus = lax.axis_index("clus")
    core = lax.rem(clus, 2)
    ids = jnp.stack([core, samp, clus]).astype(jnp.int32)
    partner = [(i, i ^ 1) for i in range(lax.axis_size("clus"))]
    codes = (far_dev * 4 + far_loc).astype(F32)
    kinds = far_type.astype(F32)
    lists = jnp.pad(codes, ((2, 2), (0, 240))) + jnp.pad(kinds, ((2, 2), (16, 224)))
    cosine = jnp.cos(shift_angle)
    sine = jnp.sin(shift_angle)

    sent = pl.pallas_call(
        radiate_kernel,
        name="radiate",
        out_shape=jax.ShapeDtypeStruct((8, 208, 256), BF),
        grid_spec=pltpu.PrefetchScalarGridSpec(
            num_scalar_prefetch=1,
            grid=(1,),
            in_specs=[
                pl.BlockSpec((4, 128, 128), lambda i, ids: (ids[1], 0, 0)),
                pl.BlockSpec((4, 2, 256, 128), lambda i, ids: (0, 0, 0, 0)),
                pl.BlockSpec((128, 256), lambda i, ids: (ids[0], 0)),
                pl.BlockSpec((1, 2, 256), lambda i, ids: (ids[2], 0, 0)),
                pl.BlockSpec((8, 256), lambda i, ids: (0, 0)),
            ],
            out_specs=pl.BlockSpec((8, 208, 256), lambda i, ids: (0, 0, 0)),
        ),
        compiler_params=params(),
    )(ids, currents, radiate, interp, transl, lists)
    got = lax.all_to_all(sent, "samp", split_axis=0, concat_axis=0, tiled=True)
    other = lax.ppermute(got[:, 64:192], "clus", partner)

    sent, whole = pl.pallas_call(
        lift_kernel,
        name="lift",
        out_shape=(
            jax.ShapeDtypeStruct((4, 8, 2, 16, 256), BF),
            jax.ShapeDtypeStruct((8, 256, 256), BF),
        ),
        in_specs=[SM, SM, VM, VM, VM, VM],
        out_specs=(VM, VM),
        scratch_shapes=[pltpu.VMEM((512, 256), BF), pltpu.SMEM((32,), jnp.int32)],
        compiler_params=params(),
    )(child_slot, ids, got, other, cosine, sine)
    got = lax.all_to_all(
        sent.reshape(64, 16, 256), "clus", split_axis=0, concat_axis=0, tiled=True
    )

    sent = pl.pallas_call(
        translate_kernel,
        name="translate",
        out_shape=jax.ShapeDtypeStruct((32, 2, 8, 256), BF),
        in_specs=[VM],
        out_specs=VM,
        scratch_shapes=[
            pltpu.VMEM((512, 256), BF),
            pltpu.VMEM((512, 256), BF),
            pltpu.VMEM((256, 128), jnp.int32),
            pltpu.VMEM((256, 256), F32),
            pltpu.VMEM((256, 256), F32),
        ],
        compiler_params=params(),
    )(got)
    got = lax.all_to_all(
        sent.reshape(64, 8, 256), "clus", split_axis=0, concat_axis=0, tiled=True
    )

    sent = pl.pallas_call(
        descend_kernel,
        name="descend",
        out_shape=jax.ShapeDtypeStruct((8, 64, 256), BF),
        in_specs=[SM, VM, VM, VM, VM],
        out_specs=VM,
        scratch_shapes=[pltpu.VMEM((512, 256), BF), pltpu.VMEM((512, 256), F32)],
        compiler_params=params(),
    )(child_slot, got.reshape(4, 8, 2, 8, 256), cosine, sine, whole)
    got = lax.all_to_all(sent, "samp", split_axis=0, concat_axis=0, tiled=True)

    near = near_field(currents, near_blocks, near_cols)
    return pl.pallas_call(
        finish_kernel,
        name="finish",
        out_shape=jax.ShapeDtypeStruct((4, 128, 128), BF),
        in_specs=[VM, VM, VM],
        out_specs=VM,
        compiler_params=params(),
    )(got, radiate, near)


def solution(mesh):
    in_specs = (
        P("clus", None, None),
        P(("clus", "samp"), None, None, None),
        P(("clus", "samp"), None, None, None, None),
        P(("clus", "samp"), None),
        P("clus"),
        P("samp", None),
        P(),
        P("clus", None),
        P("clus", None),
        P("clus", None),
        P(None, None, "samp"),
    )
    out_specs = P(("clus", "samp"), None, None)
    return jax.shard_map(body, mesh=mesh, in_specs=in_specs, out_specs=out_specs, check_vma=False)
```

time: 365 us -> 131 us (0.36)
  waiting for transfers between devices: 253 us -> 29.5 us
  blocking collectives: 0 us -> 29.2 us
  local copies, waits for them, and re-layouts: 29.8 us -> 5.95 us
  Pallas kernels: 0 us -> 22.3 us
  matrix products: 18.4 us -> 4.02 us
  between operations: 13.8 us -> 0.18 us
  other arithmetic: 14.1 us -> 3.95 us
    all_to_all x2 -> x3, waiting for transfers between devices: 193 us -> 28.9 us  [the longest x1 12 us: body(): lax.all_to_all(sent.reshape(64, 16, 256), 'clus', split_axis=0, concat_ax...]
    reduce_scatter x1 -> x0, waiting for transfers between devices: 36.2 us -> none  [body(): lax.psum_scatter(jnp.einsum('kj,ckr->cjr', interp, phased, preferred_elem...]
    all_to_all x0 -> x1, blocking collectives: none -> 29.2 us  [body(): got = lax.all_to_all(sent, 'samp', split_axis=0, concat_axis=0, tiled=True)]
    pallas_call x0 -> x5, Pallas kernels: none -> 22.3 us  [the longest x1 7.1 us: body(): pl.pallas_call(translate_kernel, name='translate', out_shape=jax.ShapeDty...]
    all_gather x1 -> x0, waiting for transfers between devices: 18.3 us -> none  [body(): lax.all_gather(rad_child, 'samp', axis=0, tiled=True)]
    gather x5 -> x1, local copies, waits for them, and re-layouts: 19 us -> 1.86 us  [near_field(): neighbours = window[local]]
    dot_general x12 -> x2, matrix products: 18.4 us -> 4.02 us  [the longest x1 2.2 us: near_field(): jnp.einsum('cjab,cjbr->car', near_blocks[:, :, 0], neighbours, preferred_...]
    reduce_sum x2 -> x0, other arithmetic: 9.18 us -> none  [the longest x1 9 us: body(): real_sum = jnp.sum(real_in * cosine_op - imag_in * sine_op, axis=1)]
  transfers between devices with their start and end apart: 6 -> 6, of which waited for: 6 -> 4; matrix products, arithmetic and copies ran while one was open for 2% -> 6% of each run, Pallas kernels for 0% -> 5%
where the time goes in v1:
time: 131 us; the launch traced here: 130 us
  starting transfers between devices  34.6 us (26%)
  waiting for transfers between devices  29.5 us (23%)
  blocking collectives  29.2 us (22%)
  Pallas kernels  22.3 us (17%)
  local copies, waits for them, and re-layouts  5.95 us (5%)
  matrix products  4.02 us (3%)
  other arithmetic  3.95 us (3%)
    all_to_all x1, blocking collectives, body(): got = lax.all_to_all(sent, 'samp', split_axis=0, concat_axis=0, tiled=True)  29.2 us
    all_to_all x1, starting transfers between devices, body(): lax.all_to_all(sent.reshape(64, 16, 256), 'clus', split_axis=0, concat_ax...  13.8 us
    all_to_all x1, waiting for transfers between devices, body(): lax.all_to_all(sent.reshape(64, 16, 256), 'clus', split_axis=0, concat_ax...  12 us
    all_to_all x1, waiting for transfers between devices, body(): got = lax.all_to_all(sent, 'samp', split_axis=0, concat_axis=0, tiled=True)  9.27 us
    all_to_all x1, waiting for transfers between devices, body(): lax.all_to_all(sent.reshape(64, 8, 256), 'clus', split_axis=0, concat_axi...  7.65 us
    pallas_call x1, Pallas kernels, body(): pl.pallas_call(translate_kernel, name='translate', out_shape=jax.ShapeDty...  7.1 us
    all_to_all x1, starting transfers between devices, body(): lax.all_to_all(sent.reshape(64, 8, 256), 'clus', split_axis=0, concat_axi...  5.98 us
    ppermute x1, starting transfers between devices, body(): other = lax.ppermute(got[:, 64:192], 'clus', partner)  5.95 us
  transfers between devices with their start and end apart: 6, of which 4 were waited for; matrix products, arithmetic and copies ran while one was open for 6% of the time, Pallas kernels for 5%

profile of v1, /device:TPU:1, one launch (start us, length us, event | category | flops | bytes accessed | tf_op | source)
XLA Modules:
  0.0 129.8 jit_solution(1221992690861473982)
XLA Ops:
  0.0 0.7 convert_element_type.11
  0.7 0.7 add_convert_fusion
  1.4 0.7 pad_add_fusion.lists
  2.1 0.6 pad_add_fusion.1.ids
  2.7 3.0 %radiate.1 = bf16[8,208,256]{2,1,0:T(8,128)(2,1)} custom-call(s32[3]{0:T(128)} %pad_add_fusion.1.ids, bf16[32,128,128]{2,1,0:T(8,128)(2,1)} %cur.1, bf16[4,2,256,128]{3,2,1,0:T(8,128)(2,1)} %rad.3, bf16[256,256]{1,0:T(8,128)(2,1)} %itp.1, bf16[64,2,256]{2,1,0:T(2,128)(2,1)} %tra.1, f32[8,256]{1,0:T(8,128)} %pad_add_fusion.lists), custom_call_target="tpu_custom_call" | custom-call | tf_op jit(solution)/shard_map/radiate/pallas_call | solution.py:231
  5.7 0.0 copy-start.7
  5.7 29.2 %all_to_all.20.got = bf16[8,208,256]{2,1,0:T(8,128)(2,1)S(1)} all-to-all(bf16[8,208,256]{2,1,0:T(8,128)(2,1)} %radiate.1), channel_id=1, replica_groups=mesh['clus'=64,'samp'=8] {'samp'}, dimensions={0} | all-to-all | bytes 1703936 | tf_op jit(solution)/shard_map/all_to_all | solution.py:249
  34.9 0.0 copy-start.1
  35.0 5.9 %collective-permute-start = (bf16[8,128,256]{2,1,0:T(8,128)(2,1)S(1)}, bf16[8,128,256]{2,1,0:T(8,128)(2,1)S(1)}, u32[]{:S(2)}, u32[]{:S(2)}) collective-permute-start(bf16[8,128,256]{2,1,0:T(8,128)(2,1)S(1)} %slice.38), channel_id=1, source_target_pairs={{0,8},{8,0},{16,24},{24,16},{32,40},{40,32},{48,56},{56,48},{64,72... | collective-permute-start | bytes 1572872 | tf_op jit(solution)/shard_map/ppermute | solution.py:250
  40.9 0.0 copy-done.7
  40.9 0.9 fusion.13
  41.8 0.0 copy-start
  41.8 0.6 collective-permute-done.other
  42.4 0.0 copy-start.6
  42.4 0.0 copy-done.1
  42.4 0.8 copy-done.6
  43.3 5.5 %lift.1 = (bf16[4,8,2,16,256]{4,3,2,1,0:T(8,128)(2,1)}, bf16[8,256,256]{2,1,0:T(8,128)(2,1)}) custom-call(s32[32]{0:T(128)} %slots.3, s32[3]{0:T(128)} %pad_add_fusion.1.ids, bf16[8,208,256]{2,1,0:T(8,128)(2,1)} %copy-done.1, bf16[8,128,256]{2,1,0:T(8,128)(2,1)} %copy-done.6, f32[8,2048]{1,0:T(8,128)} %get-tuple-element.14.cosine, ...), custom_call_target="tpu_custom_call" | custom-call | tf_op jit(solution)/shard_map/lift/pallas_call | solution.py:252
  48.8 0.0 copy-start.8
  48.8 13.8 %all-to-all-start.1 = ((bf16[64,16,256]{2,1,0:T(8,128)(2,1)}), bf16[64,16,256]{2,1,0:T(8,128)(2,1)S(1)}, u32[]{:S(2)}, u32[]{:S(2)}) async-start(bf16[64,16,256]{2,1,0:T(8,128)(2,1)} %bitcast.35), calls=%async_computation.1 | async-start | bytes 1048576 | tf_op jit(solution)/shard_map/all_to_all | solution.py:264
  62.6 0.0 copy-done
  62.7 3.5 %collective-permute-start.1 = (bf16[8,128,128]{2,1,0:T(8,128)(2,1)S(1)}, bf16[8,128,128]{2,1,0:T(8,128)(2,1)S(1)}, u32[]{:S(2)}, u32[]{:S(2)}) collective-permute-start(bf16[8,128,128]{2,1,0:T(8,128)(2,1)S(1)} %get-tuple-element.9), channel_id=1, source_target_pairs={{0,8},{8,16},{16,24},{24,32},{32,40},{40,48},{48,56},{56,64},{64,7... | collective-permute-start | bytes 786440 | tf_op jit(solution)/shard_map/ppermute | solution.py:193
  66.2 1.9 %collective-permute-start.2 = (bf16[8,128,128]{2,1,0:T(8,128)(2,1)S(1)}, bf16[8,128,128]{2,1,0:T(8,128)(2,1)S(1)}, u32[]{:S(2)}, u32[]{:S(2)}) collective-permute-start(bf16[8,128,128]{2,1,0:T(8,128)(2,1)S(1)} %get-tuple-element.10), channel_id=1, source_target_pairs={{8,0},{16,8},{24,16},{32,24},{40,32},{48,40},{56,48},{64,56},{72,6... | collective-permute-start | bytes 786440 | tf_op jit(solution)/shard_map/ppermute | solution.py:194
  68.1 0.0 copy-done.8
  68.2 0.1 reshape.14
  68.2 12.0 %all-to-all-done.1.got = bf16[64,16,256]{2,1,0:T(8,128)(2,1)S(1)} async-done(((bf16[64,16,256]{2,1,0:T(8,128)(2,1)}), bf16[64,16,256]{2,1,0:T(8,128)(2,1)S(1)}, u32[]{:S(2)}, u32[]{:S(2)}) %all-to-all-start.1) | async-done | bytes 524320 | tf_op jit(solution)/shard_map/all_to_all | solution.py:264
  80.2 0.0 copy-start.2
  80.2 0.8 copy-done.2
  81.0 7.1 %translate.1 = bf16[32,2,8,256]{3,2,1,0:T(8,128)(2,1)} custom-call(bf16[64,16,256]{2,1,0:T(8,128)(2,1)} %copy-done.2), custom_call_target="tpu_custom_call" | custom-call | tf_op jit(solution)/shard_map/translate/pallas_call | solution.py:268
  88.1 6.0 %all-to-all-start.2 = ((bf16[64,8,256]{2,1,0:T(8,128)(2,1)}), bf16[64,8,256]{2,1,0:T(8,128)(2,1)S(1)}, u32[]{:S(2)}, u32[]{:S(2)}) async-start(bf16[64,8,256]{2,1,0:T(8,128)(2,1)} %bitcast.34), calls=%async_computation.2 | async-start | bytes 524288 | tf_op jit(solution)/shard_map/all_to_all | solution.py:283
  94.1 0.0 collective-permute-done.1
  94.1 0.0 collective-permute-done.2
  94.1 0.2 pad_maximum_fusion
  94.3 1.9 %gather_fusion = bf16[40,128,128]{2,1,0:T(8,128)(2,1)} fusion(bf16[48,128,128]{2,1,0:T(8,128)(2,1)S(1)} %pad_maximum_fusion, s32[1024]{0:T(1024)S(1)} %pad_clamp_fusion), kind=kCustom, calls=%fused_computation | custom fusion | bytes 2621600 | tf_op jit(solution)/shard_map/gather | solution.py:197
  96.2 2.2 %fusion.6 = f32[4,128,128]{2,1,0:T(8,128)S(1)} fusion(bf16[4,10,128,128]{3,2,1,0:T(8,128)(2,1)} %bitcast.31, bf16[4,10,2,128,128]{4,3,2,1,0:T(8,128)(2,1)} %param.13), kind=kOutput, calls=%fused_computation.8 | convolution fusion | flops 167772160 | bytes 2883584 | tf_op jit(solution)/shard_map/cjab,cjbr->car/dot_general | solution.py:198
  98.4 0.0 copy-start.3
  98.4 7.7 %all-to-all-done.2 = bf16[64,8,256]{2,1,0:T(8,128)(2,1)S(1)} async-done(((bf16[64,8,256]{2,1,0:T(8,128)(2,1)}), bf16[64,8,256]{2,1,0:T(8,128)(2,1)S(1)}, u32[]{:S(2)}, u32[]{:S(2)}) %all-to-all-start.2) | async-done | bytes 262176 | tf_op jit(solution)/shard_map/all_to_all | solution.py:283
  106.1 0.0 copy-start.4
  106.1 0.7 copy-done.4
  106.8 4.4 %descend.1 = bf16[8,64,256]{2,1,0:T(8,128)(2,1)} custom-call(s32[32]{0:T(128)} %slots.3, bf16[4,8,2,8,256]{4,3,2,1,0:T(8,128)(2,1)} %bitcast.33, f32[8,2048]{1,0:T(8,128)} %get-tuple-element.14.cosine, f32[8,2048]{1,0:T(8,128)} %get-tuple-element.13.sine, bf16[8,256,256]{2,1,0:T(8,128)(2,1)} %get-tuple-element.8.whole), custom_call_target="tpu_custom_call" | custom-call | tf_op jit(solution)/shard_map/descend/pallas_call | solution.py:287
  111.2 3.4 %all-to-all-start.3 = ((bf16[8,64,256]{2,1,0:T(8,128)(2,1)}), bf16[8,64,256]{2,1,0:T(8,128)(2,1)S(1)}, u32[]{:S(2)}, u32[]{:S(2)}) async-start(bf16[8,64,256]{2,1,0:T(8,128)(2,1)} %descend.1), calls=%async_computation.3 | async-start | bytes 524288 | tf_op jit(solution)/shard_map/all_to_all | solution.py:296
  114.6 0.0 copy-done.3
  114.6 1.8 %fusion.9 = f32[4,128,128]{2,1,0:T(8,128)S(1)} fusion(bf16[4,10,128,128]{3,2,1,0:T(8,128)(2,1)S(1)} %bitcast.32, bf16[4,10,2,128,128]{4,3,2,1,0:T(8,128)(2,1)} %param.13), kind=kOutput, calls=%fused_computation.9 | convolution fusion | flops 167772160 | bytes 2883584 | tf_op jit(solution)/shard_map/cjab,cjbr->car/dot_general | solution.py:201
  116.4 0.2 slice_subtract_fusion
  116.6 0.8 pad_maximum_fusion.1.near
  117.5 9.3 %all-to-all-done.3.got = bf16[8,64,256]{2,1,0:T(8,128)(2,1)S(1)} async-done(((bf16[8,64,256]{2,1,0:T(8,128)(2,1)}), bf16[8,64,256]{2,1,0:T(8,128)(2,1)S(1)}, u32[]{:S(2)}, u32[]{:S(2)}) %all-to-all-start.3) | async-done | bytes 262176 | tf_op jit(solution)/shard_map/all_to_all | solution.py:296
  126.7 0.0 copy-start.5
  126.7 0.7 copy-done.5
  127.4 2.3 %finish.1 = bf16[4,128,128]{2,1,0:T(8,128)(2,1)} custom-call(bf16[8,64,256]{2,1,0:T(8,128)(2,1)} %copy-done.5, bf16[4,2,256,128]{3,2,1,0:T(8,128)(2,1)} %rad.3, f32[4,128,128]{2,1,0:T(8,128)} %pad_maximum_fusion.1.near), custom_call_target="tpu_custom_call" | custom-call | tf_op jit(solution)/shard_map/finish/pallas_call | solution.py:299
  (4 shorter events, 0.1 us)
Async XLA Ops:
  5.7 35.2 %copy-start.7 = (f32[8,2048]{1,0:T(8,128)S(1)}, f32[8,2048]{1,0:T(8,128)}, u32[]{:S(2)}) copy-start(f32[8,2048]{1,0:T(8,128)} %param.17) | copy-start | bytes 196612
  34.9 7.5 %copy-start.1 = (bf16[8,208,256]{2,1,0:T(8,128)(2,1)}, bf16[8,208,256]{2,1,0:T(8,128)(2,1)S(1)}, u32[]{:S(2)}) copy-start(bf16[8,208,256]{2,1,0:T(8,128)(2,1)S(1)} %all_to_all.20.got) | copy-start | bytes 2555908
  35.0 7.5 %collective-permute-start = (bf16[8,128,256]{2,1,0:T(8,128)(2,1)S(1)}, bf16[8,128,256]{2,1,0:T(8,128)(2,1)S(1)}, u32[]{:S(2)}, u32[]{:S(2)}) collective-permute-start(bf16[8,128,256]{2,1,0:T(8,128)(2,1)S(1)} %slice.38), channel_id=1, source_target_pairs={{0,8},{8,0},{16,24},{24,16},{32,40},{40,32},{48,56},{56,48},{64,72... | collective-permute-start | bytes 1572872 | tf_op jit(solution)/shard_map/ppermute | solution.py:250
  41.8 20.8 %copy-start = (bf16[32,128,128]{2,1,0:T(8,128)(2,1)S(1)}, bf16[32,128,128]{2,1,0:T(8,128)(2,1)}, u32[]{:S(2)}) copy-start(bf16[32,128,128]{2,1,0:T(8,128)(2,1)} %cur.1) | copy-start | bytes 3145732
  42.4 0.8 copy-start.6
  48.8 19.4 %copy-start.8 = (s32[4,10]{1,0:T(4,128)S(1)}, s32[4,10]{1,0:T(4,128)}, u32[]{:S(2)}) copy-start(s32[4,10]{1,0:T(4,128)} %param.14) | copy-start | bytes 484
  48.8 31.4 %all-to-all-start.1 = ((bf16[64,16,256]{2,1,0:T(8,128)(2,1)}), bf16[64,16,256]{2,1,0:T(8,128)(2,1)S(1)}, u32[]{:S(2)}, u32[]{:S(2)}) async-start(bf16[64,16,256]{2,1,0:T(8,128)(2,1)} %bitcast.35), calls=%async_computation.1 | async-start | bytes 1048576 | tf_op jit(solution)/shard_map/all_to_all | solution.py:264
  62.7 31.5 %collective-permute-start.1 = (bf16[8,128,128]{2,1,0:T(8,128)(2,1)S(1)}, bf16[8,128,128]{2,1,0:T(8,128)(2,1)S(1)}, u32[]{:S(2)}, u32[]{:S(2)}) collective-permute-start(bf16[8,128,128]{2,1,0:T(8,128)(2,1)S(1)} %get-tuple-element.9), channel_id=1, source_target_pairs={{0,8},{8,16},{16,24},{24,32},{32,40},{40,48},{48,56},{56,64},{64,7... | collective-permute-start | bytes 786440 | tf_op jit(solution)/shard_map/ppermute | solution.py:193
  66.2 27.9 %collective-permute-start.2 = (bf16[8,128,128]{2,1,0:T(8,128)(2,1)S(1)}, bf16[8,128,128]{2,1,0:T(8,128)(2,1)S(1)}, u32[]{:S(2)}, u32[]{:S(2)}) collective-permute-start(bf16[8,128,128]{2,1,0:T(8,128)(2,1)S(1)} %get-tuple-element.10), channel_id=1, source_target_pairs={{8,0},{16,8},{24,16},{32,24},{40,32},{48,40},{56,48},{64,56},{72,6... | collective-permute-start | bytes 786440 | tf_op jit(solution)/shard_map/ppermute | solution.py:194
  80.2 0.8 copy-start.2
  88.1 18.0 %all-to-all-start.2 = ((bf16[64,8,256]{2,1,0:T(8,128)(2,1)}), bf16[64,8,256]{2,1,0:T(8,128)(2,1)S(1)}, u32[]{:S(2)}, u32[]{:S(2)}) async-start(bf16[64,8,256]{2,1,0:T(8,128)(2,1)} %bitcast.34), calls=%async_computation.2 | async-start | bytes 524288 | tf_op jit(solution)/shard_map/all_to_all | solution.py:283
  98.4 16.2 %copy-start.3 = (bf16[40,128,128]{2,1,0:T(8,128)(2,1)S(1)}, bf16[40,128,128]{2,1,0:T(8,128)(2,1)}, u32[]{:S(2)}) copy-start(bf16[40,128,128]{2,1,0:T(8,128)(2,1)} %gather_fusion) | copy-start | bytes 3932164
  106.1 0.7 copy-start.4
  111.2 15.6 %all-to-all-start.3 = ((bf16[8,64,256]{2,1,0:T(8,128)(2,1)}), bf16[8,64,256]{2,1,0:T(8,128)(2,1)S(1)}, u32[]{:S(2)}, u32[]{:S(2)}) async-start(bf16[8,64,256]{2,1,0:T(8,128)(2,1)} %descend.1), calls=%async_computation.3 | async-start | bytes 524288 | tf_op jit(solution)/shard_map/all_to_all | solution.py:296
  126.7 0.7 copy-start.5

commit v2 on v1

v2 whole, which is shorter than its diff:
```python
import jax
import jax.numpy as jnp
from jax import lax
from jax.experimental import pallas as pl
from jax.experimental.pallas import tpu as pltpu
from jax.sharding import PartitionSpec as P

BF = jnp.bfloat16
F32 = jnp.float32
VMEM_LIMIT = 16 * 1024 * 1024
VM = pl.BlockSpec(memory_space=pltpu.VMEM)
SM = pl.BlockSpec(memory_space=pltpu.SMEM)


def nt_dot(a, b):
    return lax.dot_general(a, b, (((1,), (1,)), ((), ())), preferred_element_type=F32)


def nn_dot(a, b):
    return lax.dot_general(a, b, (((1,), (0,)), ((), ())), preferred_element_type=F32)


def tn_dot(a, b):
    return lax.dot_general(a, b, (((0,), (0,)), ((), ())), preferred_element_type=F32)


def rows_of(shape, dim):
    return lax.broadcasted_iota(jnp.int32, shape, dim)


def radiate_kernel(cur, rad_all, itp, tra, out, own, rad, half_ref, tran, sems):
    clus = lax.axis_index("clus")
    mine = pl.ds(pl.multiple_of(lax.rem(clus, 2) * 128, 128), 128)
    pairs = [
        (itp.at[mine], half_ref),
        (tra.at[clus], tran),
        (cur.at[pl.ds(lax.axis_index("samp") * 4, 4)], own),
    ] + [(rad_all.at[c], rad.at[c]) for c in range(4)]
    copies = [pltpu.make_async_copy(a, b, sems.at[i]) for i, (a, b) in enumerate(pairs)]
    for copy in copies:
        copy.start()
    copies[0].wait()
    copies[1].wait()
    half = half_ref[...]
    trow = tran[...].astype(F32)
    row = rows_of((8, 256), 0)
    extra = jnp.where(row == 0, trow[0:1], jnp.where(row == 1, trow[1:2], 0.0)).astype(BF)
    for s in range(8):
        out[s, 64:192, :] = half
        out[s, 192:200, :] = extra
    copies[2].wait()
    for c in range(4):
        copies[3 + c].wait()
        values = own[c].astype(F32).T.astype(BF)
        with_real = nt_dot(values, rad[c, 0])
        with_imag = nt_dot(values, rad[c, 1])
        real = with_real[:64] - with_imag[64:]
        imag = with_real[64:] + with_imag[:64]
        for s in range(8):
            both = jnp.concatenate([real[8 * s : 8 * s + 8], imag[8 * s : 8 * s + 8]], axis=0)
            out[s, 16 * c : 16 * c + 16, :] = both.astype(BF)


def own_lanes(k):
    core = lax.rem(lax.axis_index("clus"), 2)
    return pl.ds(pl.multiple_of(k * 256 + core * 128, 128), 128)


def other_lanes(k):
    core = lax.rem(lax.axis_index("clus"), 2)
    return pl.ds(pl.multiple_of(k * 256 + (1 - core) * 128, 128), 128)


def lift_half(rows, matrix, cos, sin):
    reals, imags = [], []
    for p in range(4):
        lifted = nt_dot(rows[128 * p : 128 * p + 128, :], matrix)
        real_sum = imag_sum = None
        for o in range(8):
            re = lifted[16 * o : 16 * o + 8]
            im = lifted[16 * o + 8 : 16 * o + 16]
            co, si = cos[o : o + 1], sin[o : o + 1]
            real = re * co - im * si
            imag = re * si + im * co
            real_sum = real if real_sum is None else real_sum + real
            imag_sum = imag if imag_sum is None else imag_sum + imag
        reals.append(real_sum)
        imags.append(imag_sum)
    return jnp.swapaxes(jnp.stack(reals + imags, axis=0), 0, 1).astype(BF)


def lift_own_kernel(slots, got, cosine, sine, out, rows, inverse):
    def note(c, carry):
        inverse[slots[c]] = c
        return carry

    lax.fori_loop(0, 32, note, 0)

    def collect(n, carry):
        c = inverse[n]
        src = pl.multiple_of(lax.rem(c, 4) * 16, 16)
        dst = pl.multiple_of(n * 16, 16)
        rows[pl.ds(dst, 16), :] = got[lax.div(c, 4), pl.ds(src, 16), :]
        return carry

    lax.fori_loop(0, 32, collect, 0)

    def step(k, carry):
        lanes = own_lanes(k)
        block = lift_half(rows, got[k, 64:192, :], cosine[:, lanes], sine[:, lanes])
        for r in range(8):
            out[r // 2, k, r % 2] = block[r]
        return carry

    lax.fori_loop(0, 8, step, 0)


def lift_other_kernel(first, rows, got, other, lists, cosine, sine, out):
    row = rows_of((8, 128), 0)

    def step(k, carry):
        lanes = other_lanes(k)
        block = lift_half(rows, other[k], cosine[:, lanes], sine[:, lanes])
        tran = got[k, 192:200, :].astype(F32)
        tile = lists[...]
        for j in range(4):
            piece = tran[j // 2 : j // 2 + 1, 128 * (j % 2) : 128 * (j % 2) + 128]
            tile = jnp.where(row == 4 + j, piece, tile)
        tile = tile.astype(BF)
        for r in range(8):
            out[r // 2, k, r % 2, :, 0:128] = first[r // 2, k, r % 2]
            out[r // 2, k, r % 2, :, 128:256] = block[r]
            out[r // 2, k, r % 2, :, 256:384] = tile
        return carry

    lax.fori_loop(0, 8, step, 0)


def translate_kernel(got, out, table, codes, tran, real_acc, imag_acc):
    def uppers(even, odd):
        low = rows_of(even.shape, 1) < 4
        return jnp.where(low, even, pltpu.roll(odd, 4, 1)).reshape(256, even.shape[2])

    def lowers(even, odd):
        low = rows_of(even.shape, 1) < 4
        return jnp.where(low, pltpu.roll(even, 4, 1), odd).reshape(256, even.shape[2])

    for h in range(2):
        even = got[:, 0, :, 128 * h : 128 * h + 128].astype(F32)
        odd = got[:, 1, :, 128 - 128 * h : 256 - 128 * h].astype(F32)
        table[:, 128 * h : 128 * h + 128] = uppers(even, odd).astype(BF)
        table[:, 256 + 128 * h : 384 + 128 * h] = lowers(even, odd).astype(BF)
    even = got[:, 0, :, 256:384].astype(F32)
    odd = got[:, 1, :, 256:384].astype(F32)
    codes[...] = uppers(even, odd).astype(jnp.int32)
    pieces = lowers(even, odd).astype(BF)
    for j in range(4):
        pick = rows_of((64, 256), 1) == rows_of((64, 256), 0) * 4 + j
        part = nn_dot(pick.astype(F32).astype(BF), pieces)
        tran[:, 128 * j : 128 * j + 128] = part.astype(BF)
    col = rows_of((256, 256), 1)
    kinds = rows_of((256, 64), 1)
    for f in range(16):
        pick = (col == codes[:, f : f + 1]).astype(F32).astype(BF)
        kind = (kinds == codes[:, 16 + f : 17 + f]).astype(F32).astype(BF)
        both = nn_dot(pick, table[...])
        factor = nn_dot(kind, tran[...])
        re, im = both[:, :256], both[:, 256:]
        tre, tim = factor[:, :256], factor[:, 256:]
        real = re * tre - im * tim
        imag = re * tim + im * tre
        if f == 0:
            real_acc[...] = real
            imag_acc[...] = imag
        else:
            real_acc[...] += real
            imag_acc[...] += imag
    low = rows_of((32, 8, 256), 1) < 4
    re = real_acc[...].reshape(32, 8, 256)
    im = imag_acc[...].reshape(32, 8, 256)
    out[:, 0] = jnp.where(low, re, pltpu.roll(im, 4, 1)).astype(BF)
    last = jnp.where(low, pltpu.roll(re, 4, 1), im).astype(BF)
    out[:, 1, :, 0:128] = last[:, :, 128:256]
    out[:, 1, :, 128:256] = last[:, :, 0:128]


def descend_kernel(slots, got, half, other, cosine, sine, out, lhs, acc):
    acc[...] = jnp.zeros_like(acc)

    def step(k, carry):
        mine, theirs = own_lanes(k), other_lanes(k)
        cos = jnp.concatenate([cosine[:, mine], cosine[:, theirs]], axis=1)
        sin = jnp.concatenate([sine[:, mine], sine[:, theirs]], axis=1)
        block = jnp.stack([got[r // 2, k, r % 2].astype(F32) for r in range(8)], axis=0)
        block = jnp.swapaxes(block, 0, 1)
        for p in range(4):
            re, im = block[p], block[4 + p]
            for o in range(8):
                co, si = cos[o : o + 1], sin[o : o + 1]
                both = jnp.concatenate([re * co + im * si, im * co - re * si], axis=0)
                n = 8 * p + o
                lhs[16 * n : 16 * n + 16, :] = both.astype(BF)
        whole = jnp.concatenate([half[k], other[k]], axis=0)
        acc[...] += nn_dot(lhs[...], whole)
        return carry

    lax.fori_loop(0, 8, step, 0)

    def place(c, carry):
        src = pl.multiple_of(slots[c] * 16, 16)
        dst = pl.multiple_of(lax.rem(c, 4) * 16, 16)
        out[lax.div(c, 4), pl.ds(dst, 16), :] = acc[pl.ds(src, 16), :].astype(BF)
        return carry

    lax.fori_loop(0, 32, place, 0)


def finish_kernel(got, rad, near, out):
    for c in range(4):
        pieces = [got[s, 16 * c : 16 * c + 16, :].astype(F32) for s in range(8)]
        rows = jnp.concatenate([q[:8] for q in pieces] + [q[8:] for q in pieces], axis=0)
        received = rows.T.astype(BF)
        with_real = tn_dot(rad[c, 0], received)
        with_imag = tn_dot(rad[c, 1], received)
        turned = pltpu.roll(with_imag, 64, 1)
        lane = rows_of((128, 128), 1)
        far = with_real + jnp.where(lane < 64, turned, -turned)
        out[c] = (near[c] + far).astype(BF)


def params(limit=VMEM_LIMIT):
    return pltpu.CompilerParams(vmem_limit_bytes=limit)


def combine_parts(with_real, with_imag, sign):
    half_width = with_real.shape[-1] // 2
    real_part = with_real[..., :half_width] - sign * with_imag[..., half_width:]
    imag_part = with_real[..., half_width:] + sign * with_imag[..., :half_width]
    return jnp.concatenate([real_part, imag_part], axis=-1)


def near_field(currents, near_blocks, near_cols):
    group = currents.shape[0]
    margin = group // 4
    count = lax.axis_size("clus")
    up = [(i, i + 1) for i in range(count - 1)]
    down = [(b, a) for a, b in up]
    low = lax.ppermute(currents[group - margin :], "clus", up)
    high = lax.ppermute(currents[:margin], "clus", down)
    window = jnp.concatenate([low, currents, high], axis=0)
    local = near_cols - (lax.axis_index("clus") * group - margin)
    neighbours = window[local]
    near_real = jnp.einsum(
        "cjab,cjbr->car", near_blocks[:, :, 0], neighbours, preferred_element_type=F32
    )
    near_imag = jnp.einsum(
        "cjab,cjbr->car", near_blocks[:, :, 1], neighbours, preferred_element_type=F32
    )
    return combine_parts(near_real, near_imag, 1.0)


def body(
    currents,
    radiate,
    near_blocks,
    near_cols,
    child_slot,
    interp,
    shift_angle,
    far_dev,
    far_loc,
    far_type,
    transl,
):
    partner = [(i, i ^ 1) for i in range(lax.axis_size("clus"))]
    exchange = lambda x, axis: lax.all_to_all(x, axis, split_axis=0, concat_axis=0, tiled=True)
    lists = jnp.pad((far_dev * 4 + far_loc).astype(F32), ((0, 4), (0, 112)))
    lists = lists + jnp.pad(far_type.astype(F32), ((0, 4), (16, 96)))
    cosine = jnp.cos(shift_angle)
    sine = jnp.sin(shift_angle)

    sent = pl.pallas_call(
        radiate_kernel,
        name="radiate",
        out_shape=jax.ShapeDtypeStruct((8, 200, 256), BF),
        in_specs=[pl.BlockSpec(memory_space=pltpu.HBM)] * 4,
        out_specs=VM,
        scratch_shapes=[
            pltpu.VMEM((4, 128, 128), BF),
            pltpu.VMEM((4, 2, 256, 128), BF),
            pltpu.VMEM((128, 256), BF),
            pltpu.VMEM((2, 256), BF),
            pltpu.SemaphoreType.DMA((7,)),
        ],
        compiler_params=params(60 * 1024 * 1024),
    )(currents, radiate, interp, transl)
    got = exchange(sent, "samp")
    half = got[:, 64:192]
    other = lax.ppermute(half, "clus", partner)

    first, rows = pl.pallas_call(
        lift_own_kernel,
        name="lift_own",
        out_shape=(
            jax.ShapeDtypeStruct((4, 8, 2, 8, 128), BF),
            jax.ShapeDtypeStruct((512, 256), BF),
        ),
        in_specs=[SM, VM, VM, VM],
        out_specs=(VM, VM),
        scratch_shapes=[pltpu.SMEM((32,), jnp.int32)],
        compiler_params=params(),
    )(child_slot, got, cosine, sine)
    sent = pl.pallas_call(
        lift_other_kernel,
        name="lift_other",
        out_shape=jax.ShapeDtypeStruct((4, 8, 2, 8, 384), BF),
        in_specs=[VM] * 7,
        out_specs=VM,
        compiler_params=params(),
    )(first, rows, got, other, lists, cosine, sine)
    moved = exchange(sent.reshape(64, 8, 384), "clus")

    sent = pl.pallas_call(
        translate_kernel,
        name="translate",
        out_shape=jax.ShapeDtypeStruct((32, 2, 8, 256), BF),
        in_specs=[VM],
        out_specs=VM,
        scratch_shapes=[
            pltpu.VMEM((256, 512), BF),
            pltpu.VMEM((256, 128), jnp.int32),
            pltpu.VMEM((64, 512), BF),
            pltpu.VMEM((256, 256), F32),
            pltpu.VMEM((256, 256), F32),
        ],
        compiler_params=params(),
    )(moved.reshape(32, 2, 8, 384))
    moved = exchange(sent.reshape(64, 8, 256), "clus")

    sent = pl.pallas_call(
        descend_kernel,
        name="descend",
        out_shape=jax.ShapeDtypeStruct((8, 64, 256), BF),
        in_specs=[SM, VM, VM, VM, VM, VM],
        out_specs=VM,
        scratch_shapes=[
            pltpu.VMEM((512, 256), BF),
            pltpu.VMEM((512, 256), F32),
        ],
        compiler_params=params(),
    )(child_slot, moved.reshape(4, 8, 2, 8, 256), half, other, cosine, sine)
    got = exchange(sent, "samp")

    near = near_field(currents, near_blocks, near_cols)
    return pl.pallas_call(
        finish_kernel,
        name="finish",
        out_shape=jax.ShapeDtypeStruct((4, 128, 128), BF),
        in_specs=[VM, VM, VM],
        out_specs=VM,
        compiler_params=params(),
    )(got, radiate, near)


def solution(mesh):
    in_specs = (
        P("clus", None, None),
        P(("clus", "samp"), None, None, None),
        P(("clus", "samp"), None, None, None, None),
        P(("clus", "samp"), None),
        P("clus"),
        P("samp", None),
        P(),
        P("clus", None),
        P("clus", None),
        P("clus", None),
        P(None, None, "samp"),
    )
    out_specs = P(("clus", "samp"), None, None)
    return jax.shard_map(body, mesh=mesh, in_specs=in_specs, out_specs=out_specs, check_vma=False)
```

time: 131 us -> 115 us (0.88)
  blocking collectives: 29.2 us -> 0 us
  waiting for transfers between devices: 29.5 us -> 45 us
  starting transfers between devices: 34.6 us -> 41 us
  Pallas kernels: 22.3 us -> 17.3 us
  other arithmetic: 3.95 us -> 1.79 us
  local copies, waits for them, and re-layouts: 5.95 us -> 4.44 us
    all_to_all x1 -> x0, blocking collectives: 29.2 us -> none  [body(): got = lax.all_to_all(sent, 'samp', split_axis=0, concat_axis=0, tiled=True)]
    all_to_all x3 -> x4, waiting for transfers between devices: 28.9 us -> 44.9 us  [body(): lax.all_to_all(x, axis, split_axis=0, concat_axis=0, tiled=True)]
    all_to_all x3 -> x4, starting transfers between devices: 23.2 us -> 30.7 us  [body(): lax.all_to_all(x, axis, split_axis=0, concat_axis=0, tiled=True)]
    pallas_call x1, Pallas kernels: 7.1 us -> 3.74 us  [body(): pl.pallas_call(translate_kernel, name='translate', out_shape=jax.ShapeDty...]
    unnamed x18 -> x16, local copies, waits for them, and re-layouts: 3.04 us -> 0.05 us
    gather x1, local copies, waits for them, and re-layouts: 1.86 us -> 3.28 us  [near_field(): neighbours = window[local]]
    convert_element_type x2, other arithmetic: 1.39 us -> 0.01 us  [the longest x1 0.01 us: body(): lists = jnp.pad((far_dev * 4 + far_loc).astype(F32), ((0, 4), (0, 112)))]
    pallas_call x1 -> x2, Pallas kernels: 5.5 us -> 5.82 us  [the longest x1 3.11 us: body(): pl.pallas_call(lift_own_kernel, name='lift_own', out_shape=(jax.ShapeDtyp...]
  transfers between devices with their start and end apart: 6 -> 7, of which waited for: 4 -> 4; matrix products, arithmetic and copies ran while one was open for 6% -> 9% of each run, Pallas kernels for 5% -> 6%
where the time goes in v2:
time: 115 us; the launch traced here: 114 us
  waiting for transfers between devices  45 us (39%)
  starting transfers between devices  41 us (36%)
  Pallas kernels  17.3 us (15%)
  local copies, waits for them, and re-layouts  4.44 us (4%)
  matrix products  4.41 us (4%)
  other arithmetic  1.79 us (2%)
    all_to_all x4, waiting for transfers between devices, body(): lax.all_to_all(x, axis, split_axis=0, concat_axis=0, tiled=True)  44.9 us
    all_to_all x4, starting transfers between devices, body(): lax.all_to_all(x, axis, split_axis=0, concat_axis=0, tiled=True)  30.7 us
    ppermute x1, starting transfers between devices, body(): other = lax.ppermute(half, 'clus', partner)  4.86 us
    pallas_call x1, Pallas kernels, body(): pl.pallas_call(translate_kernel, name='translate', out_shape=jax.ShapeDty...  3.74 us
    pallas_call x1, Pallas kernels, body(): pl.pallas_call(descend_kernel, name='descend', out_shape=jax.ShapeDtypeSt...  3.54 us
    ppermute x1, starting transfers between devices, near_field(): low = lax.ppermute(currents[group - margin:], 'clus', up)  3.53 us
    gather x1, local copies, waits for them, and re-layouts, near_field(): neighbours = window[local]  3.28 us
    pallas_call x1, Pallas kernels, body(): pl.pallas_call(lift_own_kernel, name='lift_own', out_shape=(jax.ShapeDtyp...  3.11 us
  transfers between devices with their start and end apart: 7, of which 4 were waited for; matrix products, arithmetic and copies ran while one was open for 9% of the time, Pallas kernels for 6%

profile of v2, /device:TPU:1, one launch (start us, length us, event | category | flops | bytes accessed | tf_op | source)
XLA Modules:
  0.0 114.1 jit_solution(9822265075066369621)
XLA Ops:
  0.0 3.0 %radiate.1 = bf16[8,200,256]{2,1,0:T(8,128)(2,1)} custom-call(bf16[32,128,128]{2,1,0:T(8,128)(2,1)} %cur.1, bf16[4,2,256,128]{3,2,1,0:T(8,128)(2,1)} %rad.1, bf16[256,256]{1,0:T(8,128)(2,1)} %itp.1, bf16[64,2,256]{2,1,0:T(2,128)(2,1)} %tra.1), custom_call_target="tpu_custom_call" | custom-call | tf_op jit(solution)/shard_map/radiate/pallas_call | solution.py:282
  3.0 0.0 copy-start.6
  3.0 0.0 copy-start.4
  3.0 0.0 copy-start.5
  3.0 0.0 copy-start.3
  3.1 0.0 copy-start.1
  3.1 7.8 %all-to-all-start = ((bf16[8,200,256]{2,1,0:T(8,128)(2,1)}), bf16[8,200,256]{2,1,0:T(8,128)(2,1)S(1)}, u32[]{:S(2)}, u32[]{:S(2)}) async-start(bf16[8,200,256]{2,1,0:T(8,128)(2,1)} %radiate.1), calls=%async_computation | async-start | bytes 1638400 | tf_op jit(solution)/shard_map/all_to_all | solution.py:276
  10.9 0.0 copy-done.6
  10.9 0.0 copy-done.4
  10.9 0.0 copy-done.5
  10.9 21.8 %all-to-all-done.got = bf16[8,200,256]{2,1,0:T(8,128)(2,1)S(1)} async-done(((bf16[8,200,256]{2,1,0:T(8,128)(2,1)}), bf16[8,200,256]{2,1,0:T(8,128)(2,1)S(1)}, u32[]{:S(2)}, u32[]{:S(2)}) %all-to-all-start) | async-done | bytes 819232 | tf_op jit(solution)/shard_map/all_to_all | solution.py:276
  32.8 4.9 %collective-permute-start = (bf16[8,128,256]{2,1,0:T(8,128)(2,1)S(1)}, bf16[8,128,256]{2,1,0:T(8,128)(2,1)S(1)}, u32[]{:S(2)}, u32[]{:S(2)}) collective-permute-start(bf16[8,128,256]{2,1,0:T(8,128)(2,1)S(1)} %slice.38.half), channel_id=1, source_target_pairs={{0,8},{8,0},{16,24},{24,16},{32,40},{40,32},{48,56},{56,48},{64,72... | collective-permute-start | bytes 1572872 | tf_op jit(solution)/shard_map/ppermute | solution.py:299
  37.6 0.1 pad_add_fusion.lists
  37.7 0.0 copy-done.3
  37.7 0.2 fusion.13
  37.9 0.0 copy-done.1
  38.0 3.1 %lift_own.1 = (bf16[4,8,2,8,128]{4,3,2,1,0:T(8,128)(2,1)S(1)}, bf16[512,256]{1,0:T(8,128)(2,1)S(1)}) custom-call(s32[32]{0:T(128)S(1)} %copy-done.1, bf16[8,200,256]{2,1,0:T(8,128)(2,1)S(1)} %all-to-all-done.got, f32[8,2048]{1,0:T(8,128)S(1)} %get-tuple-element.14.cosine, f32[8,2048]{1,0:T(8,128)S(1)} %get-tuple-element.13.sine), custom_call_target="tpu_custom_call" | custom-call | tf_op jit(solution)/shard_map/lift_own/pallas_call | solution.py:301
  41.1 0.0 collective-permute-done.other
  41.1 0.0 copy-start.2
  41.1 2.7 %lift_other.1 = bf16[4,8,2,8,384]{4,3,2,1,0:T(8,128)(2,1)} custom-call(bf16[4,8,2,8,128]{4,3,2,1,0:T(8,128)(2,1)S(1)} %get-tuple-element.7.first, bf16[512,256]{1,0:T(8,128)(2,1)S(1)} %get-tuple-element.8.rows, bf16[8,200,256]{2,1,0:T(8,128)(2,1)S(1)} %all-to-all-done.got, bf16[8,128,256]{2,1,0:T(8,128)(2,1)S(1)} %collective-permute-done.other, ...), custom_call_target="tpu_custom_call" | custom-call | tf_op jit(solution)/shard_map/lift_other/pallas_call | solution.py:313
  43.8 0.0 copy-start.7
  43.8 13.5 %all-to-all-start.1 = ((bf16[64,8,384]{2,1,0:T(8,128)(2,1)}), bf16[64,8,384]{2,1,0:T(8,128)(2,1)S(1)}, u32[]{:S(2)}, u32[]{:S(2)}) async-start(bf16[64,8,384]{2,1,0:T(8,128)(2,1)} %bitcast), calls=%async_computation.1 | async-start | bytes 786432 | tf_op jit(solution)/shard_map/all_to_all | solution.py:276
  57.4 0.0 copy-done.2
  57.4 0.8 fusion.12
  58.1 3.5 %collective-permute-start.1 = (bf16[8,128,128]{2,1,0:T(8,128)(2,1)}, bf16[8,128,128]{2,1,0:T(8,128)(2,1)S(1)}, u32[]{:S(2)}, u32[]{:S(2)}) collective-permute-start(bf16[8,128,128]{2,1,0:T(8,128)(2,1)} %get-tuple-element.9), channel_id=1, source_target_pairs={{0,8},{8,16},{16,24},{24,32},{32,40},{40,48},{48,56},{56,64},{64,7... | collective-permute-start | bytes 786440 | tf_op jit(solution)/shard_map/ppermute | solution.py:248
  61.7 1.9 %collective-permute-start.2 = (bf16[8,128,128]{2,1,0:T(8,128)(2,1)S(1)}, bf16[8,128,128]{2,1,0:T(8,128)(2,1)S(1)}, u32[]{:S(2)}, u32[]{:S(2)}) collective-permute-start(bf16[8,128,128]{2,1,0:T(8,128)(2,1)S(1)} %get-tuple-element.10), channel_id=1, source_target_pairs={{8,0},{16,8},{24,16},{32,24},{40,32},{48,40},{56,48},{64,56},{72,6... | collective-permute-start | bytes 786440 | tf_op jit(solution)/shard_map/ppermute | solution.py:249
  63.6 0.0 copy-done.7
  63.6 0.1 reshape.18
  63.7 8.5 %all-to-all-done.1 = bf16[64,8,384]{2,1,0:T(8,128)(2,1)S(1)} async-done(((bf16[64,8,384]{2,1,0:T(8,128)(2,1)}), bf16[64,8,384]{2,1,0:T(8,128)(2,1)S(1)}, u32[]{:S(2)}, u32[]{:S(2)}) %all-to-all-start.1) | async-done | bytes 393248 | tf_op jit(solution)/shard_map/all_to_all | solution.py:276
  72.2 3.7 %translate.1 = bf16[32,2,8,256]{3,2,1,0:T(8,128)(2,1)} custom-call(bf16[32,2,8,384]{3,2,1,0:T(8,128)(2,1)S(1)} %bitcast.29), custom_call_target="tpu_custom_call" | custom-call | tf_op jit(solution)/shard_map/translate/pallas_call | solution.py:323
  75.9 6.0 %all-to-all-start.2 = ((bf16[64,8,256]{2,1,0:T(8,128)(2,1)}), bf16[64,8,256]{2,1,0:T(8,128)(2,1)S(1)}, u32[]{:S(2)}, u32[]{:S(2)}) async-start(bf16[64,8,256]{2,1,0:T(8,128)(2,1)} %bitcast.2), calls=%async_computation.2 | async-start | bytes 524288 | tf_op jit(solution)/shard_map/all_to_all | solution.py:276
  81.9 0.0 collective-permute-done.1
  81.9 0.0 collective-permute-done.2
  81.9 1.4 %pad_maximum_fusion = bf16[48,128,128]{2,1,0:T(8,128)(2,1)} fusion(bf16[8,128,128]{2,1,0:T(8,128)(2,1)S(1)} %collective-permute-done.2, bf16[32,128,128]{2,1,0:T(8,128)(2,1)S(1)} %copy-done.2, bf16[8,128,128]{2,1,0:T(8,128)(2,1)S(1)} %collective-permute-done.1), kind=kLoop, calls=%fused_computation.1 | loop fusion | flops 1572864 | bytes 3145728 | tf_op jit(solution)/shard_map/concatenate | solution.py:250
  83.3 3.3 %gather_fusion = bf16[40,128,128]{2,1,0:T(8,128)(2,1)} fusion(bf16[48,128,128]{2,1,0:T(8,128)(2,1)} %pad_maximum_fusion, s32[1024]{0:T(1024)S(1)} %pad_clamp_fusion), kind=kCustom, calls=%fused_computation | custom fusion | bytes 2621600 | tf_op jit(solution)/shard_map/gather | solution.py:252
  86.6 2.2 %fusion.6 = f32[4,128,128]{2,1,0:T(8,128)S(1)} fusion(bf16[4,10,128,128]{3,2,1,0:T(8,128)(2,1)} %bitcast.31, bf16[4,10,2,128,128]{4,3,2,1,0:T(8,128)(2,1)} %param.13), kind=kOutput, calls=%fused_computation.8 | convolution fusion | flops 167772160 | bytes 2883584 | tf_op jit(solution)/shard_map/cjab,cjbr->car/dot_general | solution.py:253
  88.8 5.1 %all-to-all-done.2 = bf16[64,8,256]{2,1,0:T(8,128)(2,1)S(1)} async-done(((bf16[64,8,256]{2,1,0:T(8,128)(2,1)}), bf16[64,8,256]{2,1,0:T(8,128)(2,1)S(1)}, u32[]{:S(2)}, u32[]{:S(2)}) %all-to-all-start.2) | async-done | bytes 262176 | tf_op jit(solution)/shard_map/all_to_all | solution.py:276
  93.9 3.5 %descend.1 = bf16[8,64,256]{2,1,0:T(8,128)(2,1)} custom-call(s32[32]{0:T(128)S(1)} %copy-done.1, bf16[4,8,2,8,256]{4,3,2,1,0:T(8,128)(2,1)S(1)} %bitcast.30, bf16[8,128,256]{2,1,0:T(8,128)(2,1)S(1)} %slice.38.half, bf16[8,128,256]{2,1,0:T(8,128)(2,1)S(1)} %collective-permute-done.other, f32[8,2048]{1,0:T(8,128)S(1)} %get-tuple-element.14.cosine, ...), custom_call_target="tpu_custom_call" | custom-call | tf_op jit(solution)/shard_map/descend/pallas_call | solution.py:340
  97.4 3.4 %all-to-all-start.3 = ((bf16[8,64,256]{2,1,0:T(8,128)(2,1)}), bf16[8,64,256]{2,1,0:T(8,128)(2,1)S(1)}, u32[]{:S(2)}, u32[]{:S(2)}) async-start(bf16[8,64,256]{2,1,0:T(8,128)(2,1)} %descend.1), calls=%async_computation.3 | async-start | bytes 524288 | tf_op jit(solution)/shard_map/all_to_all | solution.py:276
  100.8 2.2 %fusion.9 = f32[4,128,128]{2,1,0:T(8,128)S(1)} fusion(bf16[4,10,128,128]{3,2,1,0:T(8,128)(2,1)} %bitcast.32, bf16[4,10,2,128,128]{4,3,2,1,0:T(8,128)(2,1)} %param.13), kind=kOutput, calls=%fused_computation.9 | convolution fusion | flops 167772160 | bytes 2883584 | tf_op jit(solution)/shard_map/cjab,cjbr->car/dot_general | solution.py:256
  103.0 0.0 copy-start
  103.0 0.2 slice_subtract_fusion
  103.2 0.1 pad_maximum_fusion.1.near
  103.4 9.6 %all-to-all-done.3.got = bf16[8,64,256]{2,1,0:T(8,128)(2,1)S(1)} async-done(((bf16[8,64,256]{2,1,0:T(8,128)(2,1)}), bf16[8,64,256]{2,1,0:T(8,128)(2,1)S(1)}, u32[]{:S(2)}, u32[]{:S(2)}) %all-to-all-start.3) | async-done | bytes 262176 | tf_op jit(solution)/shard_map/all_to_all | solution.py:276
  113.0 0.0 copy-done
  113.0 1.1 %finish.1 = bf16[4,128,128]{2,1,0:T(8,128)(2,1)} custom-call(bf16[8,64,256]{2,1,0:T(8,128)(2,1)S(1)} %all-to-all-done.3.got, bf16[4,2,256,128]{3,2,1,0:T(8,128)(2,1)S(1)} %copy-done, f32[4,128,128]{2,1,0:T(8,128)S(1)} %pad_maximum_fusion.1.near), custom_call_target="tpu_custom_call" | custom-call | tf_op jit(solution)/shard_map/finish/pallas_call | solution.py:355
  (5 shorter events, 0.1 us)
Async XLA Ops:
  3.0 7.8 %copy-start.6 = (s32[4,16]{1,0:T(4,128)S(1)}, s32[4,16]{1,0:T(4,128)}, u32[]{:S(2)}) copy-start(s32[4,16]{1,0:T(4,128)} %param.20) | copy-start | bytes 772
  3.0 7.8 %copy-start.4 = (s32[4,16]{1,0:T(4,128)S(1)}, s32[4,16]{1,0:T(4,128)}, u32[]{:S(2)}) copy-start(s32[4,16]{1,0:T(4,128)} %param.19) | copy-start | bytes 772
  3.0 7.8 %copy-start.5 = (s32[4,16]{1,0:T(4,128)S(1)}, s32[4,16]{1,0:T(4,128)}, u32[]{:S(2)}) copy-start(s32[4,16]{1,0:T(4,128)} %param.18) | copy-start | bytes 772
  3.0 34.7 %copy-start.3 = (f32[8,2048]{1,0:T(8,128)S(1)}, f32[8,2048]{1,0:T(8,128)}, u32[]{:S(2)}) copy-start(f32[8,2048]{1,0:T(8,128)} %param.17) | copy-start | bytes 196612
  3.1 34.9 %copy-start.1 = (s32[32]{0:T(128)S(1)}, s32[32]{0:T(128)}, u32[]{:S(2)}) copy-start(s32[32]{0:T(128)} %slots.3) | copy-start | bytes 388
  3.1 29.6 %all-to-all-start = ((bf16[8,200,256]{2,1,0:T(8,128)(2,1)}), bf16[8,200,256]{2,1,0:T(8,128)(2,1)S(1)}, u32[]{:S(2)}, u32[]{:S(2)}) async-start(bf16[8,200,256]{2,1,0:T(8,128)(2,1)} %radiate.1), calls=%async_computation | async-start | bytes 1638400 | tf_op jit(solution)/shard_map/all_to_all | solution.py:276
  32.8 8.3 %collective-permute-start = (bf16[8,128,256]{2,1,0:T(8,128)(2,1)S(1)}, bf16[8,128,256]{2,1,0:T(8,128)(2,1)S(1)}, u32[]{:S(2)}, u32[]{:S(2)}) collective-permute-start(bf16[8,128,256]{2,1,0:T(8,128)(2,1)S(1)} %slice.38.half), channel_id=1, source_target_pairs={{0,8},{8,0},{16,24},{24,16},{32,40},{40,32},{48,56},{56,48},{64,72... | collective-permute-start | bytes 1572872 | tf_op jit(solution)/shard_map/ppermute | solution.py:299
  41.1 16.3 %copy-start.2 = (bf16[32,128,128]{2,1,0:T(8,128)(2,1)S(1)}, bf16[32,128,128]{2,1,0:T(8,128)(2,1)}, u32[]{:S(2)}) copy-start(bf16[32,128,128]{2,1,0:T(8,128)(2,1)} %cur.1) | copy-start | bytes 3145732
  43.8 19.8 %copy-start.7 = (s32[4,10]{1,0:T(4,128)S(1)}, s32[4,10]{1,0:T(4,128)}, u32[]{:S(2)}) copy-start(s32[4,10]{1,0:T(4,128)} %param.14) | copy-start | bytes 484
  43.8 28.4 %all-to-all-start.1 = ((bf16[64,8,384]{2,1,0:T(8,128)(2,1)}), bf16[64,8,384]{2,1,0:T(8,128)(2,1)S(1)}, u32[]{:S(2)}, u32[]{:S(2)}) async-start(bf16[64,8,384]{2,1,0:T(8,128)(2,1)} %bitcast), calls=%async_computation.1 | async-start | bytes 786432 | tf_op jit(solution)/shard_map/all_to_all | solution.py:276
  58.1 23.8 %collective-permute-start.1 = (bf16[8,128,128]{2,1,0:T(8,128)(2,1)}, bf16[8,128,128]{2,1,0:T(8,128)(2,1)S(1)}, u32[]{:S(2)}, u32[]{:S(2)}) collective-permute-start(bf16[8,128,128]{2,1,0:T(8,128)(2,1)} %get-tuple-element.9), channel_id=1, source_target_pairs={{0,8},{8,16},{16,24},{24,32},{32,40},{40,48},{48,56},{56,64},{64,7... | collective-permute-start | bytes 786440 | tf_op jit(solution)/shard_map/ppermute | solution.py:248
  61.7 20.3 %collective-permute-start.2 = (bf16[8,128,128]{2,1,0:T(8,128)(2,1)S(1)}, bf16[8,128,128]{2,1,0:T(8,128)(2,1)S(1)}, u32[]{:S(2)}, u32[]{:S(2)}) collective-permute-start(bf16[8,128,128]{2,1,0:T(8,128)(2,1)S(1)} %get-tuple-element.10), channel_id=1, source_target_pairs={{8,0},{16,8},{24,16},{32,24},{40,32},{48,40},{56,48},{64,56},{72,6... | collective-permute-start | bytes 786440 | tf_op jit(solution)/shard_map/ppermute | solution.py:249
  75.9 18.0 %all-to-all-start.2 = ((bf16[64,8,256]{2,1,0:T(8,128)(2,1)}), bf16[64,8,256]{2,1,0:T(8,128)(2,1)S(1)}, u32[]{:S(2)}, u32[]{:S(2)}) async-start(bf16[64,8,256]{2,1,0:T(8,128)(2,1)} %bitcast.2), calls=%async_computation.2 | async-start | bytes 524288 | tf_op jit(solution)/shard_map/all_to_all | solution.py:276
  97.4 15.6 %all-to-all-start.3 = ((bf16[8,64,256]{2,1,0:T(8,128)(2,1)}), bf16[8,64,256]{2,1,0:T(8,128)(2,1)S(1)}, u32[]{:S(2)}, u32[]{:S(2)}) async-start(bf16[8,64,256]{2,1,0:T(8,128)(2,1)} %descend.1), calls=%async_computation.3 | async-start | bytes 524288 | tf_op jit(solution)/shard_map/all_to_all | solution.py:276
  103.0 9.9 %copy-start = (bf16[4,2,256,128]{3,2,1,0:T(8,128)(2,1)S(1)}, bf16[4,2,256,128]{3,2,1,0:T(8,128)(2,1)}, u32[]{:S(2)}) copy-start(bf16[4,2,256,128]{3,2,1,0:T(8,128)(2,1)} %rad.1) | copy-start | bytes 1572868

commit v3 on v2

--- a/solution.py
+++ b/solution.py
@@ -71,69 +71,64 @@
     return pl.ds(pl.multiple_of(k * 256 + (1 - core) * 128, 128), 128)
 
 
-def lift_half(rows, matrix, cos, sin):
-    reals, imags = [], []
+def lift_halves(rows, matrix, cosines, sines):
+    reals, imags = ([], []), ([], [])
     for p in range(4):
         lifted = nt_dot(rows[128 * p : 128 * p + 128, :], matrix)
-        real_sum = imag_sum = None
-        for o in range(8):
-            re = lifted[16 * o : 16 * o + 8]
-            im = lifted[16 * o + 8 : 16 * o + 16]
-            co, si = cos[o : o + 1], sin[o : o + 1]
-            real = re * co - im * si
-            imag = re * si + im * co
-            real_sum = real if real_sum is None else real_sum + real
-            imag_sum = imag if imag_sum is None else imag_sum + imag
-        reals.append(real_sum)
-        imags.append(imag_sum)
-    return jnp.swapaxes(jnp.stack(reals + imags, axis=0), 0, 1).astype(BF)
+        for h in range(2):
+            lanes = slice(128 * h, 128 * h + 128)
+            real_sum = imag_sum = None
+            for o in range(8):
+                re = lifted[16 * o : 16 * o + 8, lanes]
+                im = lifted[16 * o + 8 : 16 * o + 16, lanes]
+                co, si = cosines[h][o : o + 1], sines[h][o : o + 1]
+                real = re * co - im * si
+                imag = re * si + im * co
+                real_sum = real if real_sum is None else real_sum + real
+                imag_sum = imag if imag_sum is None else imag_sum + imag
+            reals[h].append(real_sum)
+            imags[h].append(imag_sum)
+    stacks = [jnp.stack(reals[h] + imags[h], axis=0) for h in range(2)]
+    return [jnp.swapaxes(stack, 0, 1).astype(BF) for stack in stacks]
 
 
 def lift_own_kernel(slots, got, cosine, sine, out, rows, inverse):
-    def note(c, carry):
+    for c in range(32):
         inverse[slots[c]] = c
-        return carry
-
-    lax.fori_loop(0, 32, note, 0)
-
-    def collect(n, carry):
+    for n in range(32):
         c = inverse[n]
         src = pl.multiple_of(lax.rem(c, 4) * 16, 16)
-        dst = pl.multiple_of(n * 16, 16)
-        rows[pl.ds(dst, 16), :] = got[lax.div(c, 4), pl.ds(src, 16), :]
-        return carry
-
-    lax.fori_loop(0, 32, collect, 0)
-
-    def step(k, carry):
-        lanes = own_lanes(k)
-        block = lift_half(rows, got[k, 64:192, :], cosine[:, lanes], sine[:, lanes])
-        for r in range(8):
-            out[r // 2, k, r % 2] = block[r]
-        return carry
-
-    lax.fori_loop(0, 8, step, 0)
+        rows[16 * n : 16 * n + 16, :] = got[lax.div(c, 4), pl.ds(src, 16), :]
+    for k in range(0, 8, 2):
+        lanes = [own_lanes(k), own_lanes(k + 1)]
+        matrix = jnp.concatenate([got[k, 64:192, :], got[k + 1, 64:192, :]], axis=0)
+        cosines = [cosine[:, at] for at in lanes]
+        sines = [sine[:, at] for at in lanes]
+        blocks = lift_halves(rows, matrix, cosines, sines)
+        for h in range(2):
+            for r in range(8):
+                out[r // 2, k + h, r % 2] = blocks[h][r]
 
 
 def lift_other_kernel(first, rows, got, other, lists, cosine, sine, out):
     row = rows_of((8, 128), 0)
-
-    def step(k, carry):
-        lanes = other_lanes(k)
-        block = lift_half(rows, other[k], cosine[:, lanes], sine[:, lanes])
-        tran = got[k, 192:200, :].astype(F32)
-        tile = lists[...]
-        for j in range(4):
-            piece = tran[j // 2 : j // 2 + 1, 128 * (j % 2) : 128 * (j % 2) + 128]
-            tile = jnp.where(row == 4 + j, piece, tile)
-        tile = tile.astype(BF)
-        for r in range(8):
-            out[r // 2, k, r % 2, :, 0:128] = first[r // 2, k, r % 2]
-            out[r // 2, k, r % 2, :, 128:256] = block[r]
-            out[r // 2, k, r % 2, :, 256:384] = tile
-        return carry
-
-    lax.fori_loop(0, 8, step, 0)
+    for k in range(0, 8, 2):
+        lanes = [other_lanes(k), other_lanes(k + 1)]
+        matrix = jnp.concatenate([other[k], other[k + 1]], axis=0)
+        cosines = [cosine[:, at] for at in lanes]
+        sines = [sine[:, at] for at in lanes]
+        blocks = lift_halves(rows, matrix, cosines, sines)
+        for h in range(2):
+            tran = got[k + h, 192:200, :].astype(F32)
+            tile = lists[...]
+            for j in range(4):
+                piece = tran[j // 2 : j // 2 + 1, 128 * (j % 2) : 128 * (j % 2) + 128]
+                tile = jnp.where(row == 4 + j, piece, tile)
+            tile = tile.astype(BF)
+            for r in range(8):
+                out[r // 2, k + h, r % 2, :, 0:128] = first[r // 2, k + h, r % 2]
+                out[r // 2, k + h, r % 2, :, 128:256] = blocks[h][r]
+                out[r // 2, k + h, r % 2, :, 256:384] = tile
 
 
 def translate_kernel(got, out, table, codes, tran, real_acc, imag_acc):
@@ -185,34 +180,30 @@
 
 
 def descend_kernel(slots, got, half, other, cosine, sine, out, lhs, acc):
-    acc[...] = jnp.zeros_like(acc)
-
-    def step(k, carry):
-        mine, theirs = own_lanes(k), other_lanes(k)
-        cos = jnp.concatenate([cosine[:, mine], cosine[:, theirs]], axis=1)
-        sin = jnp.concatenate([sine[:, mine], sine[:, theirs]], axis=1)
+    for k in range(8):
         block = jnp.stack([got[r // 2, k, r % 2].astype(F32) for r in range(8)], axis=0)
         block = jnp.swapaxes(block, 0, 1)
-        for p in range(4):
-            re, im = block[p], block[4 + p]
+        for h, at in enumerate((own_lanes(k), other_lanes(k))):
+            lanes = slice(128 * h, 128 * h + 128)
+            cos, sin = cosine[:, at], sine[:, at]
             for o in range(8):
-                co, si = cos[o : o + 1], sin[o : o + 1]
-                both = jnp.concatenate([re * co + im * si, im * co - re * si], axis=0)
-                n = 8 * p + o
-                lhs[16 * n : 16 * n + 16, :] = both.astype(BF)
-        whole = jnp.concatenate([half[k], other[k]], axis=0)
-        acc[...] += nn_dot(lhs[...], whole)
-        return carry
-
-    lax.fori_loop(0, 8, step, 0)
-
-    def place(c, carry):
+                co = jnp.broadcast_to(cos[o : o + 1], (8, 128))
+                si = jnp.broadcast_to(sin[o : o + 1], (8, 128))
+                for p in range(4):
+                    re, im = block[p][:, lanes], block[4 + p][:, lanes]
+                    both = jnp.concatenate([re * co + im * si, im * co - re * si], axis=0)
+                    n = 8 * p + o
+                    lhs[k, 16 * n : 16 * n + 16, lanes] = both.astype(BF)
+    for first in range(0, 512, 256):
+        total = None
+        for k in range(8):
+            whole = jnp.concatenate([half[k], other[k]], axis=0)
+            part = nn_dot(lhs[k, first : first + 256, :], whole)
+            total = part if total is None else total + part
+        acc[first : first + 256, :] = total
+    for c in range(32):
         src = pl.multiple_of(slots[c] * 16, 16)
-        dst = pl.multiple_of(lax.rem(c, 4) * 16, 16)
-        out[lax.div(c, 4), pl.ds(dst, 16), :] = acc[pl.ds(src, 16), :].astype(BF)
-        return carry
-
-    lax.fori_loop(0, 32, place, 0)
+        out[c // 4, 16 * (c % 4) : 16 * (c % 4) + 16, :] = acc[pl.ds(src, 16), :].astype(BF)
 
 
 def finish_kernel(got, rad, near, out):
@@ -344,7 +335,7 @@
         in_specs=[SM, VM, VM, VM, VM, VM],
         out_specs=VM,
         scratch_shapes=[
-            pltpu.VMEM((512, 256), BF),
+            pltpu.VMEM((8, 512, 256), BF),
             pltpu.VMEM((512, 256), F32),
         ],
         compiler_params=params(),

time: 115 us -> 111 us (0.965)
  Pallas kernels: 17.3 us -> 13.3 us
    pallas_call x1, Pallas kernels: 3.11 us -> 1.36 us  [body(): pl.pallas_call(lift_own_kernel, name='lift_own', out_shape=(jax.ShapeDtyp...]
  transfers between devices with their start and end apart: 7 -> 7, of which waited for: 4 -> 4; matrix products, arithmetic and copies ran while one was open for 9% -> 10% of each run, Pallas kernels for 6% -> 5%
where the time goes in v3:
time: 111 us; the launch traced here: 110 us
  waiting for transfers between devices  44.9 us (40%)
  starting transfers between devices  41.1 us (37%)
  Pallas kernels  13.3 us (12%)
  local copies, waits for them, and re-layouts  4.44 us (4%)
  matrix products  4.41 us (4%)
  other arithmetic  1.79 us (2%)
    all_to_all x4, waiting for transfers between devices, body(): lax.all_to_all(x, axis, split_axis=0, concat_axis=0, tiled=True)  44.9 us
    all_to_all x4, starting transfers between devices, body(): lax.all_to_all(x, axis, split_axis=0, concat_axis=0, tiled=True)  30.8 us
    ppermute x1, starting transfers between devices, body(): other = lax.ppermute(half, 'clus', partner)  4.86 us
    pallas_call x1, Pallas kernels, body(): pl.pallas_call(translate_kernel, name='translate', out_shape=jax.ShapeDty...  3.74 us
    ppermute x1, starting transfers between devices, near_field(): low = lax.ppermute(currents[group - margin:], 'clus', up)  3.53 us
    gather x1, local copies, waits for them, and re-layouts, near_field(): neighbours = window[local]  3.28 us
    pallas_call x1, Pallas kernels, body(): pl.pallas_call(radiate_kernel, name='radiate', out_shape=jax.ShapeDtypeSt...  3 us
    pallas_call x1, Pallas kernels, body(): pl.pallas_call(descend_kernel, name='descend', out_shape=jax.ShapeDtypeSt...  2.41 us
  transfers between devices with their start and end apart: 7, of which 4 were waited for; matrix products, arithmetic and copies ran while one was open for 10% of the time, Pallas kernels for 5%

profile of v3, /device:TPU:1, one launch (start us, length us, event | category | flops | bytes accessed | tf_op | source)
XLA Modules:
  0.0 110.2 jit_solution(10077877844810769288)
XLA Ops:
  0.0 3.0 %radiate.1 = bf16[8,200,256]{2,1,0:T(8,128)(2,1)} custom-call(bf16[32,128,128]{2,1,0:T(8,128)(2,1)} %cur.1, bf16[4,2,256,128]{3,2,1,0:T(8,128)(2,1)} %rad.1, bf16[256,256]{1,0:T(8,128)(2,1)} %itp.1, bf16[64,2,256]{2,1,0:T(2,128)(2,1)} %tra.1), custom_call_target="tpu_custom_call" | custom-call | tf_op jit(solution)/shard_map/radiate/pallas_call | solution.py:273
  3.0 0.0 copy-start.6
  3.0 0.0 copy-start.4
  3.0 0.0 copy-start.5
  3.0 0.0 copy-start.3
  3.1 0.0 copy-start.1
  3.1 7.8 %all-to-all-start = ((bf16[8,200,256]{2,1,0:T(8,128)(2,1)}), bf16[8,200,256]{2,1,0:T(8,128)(2,1)S(1)}, u32[]{:S(2)}, u32[]{:S(2)}) async-start(bf16[8,200,256]{2,1,0:T(8,128)(2,1)} %radiate.1), calls=%async_computation | async-start | bytes 1638400 | tf_op jit(solution)/shard_map/all_to_all | solution.py:267
  10.9 0.0 copy-done.6
  10.9 0.0 copy-done.4
  10.9 0.0 copy-done.5
  10.9 21.8 %all-to-all-done.got = bf16[8,200,256]{2,1,0:T(8,128)(2,1)S(1)} async-done(((bf16[8,200,256]{2,1,0:T(8,128)(2,1)}), bf16[8,200,256]{2,1,0:T(8,128)(2,1)S(1)}, u32[]{:S(2)}, u32[]{:S(2)}) %all-to-all-start) | async-done | bytes 819232 | tf_op jit(solution)/shard_map/all_to_all | solution.py:267
  32.8 4.9 %collective-permute-start = (bf16[8,128,256]{2,1,0:T(8,128)(2,1)S(1)}, bf16[8,128,256]{2,1,0:T(8,128)(2,1)S(1)}, u32[]{:S(2)}, u32[]{:S(2)}) collective-permute-start(bf16[8,128,256]{2,1,0:T(8,128)(2,1)S(1)} %slice.38.half), channel_id=1, source_target_pairs={{0,8},{8,0},{16,24},{24,16},{32,40},{40,32},{48,56},{56,48},{64,72... | collective-permute-start | bytes 1572872 | tf_op jit(solution)/shard_map/ppermute | solution.py:290
  37.6 0.1 pad_add_fusion.lists
  37.7 0.0 copy-done.3
  37.7 0.2 fusion.13
  37.9 0.0 copy-done.1
  38.0 1.4 %lift_own.1 = (bf16[4,8,2,8,128]{4,3,2,1,0:T(8,128)(2,1)S(1)}, bf16[512,256]{1,0:T(8,128)(2,1)S(1)}) custom-call(s32[32]{0:T(128)S(1)} %copy-done.1, bf16[8,200,256]{2,1,0:T(8,128)(2,1)S(1)} %all-to-all-done.got, f32[8,2048]{1,0:T(8,128)S(1)} %get-tuple-element.14.cosine, f32[8,2048]{1,0:T(8,128)S(1)} %get-tuple-element.13.sine), custom_call_target="tpu_custom_call" | custom-call | tf_op jit(solution)/shard_map/lift_own/pallas_call | solution.py:292
  39.3 0.0 collective-permute-done.other
  39.3 0.0 copy-start.2
  39.3 1.6 %lift_other.1 = bf16[4,8,2,8,384]{4,3,2,1,0:T(8,128)(2,1)} custom-call(bf16[4,8,2,8,128]{4,3,2,1,0:T(8,128)(2,1)S(1)} %get-tuple-element.7.first, bf16[512,256]{1,0:T(8,128)(2,1)S(1)} %get-tuple-element.8.rows, bf16[8,200,256]{2,1,0:T(8,128)(2,1)S(1)} %all-to-all-done.got, bf16[8,128,256]{2,1,0:T(8,128)(2,1)S(1)} %collective-permute-done.other, ...), custom_call_target="tpu_custom_call" | custom-call | tf_op jit(solution)/shard_map/lift_other/pallas_call | solution.py:304
  41.0 0.0 copy-start.7
  41.0 13.6 %all-to-all-start.1 = ((bf16[64,8,384]{2,1,0:T(8,128)(2,1)}), bf16[64,8,384]{2,1,0:T(8,128)(2,1)S(1)}, u32[]{:S(2)}, u32[]{:S(2)}) async-start(bf16[64,8,384]{2,1,0:T(8,128)(2,1)} %bitcast), calls=%async_computation.1 | async-start | bytes 786432 | tf_op jit(solution)/shard_map/all_to_all | solution.py:267
  54.5 0.0 copy-done.2
  54.6 0.8 fusion.12
  55.3 3.5 %collective-permute-start.1 = (bf16[8,128,128]{2,1,0:T(8,128)(2,1)}, bf16[8,128,128]{2,1,0:T(8,128)(2,1)S(1)}, u32[]{:S(2)}, u32[]{:S(2)}) collective-permute-start(bf16[8,128,128]{2,1,0:T(8,128)(2,1)} %get-tuple-element.9), channel_id=1, source_target_pairs={{0,8},{8,16},{16,24},{24,32},{32,40},{40,48},{48,56},{56,64},{64,7... | collective-permute-start | bytes 786440 | tf_op jit(solution)/shard_map/ppermute | solution.py:239
  58.8 1.9 %collective-permute-start.2 = (bf16[8,128,128]{2,1,0:T(8,128)(2,1)S(1)}, bf16[8,128,128]{2,1,0:T(8,128)(2,1)S(1)}, u32[]{:S(2)}, u32[]{:S(2)}) collective-permute-start(bf16[8,128,128]{2,1,0:T(8,128)(2,1)S(1)} %get-tuple-element.10), channel_id=1, source_target_pairs={{8,0},{16,8},{24,16},{32,24},{40,32},{48,40},{56,48},{64,56},{72,6... | collective-permute-start | bytes 786440 | tf_op jit(solution)/shard_map/ppermute | solution.py:240
  60.8 0.0 copy-done.7
  60.8 0.1 reshape.18
  60.9 8.5 %all-to-all-done.1 = bf16[64,8,384]{2,1,0:T(8,128)(2,1)S(1)} async-done(((bf16[64,8,384]{2,1,0:T(8,128)(2,1)}), bf16[64,8,384]{2,1,0:T(8,128)(2,1)S(1)}, u32[]{:S(2)}, u32[]{:S(2)}) %all-to-all-start.1) | async-done | bytes 393248 | tf_op jit(solution)/shard_map/all_to_all | solution.py:267
  69.3 3.7 %translate.1 = bf16[32,2,8,256]{3,2,1,0:T(8,128)(2,1)} custom-call(bf16[32,2,8,384]{3,2,1,0:T(8,128)(2,1)S(1)} %bitcast.29), custom_call_target="tpu_custom_call" | custom-call | tf_op jit(solution)/shard_map/translate/pallas_call | solution.py:314
  73.1 6.0 %all-to-all-start.2 = ((bf16[64,8,256]{2,1,0:T(8,128)(2,1)}), bf16[64,8,256]{2,1,0:T(8,128)(2,1)S(1)}, u32[]{:S(2)}, u32[]{:S(2)}) async-start(bf16[64,8,256]{2,1,0:T(8,128)(2,1)} %bitcast.2), calls=%async_computation.2 | async-start | bytes 524288 | tf_op jit(solution)/shard_map/all_to_all | solution.py:267
  79.1 0.0 collective-permute-done.1
  79.1 0.0 collective-permute-done.2
  79.1 1.4 %pad_maximum_fusion = bf16[48,128,128]{2,1,0:T(8,128)(2,1)} fusion(bf16[8,128,128]{2,1,0:T(8,128)(2,1)S(1)} %collective-permute-done.2, bf16[32,128,128]{2,1,0:T(8,128)(2,1)S(1)} %copy-done.2, bf16[8,128,128]{2,1,0:T(8,128)(2,1)S(1)} %collective-permute-done.1), kind=kLoop, calls=%fused_computation.1 | loop fusion | flops 1572864 | bytes 3145728 | tf_op jit(solution)/shard_map/concatenate | solution.py:241
  80.5 3.3 %gather_fusion = bf16[40,128,128]{2,1,0:T(8,128)(2,1)} fusion(bf16[48,128,128]{2,1,0:T(8,128)(2,1)} %pad_maximum_fusion, s32[1024]{0:T(1024)S(1)} %pad_clamp_fusion), kind=kCustom, calls=%fused_computation | custom fusion | bytes 2621600 | tf_op jit(solution)/shard_map/gather | solution.py:243
  83.7 2.2 %fusion.6 = f32[4,128,128]{2,1,0:T(8,128)S(1)} fusion(bf16[4,10,128,128]{3,2,1,0:T(8,128)(2,1)} %bitcast.31, bf16[4,10,2,128,128]{4,3,2,1,0:T(8,128)(2,1)} %param.13), kind=kOutput, calls=%fused_computation.8 | convolution fusion | flops 167772160 | bytes 2883584 | tf_op jit(solution)/shard_map/cjab,cjbr->car/dot_general | solution.py:244
  86.0 5.1 %all-to-all-done.2 = bf16[64,8,256]{2,1,0:T(8,128)(2,1)S(1)} async-done(((bf16[64,8,256]{2,1,0:T(8,128)(2,1)}), bf16[64,8,256]{2,1,0:T(8,128)(2,1)S(1)}, u32[]{:S(2)}, u32[]{:S(2)}) %all-to-all-start.2) | async-done | bytes 262176 | tf_op jit(solution)/shard_map/all_to_all | solution.py:267
  91.0 2.4 %descend.1 = bf16[8,64,256]{2,1,0:T(8,128)(2,1)} custom-call(s32[32]{0:T(128)S(1)} %copy-done.1, bf16[4,8,2,8,256]{4,3,2,1,0:T(8,128)(2,1)S(1)} %bitcast.30, bf16[8,128,256]{2,1,0:T(8,128)(2,1)S(1)} %slice.38.half, bf16[8,128,256]{2,1,0:T(8,128)(2,1)S(1)} %collective-permute-done.other, f32[8,2048]{1,0:T(8,128)S(1)} %get-tuple-element.14.cosine, ...), custom_call_target="tpu_custom_call" | custom-call | tf_op jit(solution)/shard_map/descend/pallas_call | solution.py:331
  93.5 3.4 %all-to-all-start.3 = ((bf16[8,64,256]{2,1,0:T(8,128)(2,1)}), bf16[8,64,256]{2,1,0:T(8,128)(2,1)S(1)}, u32[]{:S(2)}, u32[]{:S(2)}) async-start(bf16[8,64,256]{2,1,0:T(8,128)(2,1)} %descend.1), calls=%async_computation.3 | async-start | bytes 524288 | tf_op jit(solution)/shard_map/all_to_all | solution.py:267
  96.9 2.2 %fusion.9 = f32[4,128,128]{2,1,0:T(8,128)S(1)} fusion(bf16[4,10,128,128]{3,2,1,0:T(8,128)(2,1)} %bitcast.32, bf16[4,10,2,128,128]{4,3,2,1,0:T(8,128)(2,1)} %param.13), kind=kOutput, calls=%fused_computation.9 | convolution fusion | flops 167772160 | bytes 2883584 | tf_op jit(solution)/shard_map/cjab,cjbr->car/dot_general | solution.py:247
  99.1 0.0 copy-start
  99.1 0.2 slice_subtract_fusion
  99.3 0.1 pad_maximum_fusion.1.near
  99.4 9.6 %all-to-all-done.3.got = bf16[8,64,256]{2,1,0:T(8,128)(2,1)S(1)} async-done(((bf16[8,64,256]{2,1,0:T(8,128)(2,1)}), bf16[8,64,256]{2,1,0:T(8,128)(2,1)S(1)}, u32[]{:S(2)}, u32[]{:S(2)}) %all-to-all-start.3) | async-done | bytes 262176 | tf_op jit(solution)/shard_map/all_to_all | solution.py:267
  109.0 0.0 copy-done
  109.0 1.1 %finish.1 = bf16[4,128,128]{2,1,0:T(8,128)(2,1)} custom-call(bf16[8,64,256]{2,1,0:T(8,128)(2,1)S(1)} %all-to-all-done.3.got, bf16[4,2,256,128]{3,2,1,0:T(8,128)(2,1)S(1)} %copy-done, f32[4,128,128]{2,1,0:T(8,128)S(1)} %pad_maximum_fusion.1.near), custom_call_target="tpu_custom_call" | custom-call | tf_op jit(solution)/shard_map/finish/pallas_call | solution.py:346
  (5 shorter events, 0.1 us)
Async XLA Ops:
  3.0 7.8 %copy-start.6 = (s32[4,16]{1,0:T(4,128)S(1)}, s32[4,16]{1,0:T(4,128)}, u32[]{:S(2)}) copy-start(s32[4,16]{1,0:T(4,128)} %param.20) | copy-start | bytes 772
  3.0 7.8 %copy-start.4 = (s32[4,16]{1,0:T(4,128)S(1)}, s32[4,16]{1,0:T(4,128)}, u32[]{:S(2)}) copy-start(s32[4,16]{1,0:T(4,128)} %param.19) | copy-start | bytes 772
  3.0 7.8 %copy-start.5 = (s32[4,16]{1,0:T(4,128)S(1)}, s32[4,16]{1,0:T(4,128)}, u32[]{:S(2)}) copy-start(s32[4,16]{1,0:T(4,128)} %param.18) | copy-start | bytes 772
  3.0 34.7 %copy-start.3 = (f32[8,2048]{1,0:T(8,128)S(1)}, f32[8,2048]{1,0:T(8,128)}, u32[]{:S(2)}) copy-start(f32[8,2048]{1,0:T(8,128)} %param.17) | copy-start | bytes 196612
  3.1 34.9 %copy-start.1 = (s32[32]{0:T(128)S(1)}, s32[32]{0:T(128)}, u32[]{:S(2)}) copy-start(s32[32]{0:T(128)} %slots.3) | copy-start | bytes 388
  3.1 29.6 %all-to-all-start = ((bf16[8,200,256]{2,1,0:T(8,128)(2,1)}), bf16[8,200,256]{2,1,0:T(8,128)(2,1)S(1)}, u32[]{:S(2)}, u32[]{:S(2)}) async-start(bf16[8,200,256]{2,1,0:T(8,128)(2,1)} %radiate.1), calls=%async_computation | async-start | bytes 1638400 | tf_op jit(solution)/shard_map/all_to_all | solution.py:267
  32.8 6.6 %collective-permute-start = (bf16[8,128,256]{2,1,0:T(8,128)(2,1)S(1)}, bf16[8,128,256]{2,1,0:T(8,128)(2,1)S(1)}, u32[]{:S(2)}, u32[]{:S(2)}) collective-permute-start(bf16[8,128,256]{2,1,0:T(8,128)(2,1)S(1)} %slice.38.half), channel_id=1, source_target_pairs={{0,8},{8,0},{16,24},{24,16},{32,40},{40,32},{48,56},{56,48},{64,72... | collective-permute-start | bytes 1572872 | tf_op jit(solution)/shard_map/ppermute | solution.py:290
  39.3 15.2 %copy-start.2 = (bf16[32,128,128]{2,1,0:T(8,128)(2,1)S(1)}, bf16[32,128,128]{2,1,0:T(8,128)(2,1)}, u32[]{:S(2)}) copy-start(bf16[32,128,128]{2,1,0:T(8,128)(2,1)} %cur.1) | copy-start | bytes 3145732
  41.0 19.8 %copy-start.7 = (s32[4,10]{1,0:T(4,128)S(1)}, s32[4,10]{1,0:T(4,128)}, u32[]{:S(2)}) copy-start(s32[4,10]{1,0:T(4,128)} %param.14) | copy-start | bytes 484
  41.0 28.4 %all-to-all-start.1 = ((bf16[64,8,384]{2,1,0:T(8,128)(2,1)}), bf16[64,8,384]{2,1,0:T(8,128)(2,1)S(1)}, u32[]{:S(2)}, u32[]{:S(2)}) async-start(bf16[64,8,384]{2,1,0:T(8,128)(2,1)} %bitcast), calls=%async_computation.1 | async-start | bytes 786432 | tf_op jit(solution)/shard_map/all_to_all | solution.py:267
  55.3 23.8 %collective-permute-start.1 = (bf16[8,128,128]{2,1,0:T(8,128)(2,1)}, bf16[8,128,128]{2,1,0:T(8,128)(2,1)S(1)}, u32[]{:S(2)}, u32[]{:S(2)}) collective-permute-start(bf16[8,128,128]{2,1,0:T(8,128)(2,1)} %get-tuple-element.9), channel_id=1, source_target_pairs={{0,8},{8,16},{16,24},{24,32},{32,40},{40,48},{48,56},{56,64},{64,7... | collective-permute-start | bytes 786440 | tf_op jit(solution)/shard_map/ppermute | solution.py:239
  58.8 20.3 %collective-permute-start.2 = (bf16[8,128,128]{2,1,0:T(8,128)(2,1)S(1)}, bf16[8,128,128]{2,1,0:T(8,128)(2,1)S(1)}, u32[]{:S(2)}, u32[]{:S(2)}) collective-permute-start(bf16[8,128,128]{2,1,0:T(8,128)(2,1)S(1)} %get-tuple-element.10), channel_id=1, source_target_pairs={{8,0},{16,8},{24,16},{32,24},{40,32},{48,40},{56,48},{64,56},{72,6... | collective-permute-start | bytes 786440 | tf_op jit(solution)/shard_map/ppermute | solution.py:240
  73.1 18.0 %all-to-all-start.2 = ((bf16[64,8,256]{2,1,0:T(8,128)(2,1)}), bf16[64,8,256]{2,1,0:T(8,128)(2,1)S(1)}, u32[]{:S(2)}, u32[]{:S(2)}) async-start(bf16[64,8,256]{2,1,0:T(8,128)(2,1)} %bitcast.2), calls=%async_computation.2 | async-start | bytes 524288 | tf_op jit(solution)/shard_map/all_to_all | solution.py:267
  93.5 15.6 %all-to-all-start.3 = ((bf16[8,64,256]{2,1,0:T(8,128)(2,1)}), bf16[8,64,256]{2,1,0:T(8,128)(2,1)S(1)}, u32[]{:S(2)}, u32[]{:S(2)}) async-start(bf16[8,64,256]{2,1,0:T(8,128)(2,1)} %descend.1), calls=%async_computation.3 | async-start | bytes 524288 | tf_op jit(solution)/shard_map/all_to_all | solution.py:267
  99.1 9.9 %copy-start = (bf16[4,2,256,128]{3,2,1,0:T(8,128)(2,1)S(1)}, bf16[4,2,256,128]{3,2,1,0:T(8,128)(2,1)}, u32[]{:S(2)}) copy-start(bf16[4,2,256,128]{3,2,1,0:T(8,128)(2,1)} %rad.1) | copy-start | bytes 1572868

commit v4 on v3

--- a/solution.py
+++ b/solution.py
@@ -28,26 +28,30 @@
     return lax.broadcasted_iota(jnp.int32, shape, dim)
 
 
-def radiate_kernel(cur, rad_all, itp, tra, out, own, rad, half_ref, tran, sems):
+def radiate_kernel(
+    cur, rad_all, itp, tra, out, own, rad, half, tran, data, extra, in_sems, out_sems
+):
     clus = lax.axis_index("clus")
     mine = pl.ds(pl.multiple_of(lax.rem(clus, 2) * 128, 128), 128)
     pairs = [
-        (itp.at[mine], half_ref),
+        (itp.at[mine], half),
         (tra.at[clus], tran),
         (cur.at[pl.ds(lax.axis_index("samp") * 4, 4)], own),
     ] + [(rad_all.at[c], rad.at[c]) for c in range(4)]
-    copies = [pltpu.make_async_copy(a, b, sems.at[i]) for i, (a, b) in enumerate(pairs)]
+    copies = [pltpu.make_async_copy(a, b, in_sems.at[i]) for i, (a, b) in enumerate(pairs)]
     for copy in copies:
         copy.start()
     copies[0].wait()
     copies[1].wait()
-    half = half_ref[...]
     trow = tran[...].astype(F32)
     row = rows_of((8, 256), 0)
-    extra = jnp.where(row == 0, trow[0:1], jnp.where(row == 1, trow[1:2], 0.0)).astype(BF)
+    extra[...] = jnp.where(row == 0, trow[0:1], jnp.where(row == 1, trow[1:2], 0.0)).astype(BF)
+    sends = []
     for s in range(8):
-        out[s, 64:192, :] = half
-        out[s, 192:200, :] = extra
+        sends.append(pltpu.make_async_copy(half, out.at[s, 64:192, :], out_sems.at[s]))
+        sends.append(pltpu.make_async_copy(extra, out.at[s, 192:200, :], out_sems.at[8 + s]))
+    for send in sends:
+        send.start()
     copies[2].wait()
     for c in range(4):
         copies[3 + c].wait()
@@ -58,7 +62,12 @@
         imag = with_real[64:] + with_imag[:64]
         for s in range(8):
             both = jnp.concatenate([real[8 * s : 8 * s + 8], imag[8 * s : 8 * s + 8]], axis=0)
-            out[s, 16 * c : 16 * c + 16, :] = both.astype(BF)
+            data[s, 16 * c : 16 * c + 16, :] = both.astype(BF)
+    last = pltpu.make_async_copy(data, out.at[:, 0:64, :], out_sems.at[16])
+    last.start()
+    for send in sends:
+        send.wait()
+    last.wait()
 
 
 def own_lanes(k):
@@ -150,21 +159,26 @@
     codes[...] = uppers(even, odd).astype(jnp.int32)
     pieces = lowers(even, odd).astype(BF)
     for j in range(4):
-        pick = rows_of((64, 256), 1) == rows_of((64, 256), 0) * 4 + j
+        pick = rows_of((128, 256), 1) == rows_of((128, 256), 0) * 4 + j
         part = nn_dot(pick.astype(F32).astype(BF), pieces)
         tran[:, 128 * j : 128 * j + 128] = part.astype(BF)
     col = rows_of((256, 256), 1)
-    kinds = rows_of((256, 64), 1)
-    for f in range(16):
-        pick = (col == codes[:, f : f + 1]).astype(F32).astype(BF)
-        kind = (kinds == codes[:, 16 + f : 17 + f]).astype(F32).astype(BF)
-        both = nn_dot(pick, table[...])
-        factor = nn_dot(kind, tran[...])
-        re, im = both[:, :256], both[:, 256:]
-        tre, tim = factor[:, :256], factor[:, 256:]
-        real = re * tre - im * tim
-        imag = re * tim + im * tre
-        if f == 0:
+    kinds = rows_of((256, 128), 1)
+    for first in range(0, 16, 4):
+        picks = [(col == codes[:, first + f : first + f + 1]).astype(F32) for f in range(4)]
+        turns = [(kinds == codes[:, 16 + first + f : 17 + first + f]).astype(F32) for f in range(4)]
+        both = nn_dot(jnp.concatenate([p.astype(BF) for p in picks], axis=0), table[...])
+        factor = nn_dot(jnp.concatenate([t.astype(BF) for t in turns], axis=0), tran[...])
+        real = imag = None
+        for f in range(4):
+            rows = slice(256 * f, 256 * f + 256)
+            re, im = both[rows, :256], both[rows, 256:]
+            tre, tim = factor[rows, :256], factor[rows, 256:]
+            add_real = re * tre - im * tim
+            add_imag = re * tim + im * tre
+            real = add_real if real is None else real + add_real
+            imag = add_imag if imag is None else imag + add_imag
+        if first == 0:
             real_acc[...] = real
             imag_acc[...] = imag
         else:
@@ -223,31 +237,46 @@
     return pltpu.CompilerParams(vmem_limit_bytes=limit)
 
 
-def combine_parts(with_real, with_imag, sign):
-    half_width = with_real.shape[-1] // 2
-    real_part = with_real[..., :half_width] - sign * with_imag[..., half_width:]
-    imag_part = with_real[..., half_width:] + sign * with_imag[..., :half_width]
-    return jnp.concatenate([real_part, imag_part], axis=-1)
-
-
-def near_field(currents, near_blocks, near_cols):
-    group = currents.shape[0]
-    margin = group // 4
-    count = lax.axis_size("clus")
-    up = [(i, i + 1) for i in range(count - 1)]
+def near_kernel(cols, low, cur, high, blocks, out, window, sems):
+    pairs = [(low, window.at[0:8]), (cur, window.at[8:40]), (high, window.at[40:48])]
+    copies = [pltpu.make_async_copy(a, b, sems.at[i]) for i, (a, b) in enumerate(pairs)]
+    for copy in copies:
+        copy.start()
+    for copy in copies:
+        copy.wait()
+    start = lax.axis_index("clus") * 32 - 8
+
+    def row(c, carry):
+        total = None
+        for j in range(10):
+            part = nn_dot(blocks[c, j].reshape(256, 128), window[cols[c, j] - start])
+            total = part if total is None else total + part
+        turned = pltpu.roll(total[128:], 64, 1)
+        lane = rows_of((128, 128), 1)
+        out[c] = total[:128] + jnp.where(lane < 64, -turned, turned)
+        return carry
+
+    lax.fori_loop(0, 4, row, 0)
+
+
+def halo(currents):
+    up = [(i, i + 1) for i in range(lax.axis_size("clus") - 1)]
     down = [(b, a) for a, b in up]
-    low = lax.ppermute(currents[group - margin :], "clus", up)
-    high = lax.ppermute(currents[:margin], "clus", down)
-    window = jnp.concatenate([low, currents, high], axis=0)
-    local = near_cols - (lax.axis_index("clus") * group - margin)
-    neighbours = window[local]
-    near_real = jnp.einsum(
-        "cjab,cjbr->car", near_blocks[:, :, 0], neighbours, preferred_element_type=F32
-    )
-    near_imag = jnp.einsum(
-        "cjab,cjbr->car", near_blocks[:, :, 1], neighbours, preferred_element_type=F32
-    )
-    return combine_parts(near_real, near_imag, 1.0)
+    return lax.ppermute(currents[24:32], "clus", up), lax.ppermute(currents[0:8], "clus", down)
+
+
+def near_field(currents, low, high, near_blocks, near_cols):
+    hbm = pl.BlockSpec(memory_space=pltpu.HBM)
+    return pl.pallas_call(
+        near_kernel,
+        name="near",
+        out_shape=jax.ShapeDtypeStruct((4, 128, 128), F32),
+        in_specs=[SM, hbm, hbm, hbm, VM],
+        out_specs=VM,
+        scratch_shapes=[pltpu.VMEM((48, 128, 128), BF), pltpu.SemaphoreType.DMA((3,))],
+        cost_estimate=pl.CostEstimate(flops=168000000, bytes_accessed=4600000, transcendentals=0),
+        compiler_params=params(),
+    )(near_cols, low, currents, high, near_blocks)
 
 
 def body(
@@ -275,13 +304,16 @@
         name="radiate",
         out_shape=jax.ShapeDtypeStruct((8, 200, 256), BF),
         in_specs=[pl.BlockSpec(memory_space=pltpu.HBM)] * 4,
-        out_specs=VM,
+        out_specs=pl.BlockSpec(memory_space=pltpu.HBM),
         scratch_shapes=[
             pltpu.VMEM((4, 128, 128), BF),
             pltpu.VMEM((4, 2, 256, 128), BF),
             pltpu.VMEM((128, 256), BF),
             pltpu.VMEM((2, 256), BF),
+            pltpu.VMEM((8, 64, 256), BF),
+            pltpu.VMEM((8, 256), BF),
             pltpu.SemaphoreType.DMA((7,)),
+            pltpu.SemaphoreType.DMA((17,)),
         ],
         compiler_params=params(60 * 1024 * 1024),
     )(currents, radiate, interp, transl)
@@ -310,6 +342,8 @@
         compiler_params=params(),
     )(first, rows, got, other, lists, cosine, sine)
     moved = exchange(sent.reshape(64, 8, 384), "clus")
+    low, high = halo(currents)
+    moved, low, high = lax.optimization_barrier((moved, low, high))
 
     sent = pl.pallas_call(
         translate_kernel,
@@ -320,13 +354,15 @@
         scratch_shapes=[
             pltpu.VMEM((256, 512), BF),
             pltpu.VMEM((256, 128), jnp.int32),
-            pltpu.VMEM((64, 512), BF),
+            pltpu.VMEM((128, 512), BF),
             pltpu.VMEM((256, 256), F32),
             pltpu.VMEM((256, 256), F32),
         ],
         compiler_params=params(),
     )(moved.reshape(32, 2, 8, 384))
     moved = exchange(sent.reshape(64, 8, 256), "clus")
+    near = near_field(currents, low, high, near_blocks, near_cols)
+    moved, near = lax.optimization_barrier((moved, near))
 
     sent = pl.pallas_call(
         descend_kernel,
@@ -342,7 +378,6 @@
     )(child_slot, moved.reshape(4, 8, 2, 8, 256), half, other, cosine, sine)
     got = exchange(sent, "samp")
 
-    near = near_field(currents, near_blocks, near_cols)
     return pl.pallas_call(
         finish_kernel,
         name="finish",

time: 111 us -> 112 us (level)
  blocking collectives: 0 us -> 14.6 us
  waiting for transfers between devices: 44.9 us -> 36.4 us
  matrix products: 4.41 us -> 0 us
  other arithmetic: 1.79 us -> 0.09 us
  Pallas kernels: 13.3 us -> 14.7 us
    all_to_all x4 -> x3, waiting for transfers between devices: 44.9 us -> 28.2 us  [body(): lax.all_to_all(x, axis, split_axis=0, concat_axis=0, tiled=True)]
    all_to_all x0 -> x1, blocking collectives: none -> 14.6 us  [body(): lax.all_to_all(x, axis, split_axis=0, concat_axis=0, tiled=True)]
    ppermute x2, waiting for transfers between devices: 0.01 us -> 8.14 us  [the longest x1 5.91 us: halo(): lax.ppermute(currents[24:32], 'clus', up)]
    dot_general x2 -> x0, matrix products: 4.41 us -> none  [the longest x1 2.21 us: near_field(): jnp.einsum('cjab,cjbr->car', near_blocks[:, :, 1], neighbours, preferred_...]
    unnamed x16 -> x26, local copies, waits for them, and re-layouts: 0.05 us -> 4.38 us
    gather x1 -> x0, local copies, waits for them, and re-layouts: 3.28 us -> none  [near_field(): neighbours = window[local]]
    pallas_call x0 -> x1, Pallas kernels: none -> 2.3 us  [near_field(): pl.pallas_call(near_kernel, name='near', out_shape=jax.ShapeDtypeStruct((...]
    concatenate x2 -> x0, other arithmetic: 1.49 us -> none  [the longest x1 1.35 us: near_field(): window = jnp.concatenate([low, currents, high], axis=0)]
  transfers between devices with their start and end apart: 7 -> 6, of which waited for: 4 -> 5; matrix products, arithmetic and copies ran while one was open for 10% -> 0% of each run, Pallas kernels for 5% -> 3%
where the time goes in v4:
time: 112 us; the launch traced here: 111 us
  starting transfers between devices  40.3 us (36%)
  waiting for transfers between devices  36.4 us (32%)
  Pallas kernels  14.7 us (13%)
  blocking collectives  14.6 us (13%)
  local copies, waits for them, and re-layouts  4.69 us (4%)
    all_to_all x3, starting transfers between devices, body(): lax.all_to_all(x, axis, split_axis=0, concat_axis=0, tiled=True)  30 us
    all_to_all x3, waiting for transfers between devices, body(): lax.all_to_all(x, axis, split_axis=0, concat_axis=0, tiled=True)  28.2 us
    all_to_all x1, blocking collectives, body(): lax.all_to_all(x, axis, split_axis=0, concat_axis=0, tiled=True)  14.6 us
    ppermute x1, waiting for transfers between devices, halo(): lax.ppermute(currents[24:32], 'clus', up)  5.91 us
    ppermute x1, starting transfers between devices, body(): other = lax.ppermute(half, 'clus', partner)  4.86 us
    unnamed x26, local copies, waits for them, and re-layouts  4.38 us
    pallas_call x1, Pallas kernels, body(): pl.pallas_call(translate_kernel, name='translate', out_shape=jax.ShapeDty...  3.57 us
    ppermute x1, starting transfers between devices, halo(): lax.ppermute(currents[24:32], 'clus', up)  3.54 us
  transfers between devices with their start and end apart: 6, of which 5 were waited for; matrix products, arithmetic and copies ran while one was open for 0% of the time, Pallas kernels for 3%

profile of v4, /device:TPU:1, one launch (start us, length us, event | category | flops | bytes accessed | tf_op | source)
XLA Modules:
  0.0 111.1 jit_solution(16448749176768339305)
XLA Ops:
  0.0 0.0 copy-start.12
  0.0 0.0 copy-start.11
  0.0 0.0 copy-start.10
  0.0 0.0 copy-start.9
  0.0 0.0 copy-start.7
  0.0 3.0 %radiate.1 = bf16[8,200,256]{2,1,0:T(8,128)(2,1)} custom-call(bf16[32,128,128]{2,1,0:T(8,128)(2,1)} %cur.3, bf16[4,2,256,128]{3,2,1,0:T(8,128)(2,1)} %rad.1, bf16[256,256]{1,0:T(8,128)(2,1)} %itp.1, bf16[64,2,256]{2,1,0:T(2,128)(2,1)} %tra.1), custom_call_target="tpu_custom_call" | custom-call | tf_op jit(solution)/shard_map/radiate/pallas_call | solution.py:302
  3.1 7.7 %all-to-all-start = ((bf16[8,200,256]{2,1,0:T(8,128)(2,1)}), bf16[8,200,256]{2,1,0:T(8,128)(2,1)S(1)}, u32[]{:S(2)}, u32[]{:S(2)}) async-start(bf16[8,200,256]{2,1,0:T(8,128)(2,1)} %radiate.1), calls=%async_computation | async-start | bytes 1638400 | tf_op jit(solution)/shard_map/all_to_all | solution.py:296
  10.7 0.0 copy-done.12
  10.7 0.0 copy-done.11
  10.8 0.0 copy-done.10
  10.8 0.0 copy-start
  10.8 21.8 %all-to-all-done.got = bf16[8,200,256]{2,1,0:T(8,128)(2,1)S(1)} async-done(((bf16[8,200,256]{2,1,0:T(8,128)(2,1)}), bf16[8,200,256]{2,1,0:T(8,128)(2,1)S(1)}, u32[]{:S(2)}, u32[]{:S(2)}) %all-to-all-start) | async-done | bytes 819232 | tf_op jit(solution)/shard_map/all_to_all | solution.py:296
  32.6 4.9 %collective-permute-start = (bf16[8,128,256]{2,1,0:T(8,128)(2,1)S(1)}, bf16[8,128,256]{2,1,0:T(8,128)(2,1)S(1)}, u32[]{:S(2)}, u32[]{:S(2)}) collective-permute-start(bf16[8,128,256]{2,1,0:T(8,128)(2,1)S(1)} %slice.12.half), channel_id=1, source_target_pairs={{0,8},{8,0},{16,24},{24,16},{32,40},{40,32},{48,56},{56,48},{64,72... | collective-permute-start | bytes 1572872 | tf_op jit(solution)/shard_map/ppermute | solution.py:322
  37.5 0.1 pad_add_fusion.lists
  37.6 0.0 copy-done.9
  37.6 0.2 fusion.1
  37.8 0.0 copy-done.7
  37.8 1.4 %lift_own.1 = (bf16[4,8,2,8,128]{4,3,2,1,0:T(8,128)(2,1)S(1)}, bf16[512,256]{1,0:T(8,128)(2,1)S(1)}) custom-call(s32[32]{0:T(128)S(1)} %copy-done.7, bf16[8,200,256]{2,1,0:T(8,128)(2,1)S(1)} %all-to-all-done.got, f32[8,2048]{1,0:T(8,128)S(1)} %get-tuple-element.22.cosine, f32[8,2048]{1,0:T(8,128)S(1)} %get-tuple-element.21.sine), custom_call_target="tpu_custom_call" | custom-call | tf_op jit(solution)/shard_map/lift_own/pallas_call | solution.py:324
  39.2 0.0 collective-permute-done.other
  39.2 0.0 copy-start.8
  39.2 1.6 %lift_other.1 = bf16[4,8,2,8,384]{4,3,2,1,0:T(8,128)(2,1)} custom-call(bf16[4,8,2,8,128]{4,3,2,1,0:T(8,128)(2,1)S(1)} %get-tuple-element.12.first, bf16[512,256]{1,0:T(8,128)(2,1)S(1)} %get-tuple-element.13.rows, bf16[8,200,256]{2,1,0:T(8,128)(2,1)S(1)} %all-to-all-done.got, bf16[8,128,256]{2,1,0:T(8,128)(2,1)S(1)} %collective-permute-done.other, ...), custom_call_target="tpu_custom_call" | custom-call | tf_op jit(solution)/shard_map/lift_other/pallas_call | solution.py:336
  40.8 13.4 %all-to-all-start.1 = ((bf16[64,8,384]{2,1,0:T(8,128)(2,1)}), bf16[64,8,384]{2,1,0:T(8,128)(2,1)S(1)}, u32[]{:S(2)}, u32[]{:S(2)}) async-start(bf16[64,8,384]{2,1,0:T(8,128)(2,1)} %bitcast), calls=%async_computation.1 | async-start | bytes 786432 | tf_op jit(solution)/shard_map/all_to_all | solution.py:296
  54.3 0.0 copy-done
  54.3 3.5 %collective-permute-start.1 = (bf16[8,128,128]{2,1,0:T(8,128)(2,1)S(1)}, bf16[8,128,128]{2,1,0:T(8,128)(2,1)S(1)}, u32[]{:S(2)}, u32[]{:S(2)}) collective-permute-start(bf16[8,128,128]{2,1,0:T(8,128)(2,1)S(1)} %get-tuple-element.20), channel_id=1, source_target_pairs={{0,8},{8,16},{16,24},{24,32},{32,40},{40,48},{48,56},{56,64},{64,7... | collective-permute-start | bytes 786440 | tf_op jit(solution)/shard_map/ppermute | solution.py:265
  57.9 1.9 %collective-permute-start.2 = (bf16[8,128,128]{2,1,0:T(8,128)(2,1)S(1)}, bf16[8,128,128]{2,1,0:T(8,128)(2,1)S(1)}, u32[]{:S(2)}, u32[]{:S(2)}) collective-permute-start(bf16[8,128,128]{2,1,0:T(8,128)(2,1)S(1)} %get-tuple-element.19), channel_id=1, source_target_pairs={{8,0},{16,8},{24,16},{32,24},{40,32},{48,40},{56,48},{64,56},{72,6... | collective-permute-start | bytes 786440 | tf_op jit(solution)/shard_map/ppermute | solution.py:265
  59.8 5.9 %collective-permute-done.1.low = bf16[8,128,128]{2,1,0:T(8,128)(2,1)S(1)} collective-permute-done((bf16[8,128,128]{2,1,0:T(8,128)(2,1)S(1)}, bf16[8,128,128]{2,1,0:T(8,128)(2,1)S(1)}, u32[]{:S(2)}, u32[]{:S(2)}) %collective-permute-start.1) | collective-permute-done | bytes 262176 | tf_op jit(solution)/shard_map/ppermute | solution.py:265
  65.7 0.0 copy-start.3
  65.7 2.2 %collective-permute-done.2.high = bf16[8,128,128]{2,1,0:T(8,128)(2,1)S(1)} collective-permute-done((bf16[8,128,128]{2,1,0:T(8,128)(2,1)S(1)}, bf16[8,128,128]{2,1,0:T(8,128)(2,1)S(1)}, u32[]{:S(2)}, u32[]{:S(2)}) %collective-permute-start.2) | collective-permute-done | bytes 262176 | tf_op jit(solution)/shard_map/ppermute | solution.py:265
  68.0 0.0 copy-start.5
  68.0 0.7 copy-done.5
  68.7 0.4 all-to-all-done.1
  69.1 3.6 %translate.1 = bf16[32,2,8,256]{3,2,1,0:T(8,128)(2,1)} custom-call(bf16[32,2,8,384]{3,2,1,0:T(8,128)(2,1)S(1)} %bitcast.4), custom_call_target="tpu_custom_call" | custom-call | tf_op jit(solution)/shard_map/translate/pallas_call | solution.py:348
  72.7 0.0 copy-done.3
  72.7 8.9 %all-to-all-start.2 = ((bf16[64,8,256]{2,1,0:T(8,128)(2,1)}), bf16[64,8,256]{2,1,0:T(8,128)(2,1)S(1)}, u32[]{:S(2)}, u32[]{:S(2)}) async-start(bf16[64,8,256]{2,1,0:T(8,128)(2,1)} %bitcast.2), calls=%async_computation.2 | async-start | bytes 524288 | tf_op jit(solution)/shard_map/all_to_all | solution.py:296
  81.6 0.0 copy-done.8
  81.6 0.0 copy-start.1
  81.6 1.7 %copy-done.1 = bf16[4,10,2,128,128]{4,3,2,1,0:T(8,128)(2,1)S(1)} copy-done((bf16[4,10,2,128,128]{4,3,2,1,0:T(8,128)(2,1)S(1)}, bf16[4,10,2,128,128]{4,3,2,1,0:T(8,128)(2,1)}, u32[]{:S(2)}) %copy-start.1) | copy-done | bytes 2621464
  83.3 0.0 copy-start.4
  83.3 0.9 copy-done.4
  84.3 0.0 copy-start.6
  84.3 0.9 copy-done.6
  85.2 0.0 copy-start.2
  85.2 2.3 %near.1 = f32[4,128,128]{2,1,0:T(8,128)S(1)} custom-call(s32[4,10]{1,0:T(4,128)S(1)} %copy-done.8, bf16[8,128,128]{2,1,0:T(8,128)(2,1)S(1)} %copy-done.4, bf16[32,128,128]{2,1,0:T(8,128)(2,1)S(1)} %copy-done, bf16[8,128,128]{2,1,0:T(8,128)(2,1)S(1)} %copy-done.6, bf16[4,10,2,128,128]{4,3,2,1,0:T(8,128)(2,1)S(1)} %copy-done.1), custom_call_target="tpu_custom_call" | custom-call | flops 168000000 | bytes 4600000 | tf_op jit(solution)/shard_map/near/pallas_call | solution.py:270
  87.5 6.0 %all-to-all-done.2 = bf16[64,8,256]{2,1,0:T(8,128)(2,1)S(1)} async-done(((bf16[64,8,256]{2,1,0:T(8,128)(2,1)}), bf16[64,8,256]{2,1,0:T(8,128)(2,1)S(1)}, u32[]{:S(2)}, u32[]{:S(2)}) %all-to-all-start.2) | async-done | bytes 262176 | tf_op jit(solution)/shard_map/all_to_all | solution.py:296
  93.5 1.7 %descend.1 = bf16[8,64,256]{2,1,0:T(8,128)(2,1)S(1)} custom-call(s32[32]{0:T(128)S(1)} %copy-done.7, bf16[4,8,2,8,256]{4,3,2,1,0:T(8,128)(2,1)S(1)} %bitcast.5, bf16[8,128,256]{2,1,0:T(8,128)(2,1)S(1)} %slice.12.half, bf16[8,128,256]{2,1,0:T(8,128)(2,1)S(1)} %collective-permute-done.other, f32[8,2048]{1,0:T(8,128)S(1)} %get-tuple-element.22.cosine, ...), custom_call_target="tpu_custom_call" | custom-call | tf_op jit(solution)/shard_map/descend/pallas_call | solution.py:367
  95.2 14.6 %all_to_all.20.got = bf16[8,64,256]{2,1,0:T(8,128)(2,1)S(1)} all-to-all(bf16[8,64,256]{2,1,0:T(8,128)(2,1)S(1)} %descend.1), channel_id=1, replica_groups=mesh['clus'=64,'samp'=8] {'samp'}, dimensions={0} | all-to-all | bytes 524288 | tf_op jit(solution)/shard_map/all_to_all | solution.py:296
  109.9 0.0 copy-done.2
  109.9 1.2 %finish.1 = bf16[4,128,128]{2,1,0:T(8,128)(2,1)} custom-call(bf16[8,64,256]{2,1,0:T(8,128)(2,1)S(1)} %all_to_all.20.got, bf16[4,2,256,128]{3,2,1,0:T(8,128)(2,1)S(1)} %copy-done.2, f32[4,128,128]{2,1,0:T(8,128)S(1)} %near.1), custom_call_target="tpu_custom_call" | custom-call | tf_op jit(solution)/shard_map/finish/pallas_call | solution.py:381
  (4 shorter events, 0.1 us)
Async XLA Ops:
  0.0 10.7 %copy-start.12 = (s32[4,16]{1,0:T(4,128)S(1)}, s32[4,16]{1,0:T(4,128)}, u32[]{:S(2)}) copy-start(s32[4,16]{1,0:T(4,128)} %param.20) | copy-start | bytes 772
  0.0 10.7 %copy-start.11 = (s32[4,16]{1,0:T(4,128)S(1)}, s32[4,16]{1,0:T(4,128)}, u32[]{:S(2)}) copy-start(s32[4,16]{1,0:T(4,128)} %param.18) | copy-start | bytes 772
  0.0 10.7 %copy-start.10 = (s32[4,16]{1,0:T(4,128)S(1)}, s32[4,16]{1,0:T(4,128)}, u32[]{:S(2)}) copy-start(s32[4,16]{1,0:T(4,128)} %param.19) | copy-start | bytes 772
  0.0 37.6 %copy-start.9 = (f32[8,2048]{1,0:T(8,128)S(1)}, f32[8,2048]{1,0:T(8,128)}, u32[]{:S(2)}) copy-start(f32[8,2048]{1,0:T(8,128)} %param.17) | copy-start | bytes 196612
  0.0 37.8 %copy-start.7 = (s32[32]{0:T(128)S(1)}, s32[32]{0:T(128)}, u32[]{:S(2)}) copy-start(s32[32]{0:T(128)} %slots.3) | copy-start | bytes 388
  3.1 29.5 %all-to-all-start = ((bf16[8,200,256]{2,1,0:T(8,128)(2,1)}), bf16[8,200,256]{2,1,0:T(8,128)(2,1)S(1)}, u32[]{:S(2)}, u32[]{:S(2)}) async-start(bf16[8,200,256]{2,1,0:T(8,128)(2,1)} %radiate.1), calls=%async_computation | async-start | bytes 1638400 | tf_op jit(solution)/shard_map/all_to_all | solution.py:296
  10.8 43.5 %copy-start = (bf16[32,128,128]{2,1,0:T(8,128)(2,1)S(1)}, bf16[32,128,128]{2,1,0:T(8,128)(2,1)}, u32[]{:S(2)}) copy-start(bf16[32,128,128]{2,1,0:T(8,128)(2,1)} %cur.3) | copy-start | bytes 3145732
  32.6 6.6 %collective-permute-start = (bf16[8,128,256]{2,1,0:T(8,128)(2,1)S(1)}, bf16[8,128,256]{2,1,0:T(8,128)(2,1)S(1)}, u32[]{:S(2)}, u32[]{:S(2)}) collective-permute-start(bf16[8,128,256]{2,1,0:T(8,128)(2,1)S(1)} %slice.12.half), channel_id=1, source_target_pairs={{0,8},{8,0},{16,24},{24,16},{32,40},{40,32},{48,56},{56,48},{64,72... | collective-permute-start | bytes 1572872 | tf_op jit(solution)/shard_map/ppermute | solution.py:322
  39.2 42.4 %copy-start.8 = (s32[4,10]{1,0:T(4,128)S(1)}, s32[4,10]{1,0:T(4,128)}, u32[]{:S(2)}) copy-start(s32[4,10]{1,0:T(4,128)} %cols.1) | copy-start | bytes 484
  40.8 28.3 %all-to-all-start.1 = ((bf16[64,8,384]{2,1,0:T(8,128)(2,1)}), bf16[64,8,384]{2,1,0:T(8,128)(2,1)S(1)}, u32[]{:S(2)}, u32[]{:S(2)}) async-start(bf16[64,8,384]{2,1,0:T(8,128)(2,1)} %bitcast), calls=%async_computation.1 | async-start | bytes 786432 | tf_op jit(solution)/shard_map/all_to_all | solution.py:296
  54.3 11.4 %collective-permute-start.1 = (bf16[8,128,128]{2,1,0:T(8,128)(2,1)S(1)}, bf16[8,128,128]{2,1,0:T(8,128)(2,1)S(1)}, u32[]{:S(2)}, u32[]{:S(2)}) collective-permute-start(bf16[8,128,128]{2,1,0:T(8,128)(2,1)S(1)} %get-tuple-element.20), channel_id=1, source_target_pairs={{0,8},{8,16},{16,24},{24,32},{32,40},{40,48},{48,56},{56,64},{64,7... | collective-permute-start | bytes 786440 | tf_op jit(solution)/shard_map/ppermute | solution.py:265
  57.9 10.1 %collective-permute-start.2 = (bf16[8,128,128]{2,1,0:T(8,128)(2,1)S(1)}, bf16[8,128,128]{2,1,0:T(8,128)(2,1)S(1)}, u32[]{:S(2)}, u32[]{:S(2)}) collective-permute-start(bf16[8,128,128]{2,1,0:T(8,128)(2,1)S(1)} %get-tuple-element.19), channel_id=1, source_target_pairs={{8,0},{16,8},{24,16},{32,24},{40,32},{48,40},{56,48},{64,56},{72,6... | collective-permute-start | bytes 786440 | tf_op jit(solution)/shard_map/ppermute | solution.py:265
  65.7 6.9 %copy-start.3 = (bf16[8,128,128]{2,1,0:T(8,128)(2,1)}, bf16[8,128,128]{2,1,0:T(8,128)(2,1)S(1)}, u32[]{:S(2)}) copy-start(bf16[8,128,128]{2,1,0:T(8,128)(2,1)S(1)} %collective-permute-done.1.low) | copy-start | bytes 786436
  68.0 0.7 copy-start.5
  72.7 20.9 %all-to-all-start.2 = ((bf16[64,8,256]{2,1,0:T(8,128)(2,1)}), bf16[64,8,256]{2,1,0:T(8,128)(2,1)S(1)}, u32[]{:S(2)}, u32[]{:S(2)}) async-start(bf16[64,8,256]{2,1,0:T(8,128)(2,1)} %bitcast.2), calls=%async_computation.2 | async-start | bytes 524288 | tf_op jit(solution)/shard_map/all_to_all | solution.py:296
  81.6 1.7 %copy-start.1 = (bf16[4,10,2,128,128]{4,3,2,1,0:T(8,128)(2,1)S(1)}, bf16[4,10,2,128,128]{4,3,2,1,0:T(8,128)(2,1)}, u32[]{:S(2)}) copy-start(bf16[4,10,2,128,128]{4,3,2,1,0:T(8,128)(2,1)} %blocks.1) | copy-start | bytes 7864324
  83.3 0.9 copy-start.4
  84.3 0.9 copy-start.6
  85.2 24.7 %copy-start.2 = (bf16[4,2,256,128]{3,2,1,0:T(8,128)(2,1)S(1)}, bf16[4,2,256,128]{3,2,1,0:T(8,128)(2,1)}, u32[]{:S(2)}) copy-start(bf16[4,2,256,128]{3,2,1,0:T(8,128)(2,1)} %rad.1) | copy-start | bytes 1572868

commit v5 on v4

--- a/solution.py
+++ b/solution.py
@@ -317,7 +317,11 @@
         ],
         compiler_params=params(60 * 1024 * 1024),
     )(currents, radiate, interp, transl)
+    sent, mine = lax.optimization_barrier((sent, currents))
     got = exchange(sent, "samp")
+    low, high = halo(mine)
+    near = near_field(mine, low, high, near_blocks, near_cols)
+    got, near = lax.optimization_barrier((got, near))
     half = got[:, 64:192]
     other = lax.ppermute(half, "clus", partner)
 
@@ -342,8 +346,6 @@
         compiler_params=params(),
     )(first, rows, got, other, lists, cosine, sine)
     moved = exchange(sent.reshape(64, 8, 384), "clus")
-    low, high = halo(currents)
-    moved, low, high = lax.optimization_barrier((moved, low, high))
 
     sent = pl.pallas_call(
         translate_kernel,
@@ -361,8 +363,6 @@
         compiler_params=params(),
     )(moved.reshape(32, 2, 8, 384))
     moved = exchange(sent.reshape(64, 8, 256), "clus")
-    near = near_field(currents, low, high, near_blocks, near_cols)
-    moved, near = lax.optimization_barrier((moved, near))
 
     sent = pl.pallas_call(
         descend_kernel,

time: 112 us -> 107 us (0.955)
  blocking collectives: 14.6 us -> 60.6 us
  waiting for transfers between devices: 36.4 us -> 10.9 us
  starting transfers between devices: 40.3 us -> 19.3 us
  local copies, waits for them, and re-layouts: 4.69 us -> 2.09 us
  Pallas kernels: 14.7 us -> 13.2 us
    all_to_all x1 -> x3, blocking collectives: 14.6 us -> 60.6 us  [body(): lax.all_to_all(x, axis, split_axis=0, concat_axis=0, tiled=True)]
    all_to_all x3 -> x1, starting transfers between devices: 30 us -> 7.65 us  [body(): lax.all_to_all(x, axis, split_axis=0, concat_axis=0, tiled=True)]
    all_to_all x3 -> x1, waiting for transfers between devices: 28.2 us -> 7.69 us  [body(): lax.all_to_all(x, axis, split_axis=0, concat_axis=0, tiled=True)]
    ppermute x1, waiting for transfers between devices: 5.91 us -> 0.89 us  [halo(): lax.ppermute(currents[24:32], 'clus', up)]
    ppermute x1, starting transfers between devices: 1.92 us -> 4.65 us  [halo(): lax.ppermute(currents[0:8], 'clus', down)]
    unnamed x26 -> x18, local copies, waits for them, and re-layouts: 4.38 us -> 1.78 us
    ppermute x1, starting transfers between devices: 3.54 us -> 2.11 us  [halo(): lax.ppermute(currents[24:32], 'clus', up)]
  transfers between devices with their start and end apart: 6 -> 4, of which waited for: 5 -> 3; matrix products, arithmetic and copies ran while one was open for 0% -> 0% of each run, Pallas kernels for 3% -> 3%
where the time goes in v5:
time: 107 us; the launch traced here: 106 us
  blocking collectives  60.6 us (57%)
  starting transfers between devices  19.3 us (18%)
  Pallas kernels  13.2 us (12%)
  waiting for transfers between devices  10.9 us (10%)
  local copies, waits for them, and re-layouts  2.09 us (2%)
    all_to_all x3, blocking collectives, body(): lax.all_to_all(x, axis, split_axis=0, concat_axis=0, tiled=True)  60.6 us
    all_to_all x1, waiting for transfers between devices, body(): lax.all_to_all(x, axis, split_axis=0, concat_axis=0, tiled=True)  7.69 us
    all_to_all x1, starting transfers between devices, body(): lax.all_to_all(x, axis, split_axis=0, concat_axis=0, tiled=True)  7.65 us
    ppermute x1, starting transfers between devices, body(): other = lax.ppermute(half, 'clus', partner)  4.85 us
    ppermute x1, starting transfers between devices, halo(): lax.ppermute(currents[0:8], 'clus', down)  4.65 us
    pallas_call x1, Pallas kernels, body(): pl.pallas_call(radiate_kernel, name='radiate', out_shape=jax.ShapeDtypeSt...  3.05 us
    pallas_call x1, Pallas kernels, body(): pl.pallas_call(translate_kernel, name='translate', out_shape=jax.ShapeDty...  2.83 us
    ppermute x1, waiting for transfers between devices, halo(): lax.ppermute(currents[0:8], 'clus', down)  2.34 us
  transfers between devices with their start and end apart: 4, of which 3 were waited for; matrix products, arithmetic and copies ran while one was open for 0% of the time, Pallas kernels for 3%

profile of v5, /device:TPU:1, one launch (start us, length us, event | category | flops | bytes accessed | tf_op | source)
XLA Modules:
  0.0 106.4 jit_solution(10536891610501955948)
XLA Ops:
  0.0 0.0 copy-start
  0.0 0.0 copy-start.8
  0.0 0.0 copy-start.6
  0.0 0.0 copy-start.7
  0.0 0.0 copy-start.4
  0.0 3.1 %radiate.1 = bf16[8,200,256]{2,1,0:T(8,128)(2,1)} custom-call(bf16[32,128,128]{2,1,0:T(8,128)(2,1)} %cur.2, bf16[4,2,256,128]{3,2,1,0:T(8,128)(2,1)} %rad.1, bf16[256,256]{1,0:T(8,128)(2,1)} %itp.1, bf16[64,2,256]{2,1,0:T(2,128)(2,1)} %tra.1), custom_call_target="tpu_custom_call" | custom-call | tf_op jit(solution)/shard_map/radiate/pallas_call | solution.py:302
  3.1 7.7 %all-to-all-start = ((bf16[8,200,256]{2,1,0:T(8,128)(2,1)}), bf16[8,200,256]{2,1,0:T(8,128)(2,1)S(1)}, u32[]{:S(2)}, u32[]{:S(2)}) async-start(bf16[8,200,256]{2,1,0:T(8,128)(2,1)} %radiate.1), calls=%async_computation | async-start | bytes 1638400 | tf_op jit(solution)/shard_map/all_to_all | solution.py:296
  10.7 0.0 copy-done
  10.8 4.7 %collective-permute-start.1 = (bf16[8,128,128]{2,1,0:T(8,128)(2,1)S(1)}, bf16[8,128,128]{2,1,0:T(8,128)(2,1)S(1)}, u32[]{:S(2)}, u32[]{:S(2)}) collective-permute-start(bf16[8,128,128]{2,1,0:T(8,128)(2,1)S(1)} %get-tuple-element.17), channel_id=1, source_target_pairs={{8,0},{16,8},{24,16},{32,24},{40,32},{48,40},{56,48},{64,56},{72,6... | collective-permute-start | bytes 786440 | tf_op jit(solution)/shard_map/ppermute | solution.py:265
  15.5 2.1 %collective-permute-start = (bf16[8,128,128]{2,1,0:T(8,128)(2,1)S(1)}, bf16[8,128,128]{2,1,0:T(8,128)(2,1)S(1)}, u32[]{:S(2)}, u32[]{:S(2)}) collective-permute-start(bf16[8,128,128]{2,1,0:T(8,128)(2,1)S(1)} %get-tuple-element.18), channel_id=1, source_target_pairs={{0,8},{8,16},{16,24},{24,32},{32,40},{40,48},{48,56},{56,64},{64,7... | collective-permute-start | bytes 786440 | tf_op jit(solution)/shard_map/ppermute | solution.py:265
  17.6 0.0 copy-done.8
  17.6 0.0 copy-done.6
  17.6 0.0 copy-done.7
  17.6 0.0 copy-start.3
  17.6 2.3 %collective-permute-done.1.high = bf16[8,128,128]{2,1,0:T(8,128)(2,1)S(1)} collective-permute-done((bf16[8,128,128]{2,1,0:T(8,128)(2,1)S(1)}, bf16[8,128,128]{2,1,0:T(8,128)(2,1)S(1)}, u32[]{:S(2)}, u32[]{:S(2)}) %collective-permute-start.1) | collective-permute-done | bytes 262176 | tf_op jit(solution)/shard_map/ppermute | solution.py:265
  20.0 0.9 collective-permute-done.low
  20.9 0.0 copy-done.4
  20.9 0.0 copy-start.1
  20.9 1.7 %copy-done.1 = bf16[4,10,2,128,128]{4,3,2,1,0:T(8,128)(2,1)S(1)} copy-done((bf16[4,10,2,128,128]{4,3,2,1,0:T(8,128)(2,1)S(1)}, bf16[4,10,2,128,128]{4,3,2,1,0:T(8,128)(2,1)}, u32[]{:S(2)}) %copy-start.1) | copy-done | bytes 2621464
  22.6 0.0 copy-start.5
  22.6 2.3 %near.1 = f32[4,128,128]{2,1,0:T(8,128)S(1)} custom-call(s32[4,10]{1,0:T(4,128)S(1)} %copy-done.4, bf16[8,128,128]{2,1,0:T(8,128)(2,1)S(1)} %collective-permute-done.low, bf16[32,128,128]{2,1,0:T(8,128)(2,1)S(1)} %copy-done, bf16[8,128,128]{2,1,0:T(8,128)(2,1)S(1)} %collective-permute-done.1.high, bf16[4,10,2,128,128]{4,3,2,1,0:T(8,128)(2,1)S(1)} %copy-done.1), custom_call_target="tpu_custom_call" | custom-call | flops 168000000 | bytes 4600000 | tf_op jit(solution)/shard_map/near/pallas_call | solution.py:270
  24.9 7.7 %all-to-all-done.got = bf16[8,200,256]{2,1,0:T(8,128)(2,1)S(1)} async-done(((bf16[8,200,256]{2,1,0:T(8,128)(2,1)}), bf16[8,200,256]{2,1,0:T(8,128)(2,1)S(1)}, u32[]{:S(2)}, u32[]{:S(2)}) %all-to-all-start) | async-done | bytes 819232 | tf_op jit(solution)/shard_map/all_to_all | solution.py:296
  32.6 4.9 %collective-permute-start.2 = (bf16[8,128,256]{2,1,0:T(8,128)(2,1)S(1)}, bf16[8,128,256]{2,1,0:T(8,128)(2,1)S(1)}, u32[]{:S(2)}, u32[]{:S(2)}) collective-permute-start(bf16[8,128,256]{2,1,0:T(8,128)(2,1)S(1)} %slice.11.half), channel_id=1, source_target_pairs={{0,8},{8,0},{16,24},{24,16},{32,40},{40,32},{48,56},{56,48},{64,72... | collective-permute-start | bytes 1572872 | tf_op jit(solution)/shard_map/ppermute | solution.py:326
  37.5 0.1 pad_add_fusion.lists
  37.6 0.0 copy-done.5
  37.6 0.2 fusion.1
  37.8 0.0 copy-done.3
  37.8 1.4 %lift_own.1 = (bf16[4,8,2,8,128]{4,3,2,1,0:T(8,128)(2,1)S(1)}, bf16[512,256]{1,0:T(8,128)(2,1)S(1)}) custom-call(s32[32]{0:T(128)S(1)} %copy-done.3, bf16[8,200,256]{2,1,0:T(8,128)(2,1)S(1)} %all-to-all-done.got, f32[8,2048]{1,0:T(8,128)S(1)} %get-tuple-element.20.cosine, f32[8,2048]{1,0:T(8,128)S(1)} %get-tuple-element.19.sine), custom_call_target="tpu_custom_call" | custom-call | tf_op jit(solution)/shard_map/lift_own/pallas_call | solution.py:328
  39.2 0.0 collective-permute-done.2.other
  39.2 0.8 lift_other.1
  40.1 0.0 copy-start.2
  40.1 27.9 %all_to_all.20 = bf16[64,8,384]{2,1,0:T(8,128)(2,1)S(1)} all-to-all(bf16[64,8,384]{2,1,0:T(8,128)(2,1)S(1)} %bitcast.5), channel_id=1, replica_groups=mesh['clus'=64,'samp'=8] {'clus'}, dimensions={0} | all-to-all | bytes 786432 | tf_op jit(solution)/shard_map/all_to_all | solution.py:296
  68.0 2.8 %translate.1 = bf16[32,2,8,256]{3,2,1,0:T(8,128)(2,1)S(1)} custom-call(bf16[32,2,8,384]{3,2,1,0:T(8,128)(2,1)S(1)} %bitcast.4), custom_call_target="tpu_custom_call" | custom-call | tf_op jit(solution)/shard_map/translate/pallas_call | solution.py:350
  70.9 18.0 %all_to_all.21 = bf16[64,8,256]{2,1,0:T(8,128)(2,1)S(1)} all-to-all(bf16[64,8,256]{2,1,0:T(8,128)(2,1)S(1)} %bitcast.7), channel_id=1, replica_groups=mesh['clus'=64,'samp'=8] {'clus'}, dimensions={0} | all-to-all | bytes 524288 | tf_op jit(solution)/shard_map/all_to_all | solution.py:296
  88.9 1.7 %descend.1 = bf16[8,64,256]{2,1,0:T(8,128)(2,1)S(1)} custom-call(s32[32]{0:T(128)S(1)} %copy-done.3, bf16[4,8,2,8,256]{4,3,2,1,0:T(8,128)(2,1)S(1)} %bitcast.6, bf16[8,128,256]{2,1,0:T(8,128)(2,1)S(1)} %slice.11.half, bf16[8,128,256]{2,1,0:T(8,128)(2,1)S(1)} %collective-permute-done.2.other, f32[8,2048]{1,0:T(8,128)S(1)} %get-tuple-element.20.cosine, ...), custom_call_target="tpu_custom_call" | custom-call | tf_op jit(solution)/shard_map/descend/pallas_call | solution.py:367
  90.6 14.6 %all_to_all.22.got = bf16[8,64,256]{2,1,0:T(8,128)(2,1)S(1)} all-to-all(bf16[8,64,256]{2,1,0:T(8,128)(2,1)S(1)} %descend.1), channel_id=1, replica_groups=mesh['clus'=64,'samp'=8] {'samp'}, dimensions={0} | all-to-all | bytes 524288 | tf_op jit(solution)/shard_map/all_to_all | solution.py:296
  105.2 0.0 copy-done.2
  105.2 1.1 %finish.1 = bf16[4,128,128]{2,1,0:T(8,128)(2,1)} custom-call(bf16[8,64,256]{2,1,0:T(8,128)(2,1)S(1)} %all_to_all.22.got, bf16[4,2,256,128]{3,2,1,0:T(8,128)(2,1)S(1)} %copy-done.2, f32[4,128,128]{2,1,0:T(8,128)S(1)} %near.1), custom_call_target="tpu_custom_call" | custom-call | tf_op jit(solution)/shard_map/finish/pallas_call | solution.py:381
  (4 shorter events, 0.1 us)
Async XLA Ops:
  0.0 10.7 %copy-start = (bf16[32,128,128]{2,1,0:T(8,128)(2,1)S(1)}, bf16[32,128,128]{2,1,0:T(8,128)(2,1)}, u32[]{:S(2)}) copy-start(bf16[32,128,128]{2,1,0:T(8,128)(2,1)} %cur.2) | copy-start | bytes 3145732
  0.0 17.6 %copy-start.8 = (s32[4,16]{1,0:T(4,128)S(1)}, s32[4,16]{1,0:T(4,128)}, u32[]{:S(2)}) copy-start(s32[4,16]{1,0:T(4,128)} %param.20) | copy-start | bytes 772
  0.0 17.6 %copy-start.6 = (s32[4,16]{1,0:T(4,128)S(1)}, s32[4,16]{1,0:T(4,128)}, u32[]{:S(2)}) copy-start(s32[4,16]{1,0:T(4,128)} %param.19) | copy-start | bytes 772
  0.0 17.6 %copy-start.7 = (s32[4,16]{1,0:T(4,128)S(1)}, s32[4,16]{1,0:T(4,128)}, u32[]{:S(2)}) copy-start(s32[4,16]{1,0:T(4,128)} %param.18) | copy-start | bytes 772
  0.0 20.9 %copy-start.4 = (s32[4,10]{1,0:T(4,128)S(1)}, s32[4,10]{1,0:T(4,128)}, u32[]{:S(2)}) copy-start(s32[4,10]{1,0:T(4,128)} %cols.1) | copy-start | bytes 484
  3.1 29.5 %all-to-all-start = ((bf16[8,200,256]{2,1,0:T(8,128)(2,1)}), bf16[8,200,256]{2,1,0:T(8,128)(2,1)S(1)}, u32[]{:S(2)}, u32[]{:S(2)}) async-start(bf16[8,200,256]{2,1,0:T(8,128)(2,1)} %radiate.1), calls=%async_computation | async-start | bytes 1638400 | tf_op jit(solution)/shard_map/all_to_all | solution.py:296
  10.8 9.2 %collective-permute-start.1 = (bf16[8,128,128]{2,1,0:T(8,128)(2,1)S(1)}, bf16[8,128,128]{2,1,0:T(8,128)(2,1)S(1)}, u32[]{:S(2)}, u32[]{:S(2)}) collective-permute-start(bf16[8,128,128]{2,1,0:T(8,128)(2,1)S(1)} %get-tuple-element.17), channel_id=1, source_target_pairs={{8,0},{16,8},{24,16},{32,24},{40,32},{48,40},{56,48},{64,56},{72,6... | collective-permute-start | bytes 786440 | tf_op jit(solution)/shard_map/ppermute | solution.py:265
  15.5 5.4 %collective-permute-start = (bf16[8,128,128]{2,1,0:T(8,128)(2,1)S(1)}, bf16[8,128,128]{2,1,0:T(8,128)(2,1)S(1)}, u32[]{:S(2)}, u32[]{:S(2)}) collective-permute-start(bf16[8,128,128]{2,1,0:T(8,128)(2,1)S(1)} %get-tuple-element.18), channel_id=1, source_target_pairs={{0,8},{8,16},{16,24},{24,32},{32,40},{40,48},{48,56},{56,64},{64,7... | collective-permute-start | bytes 786440 | tf_op jit(solution)/shard_map/ppermute | solution.py:265
  17.6 20.2 %copy-start.3 = (s32[32]{0:T(128)S(1)}, s32[32]{0:T(128)}, u32[]{:S(2)}) copy-start(s32[32]{0:T(128)} %slots.3) | copy-start | bytes 388
  20.9 1.7 %copy-start.1 = (bf16[4,10,2,128,128]{4,3,2,1,0:T(8,128)(2,1)S(1)}, bf16[4,10,2,128,128]{4,3,2,1,0:T(8,128)(2,1)}, u32[]{:S(2)}) copy-start(bf16[4,10,2,128,128]{4,3,2,1,0:T(8,128)(2,1)} %blocks.1) | copy-start | bytes 7864324
  22.6 15.0 %copy-start.5 = (f32[8,2048]{1,0:T(8,128)S(1)}, f32[8,2048]{1,0:T(8,128)}, u32[]{:S(2)}) copy-start(f32[8,2048]{1,0:T(8,128)} %param.17) | copy-start | bytes 196612
  32.6 6.6 %collective-permute-start.2 = (bf16[8,128,256]{2,1,0:T(8,128)(2,1)S(1)}, bf16[8,128,256]{2,1,0:T(8,128)(2,1)S(1)}, u32[]{:S(2)}, u32[]{:S(2)}) collective-permute-start(bf16[8,128,256]{2,1,0:T(8,128)(2,1)S(1)} %slice.11.half), channel_id=1, source_target_pairs={{0,8},{8,0},{16,24},{24,16},{32,40},{40,32},{48,56},{56,48},{64,72... | collective-permute-start | bytes 1572872 | tf_op jit(solution)/shard_map/ppermute | solution.py:326
  40.1 65.2 %copy-start.2 = (bf16[4,2,256,128]{3,2,1,0:T(8,128)(2,1)S(1)}, bf16[4,2,256,128]{3,2,1,0:T(8,128)(2,1)}, u32[]{:S(2)}) copy-start(bf16[4,2,256,128]{3,2,1,0:T(8,128)(2,1)} %rad.1) | copy-start | bytes 1572868

commit v6 on v5

--- a/solution.py
+++ b/solution.py
@@ -28,33 +28,25 @@
     return lax.broadcasted_iota(jnp.int32, shape, dim)
 
 
-def radiate_kernel(
-    cur, rad_all, itp, tra, out, own, rad, half, tran, data, extra, in_sems, out_sems
-):
+def radiate_kernel(cur, rad_all, itp, out, own, rad, half, data, in_sems, out_sems):
     clus = lax.axis_index("clus")
     mine = pl.ds(pl.multiple_of(lax.rem(clus, 2) * 128, 128), 128)
     pairs = [
         (itp.at[mine], half),
-        (tra.at[clus], tran),
         (cur.at[pl.ds(lax.axis_index("samp") * 4, 4)], own),
     ] + [(rad_all.at[c], rad.at[c]) for c in range(4)]
     copies = [pltpu.make_async_copy(a, b, in_sems.at[i]) for i, (a, b) in enumerate(pairs)]
     for copy in copies:
         copy.start()
     copies[0].wait()
-    copies[1].wait()
-    trow = tran[...].astype(F32)
-    row = rows_of((8, 256), 0)
-    extra[...] = jnp.where(row == 0, trow[0:1], jnp.where(row == 1, trow[1:2], 0.0)).astype(BF)
-    sends = []
-    for s in range(8):
-        sends.append(pltpu.make_async_copy(half, out.at[s, 64:192, :], out_sems.at[s]))
-        sends.append(pltpu.make_async_copy(extra, out.at[s, 192:200, :], out_sems.at[8 + s]))
+    sends = [
+        pltpu.make_async_copy(half, out.at[s, 64:192, :], out_sems.at[s]) for s in range(8)
+    ]
     for send in sends:
         send.start()
-    copies[2].wait()
+    copies[1].wait()
     for c in range(4):
-        copies[3 + c].wait()
+        copies[2 + c].wait()
         values = own[c].astype(F32).T.astype(BF)
         with_real = nt_dot(values, rad[c, 0])
         with_imag = nt_dot(values, rad[c, 1])
@@ -63,7 +55,7 @@
         for s in range(8):
             both = jnp.concatenate([real[8 * s : 8 * s + 8], imag[8 * s : 8 * s + 8]], axis=0)
             data[s, 16 * c : 16 * c + 16, :] = both.astype(BF)
-    last = pltpu.make_async_copy(data, out.at[:, 0:64, :], out_sems.at[16])
+    last = pltpu.make_async_copy(data, out.at[:, 0:64, :], out_sems.at[8])
     last.start()
     for send in sends:
         send.wait()
@@ -119,8 +111,8 @@
                 out[r // 2, k + h, r % 2] = blocks[h][r]
 
 
-def lift_other_kernel(first, rows, got, other, lists, cosine, sine, out):
-    row = rows_of((8, 128), 0)
+def lift_other_kernel(first, rows, other, lists, cosine, sine, out):
+    tile = lists[...].astype(BF)
     for k in range(0, 8, 2):
         lanes = [other_lanes(k), other_lanes(k + 1)]
         matrix = jnp.concatenate([other[k], other[k + 1]], axis=0)
@@ -128,19 +120,13 @@
         sines = [sine[:, at] for at in lanes]
         blocks = lift_halves(rows, matrix, cosines, sines)
         for h in range(2):
-            tran = got[k + h, 192:200, :].astype(F32)
-            tile = lists[...]
-            for j in range(4):
-                piece = tran[j // 2 : j // 2 + 1, 128 * (j % 2) : 128 * (j % 2) + 128]
-                tile = jnp.where(row == 4 + j, piece, tile)
-            tile = tile.astype(BF)
             for r in range(8):
                 out[r // 2, k + h, r % 2, :, 0:128] = first[r // 2, k + h, r % 2]
                 out[r // 2, k + h, r % 2, :, 128:256] = blocks[h][r]
                 out[r // 2, k + h, r % 2, :, 256:384] = tile
 
 
-def translate_kernel(got, out, table, codes, tran, real_acc, imag_acc):
+def translate_kernel(got, tran, out, table, codes, real_acc, imag_acc):
     def uppers(even, odd):
         low = rows_of(even.shape, 1) < 4
         return jnp.where(low, even, pltpu.roll(odd, 4, 1)).reshape(256, even.shape[2])
@@ -157,13 +143,8 @@
     even = got[:, 0, :, 256:384].astype(F32)
     odd = got[:, 1, :, 256:384].astype(F32)
     codes[...] = uppers(even, odd).astype(jnp.int32)
-    pieces = lowers(even, odd).astype(BF)
-    for j in range(4):
-        pick = rows_of((128, 256), 1) == rows_of((128, 256), 0) * 4 + j
-        part = nn_dot(pick.astype(F32).astype(BF), pieces)
-        tran[:, 128 * j : 128 * j + 128] = part.astype(BF)
     col = rows_of((256, 256), 1)
-    kinds = rows_of((256, 128), 1)
+    kinds = rows_of((256, 64), 1)
     for first in range(0, 16, 4):
         picks = [(col == codes[:, first + f : first + f + 1]).astype(F32) for f in range(4)]
         turns = [(kinds == codes[:, 16 + first + f : 17 + first + f]).astype(F32) for f in range(4)]
@@ -302,26 +283,31 @@
     sent = pl.pallas_call(
         radiate_kernel,
         name="radiate",
-        out_shape=jax.ShapeDtypeStruct((8, 200, 256), BF),
-        in_specs=[pl.BlockSpec(memory_space=pltpu.HBM)] * 4,
+        out_shape=jax.ShapeDtypeStruct((8, 192, 256), BF),
+        in_specs=[pl.BlockSpec(memory_space=pltpu.HBM)] * 3,
         out_specs=pl.BlockSpec(memory_space=pltpu.HBM),
         scratch_shapes=[
             pltpu.VMEM((4, 128, 128), BF),
             pltpu.VMEM((4, 2, 256, 128), BF),
             pltpu.VMEM((128, 256), BF),
-            pltpu.VMEM((2, 256), BF),
             pltpu.VMEM((8, 64, 256), BF),
-            pltpu.VMEM((8, 256), BF),
-            pltpu.SemaphoreType.DMA((7,)),
-            pltpu.SemaphoreType.DMA((17,)),
+            pltpu.SemaphoreType.DMA((6,)),
+            pltpu.SemaphoreType.DMA((9,)),
         ],
         compiler_params=params(60 * 1024 * 1024),
-    )(currents, radiate, interp, transl)
-    sent, mine = lax.optimization_barrier((sent, currents))
+    )(currents, radiate, interp)
+    sent, mine, slices = lax.optimization_barrier((sent, currents, transl))
     got = exchange(sent, "samp")
+    swap = []
+    for clus in range(64):
+        for samp in range(8):
+            taker = (clus // 16) * 16 + samp * 2 + clus % 2
+            swap.append((clus * 8 + samp, taker * 8 + (clus // 2) % 8))
+    tran = lax.ppermute(slices, ("clus", "samp"), swap).reshape(64, 512)
     low, high = halo(mine)
     near = near_field(mine, low, high, near_blocks, near_cols)
-    got, near = lax.optimization_barrier((got, near))
+    early = (got, near, tran, cosine, sine, lists)
+    got, near, tran, cosine, sine, lists = lax.optimization_barrier(early)
     half = got[:, 64:192]
     other = lax.ppermute(half, "clus", partner)
 
@@ -341,27 +327,26 @@
         lift_other_kernel,
         name="lift_other",
         out_shape=jax.ShapeDtypeStruct((4, 8, 2, 8, 384), BF),
-        in_specs=[VM] * 7,
-        out_specs=VM,
-        compiler_params=params(),
-    )(first, rows, got, other, lists, cosine, sine)
+        in_specs=[VM] * 6,
+        out_specs=VM,
+        compiler_params=params(),
+    )(first, rows, other, lists, cosine, sine)
     moved = exchange(sent.reshape(64, 8, 384), "clus")
 
     sent = pl.pallas_call(
         translate_kernel,
         name="translate",
         out_shape=jax.ShapeDtypeStruct((32, 2, 8, 256), BF),
-        in_specs=[VM],
+        in_specs=[VM, VM],
         out_specs=VM,
         scratch_shapes=[
             pltpu.VMEM((256, 512), BF),
             pltpu.VMEM((256, 128), jnp.int32),
-            pltpu.VMEM((128, 512), BF),
             pltpu.VMEM((256, 256), F32),
             pltpu.VMEM((256, 256), F32),
         ],
         compiler_params=params(),
-    )(moved.reshape(32, 2, 8, 384))
+    )(moved.reshape(32, 2, 8, 384), tran)
     moved = exchange(sent.reshape(64, 8, 256), "clus")
 
     sent = pl.pallas_call(

time: 107 us -> 114 us (1.065)
  blocking collectives: 60.6 us -> 67.6 us
  waiting for transfers between devices: 10.9 us -> 5.28 us
  starting transfers between devices: 19.3 us -> 24.8 us
    all_to_all x3, blocking collectives: 60.6 us -> 67.6 us  [body(): lax.all_to_all(x, axis, split_axis=0, concat_axis=0, tiled=True)]
    all_to_all x1, waiting for transfers between devices: 7.69 us -> 1.12 us  [body(): lax.all_to_all(x, axis, split_axis=0, concat_axis=0, tiled=True)]
    ppermute x1, starting transfers between devices: 2.11 us -> 6.13 us  [halo(): lax.ppermute(currents[24:32], 'clus', up)]
  transfers between devices with their start and end apart: 4 -> 5, of which waited for: 3 -> 4; matrix products, arithmetic and copies ran while one was open for 0% -> 0% of each run, Pallas kernels for 3% -> 3%
where the time goes in v6:
time: 114 us; the launch traced here: 113 us
  blocking collectives  67.6 us (59%)
  starting transfers between devices  24.8 us (22%)
  Pallas kernels  13.1 us (11%)
  waiting for transfers between devices  5.28 us (5%)
  local copies, waits for them, and re-layouts  2.1 us (2%)
    all_to_all x3, blocking collectives, body(): lax.all_to_all(x, axis, split_axis=0, concat_axis=0, tiled=True)  67.6 us
    all_to_all x1, starting transfers between devices, body(): lax.all_to_all(x, axis, split_axis=0, concat_axis=0, tiled=True)  7.65 us
    ppermute x1, starting transfers between devices, halo(): lax.ppermute(currents[24:32], 'clus', up)  6.13 us
    ppermute x1, starting transfers between devices, body(): other = lax.ppermute(half, 'clus', partner)  5.69 us
    ppermute x1, starting transfers between devices, halo(): lax.ppermute(currents[0:8], 'clus', down)  4.65 us
    pallas_call x1, Pallas kernels, body(): pl.pallas_call(radiate_kernel, name='radiate', out_shape=jax.ShapeDtypeSt...  2.99 us
    pallas_call x1, Pallas kernels, body(): pl.pallas_call(translate_kernel, name='translate', out_shape=jax.ShapeDty...  2.75 us
    pallas_call x1, Pallas kernels, near_field(): pl.pallas_call(near_kernel, name='near', out_shape=jax.ShapeDtypeStruct((...  2.3 us
  transfers between devices with their start and end apart: 5, of which 4 were waited for; matrix products, arithmetic and copies ran while one was open for 0% of the time, Pallas kernels for 3%

profile of v6, /device:TPU:1, one launch (start us, length us, event | category | flops | bytes accessed | tf_op | source)
XLA Modules:
  0.0 113.2 jit_solution(1506082836272093671)
XLA Ops:
  0.0 0.0 copy-start
  0.0 0.0 copy-start.9
  0.0 0.0 copy-start.8
  0.0 0.0 copy-start.5
  0.0 0.0 copy-start.6
  0.0 0.0 copy-start.7
  0.0 0.0 copy-start.4
  0.0 3.0 %radiate.1 = bf16[8,192,256]{2,1,0:T(8,128)(2,1)} custom-call(bf16[32,128,128]{2,1,0:T(8,128)(2,1)} %cur.2, bf16[4,2,256,128]{3,2,1,0:T(8,128)(2,1)} %rad.1, bf16[256,256]{1,0:T(8,128)(2,1)} %itp.1), custom_call_target="tpu_custom_call" | custom-call | tf_op jit(solution)/shard_map/radiate/pallas_call | solution.py:283
  3.0 7.7 %all-to-all-start = ((bf16[8,192,256]{2,1,0:T(8,128)(2,1)}), bf16[8,192,256]{2,1,0:T(8,128)(2,1)S(1)}, u32[]{:S(2)}, u32[]{:S(2)}) async-start(bf16[8,192,256]{2,1,0:T(8,128)(2,1)} %radiate.1), calls=%async_computation | async-start | bytes 1572864 | tf_op jit(solution)/shard_map/all_to_all | solution.py:277
  10.7 0.0 copy-done.9
  10.7 0.7 collective-permute-start.2
  11.4 0.0 copy-done
  11.4 4.7 %collective-permute-start.1 = (bf16[8,128,128]{2,1,0:T(8,128)(2,1)S(1)}, bf16[8,128,128]{2,1,0:T(8,128)(2,1)S(1)}, u32[]{:S(2)}, u32[]{:S(2)}) collective-permute-start(bf16[8,128,128]{2,1,0:T(8,128)(2,1)S(1)} %get-tuple-element.27), channel_id=1, source_target_pairs={{8,0},{16,8},{24,16},{32,24},{40,32},{48,40},{56,48},{64,56},{72,6... | collective-permute-start | bytes 786440 | tf_op jit(solution)/shard_map/ppermute | solution.py:246
  16.1 6.1 %collective-permute-start = (bf16[8,128,128]{2,1,0:T(8,128)(2,1)S(1)}, bf16[8,128,128]{2,1,0:T(8,128)(2,1)S(1)}, u32[]{:S(2)}, u32[]{:S(2)}) collective-permute-start(bf16[8,128,128]{2,1,0:T(8,128)(2,1)S(1)} %get-tuple-element.28), channel_id=1, source_target_pairs={{0,8},{8,16},{16,24},{24,32},{32,40},{40,48},{48,56},{56,64},{64,7... | collective-permute-start | bytes 786440 | tf_op jit(solution)/shard_map/ppermute | solution.py:246
  22.2 0.0 copy-done.8
  22.3 0.0 copy-done.5
  22.3 0.2 fusion.1
  22.5 0.0 copy-done.6
  22.5 0.0 copy-done.7
  22.5 0.1 pad_add_fusion.lists
  22.6 0.0 collective-permute-done.2
  22.6 0.0 copy-start.3
  22.6 2.0 %collective-permute-done.1.high = bf16[8,128,128]{2,1,0:T(8,128)(2,1)S(1)} collective-permute-done((bf16[8,128,128]{2,1,0:T(8,128)(2,1)S(1)}, bf16[8,128,128]{2,1,0:T(8,128)(2,1)S(1)}, u32[]{:S(2)}, u32[]{:S(2)}) %collective-permute-start.1) | collective-permute-done | bytes 262176 | tf_op jit(solution)/shard_map/ppermute | solution.py:246
  24.6 2.0 %collective-permute-done.low = bf16[8,128,128]{2,1,0:T(8,128)(2,1)S(1)} collective-permute-done((bf16[8,128,128]{2,1,0:T(8,128)(2,1)S(1)}, bf16[8,128,128]{2,1,0:T(8,128)(2,1)S(1)}, u32[]{:S(2)}, u32[]{:S(2)}) %collective-permute-start) | collective-permute-done | bytes 262176 | tf_op jit(solution)/shard_map/ppermute | solution.py:246
  26.7 0.0 copy-done.4
  26.7 0.0 copy-start.1
  26.7 1.7 %copy-done.1 = bf16[4,10,2,128,128]{4,3,2,1,0:T(8,128)(2,1)S(1)} copy-done((bf16[4,10,2,128,128]{4,3,2,1,0:T(8,128)(2,1)S(1)}, bf16[4,10,2,128,128]{4,3,2,1,0:T(8,128)(2,1)}, u32[]{:S(2)}) %copy-start.1) | copy-done | bytes 2621464
  28.4 2.3 %near.1 = f32[4,128,128]{2,1,0:T(8,128)S(1)} custom-call(s32[4,10]{1,0:T(4,128)S(1)} %copy-done.4, bf16[8,128,128]{2,1,0:T(8,128)(2,1)S(1)} %collective-permute-done.low, bf16[32,128,128]{2,1,0:T(8,128)(2,1)S(1)} %copy-done, bf16[8,128,128]{2,1,0:T(8,128)(2,1)S(1)} %collective-permute-done.1.high, bf16[4,10,2,128,128]{4,3,2,1,0:T(8,128)(2,1)S(1)} %copy-done.1), custom_call_target="tpu_custom_call" | custom-call | flops 168000000 | bytes 4600000 | tf_op jit(solution)/shard_map/near/pallas_call | solution.py:251
  30.7 1.1 all-to-all-done.got
  31.9 5.7 %collective-permute-start.3 = (bf16[8,128,256]{2,1,0:T(8,128)(2,1)S(1)}, bf16[8,128,256]{2,1,0:T(8,128)(2,1)S(1)}, u32[]{:S(2)}, u32[]{:S(2)}) collective-permute-start(bf16[8,128,256]{2,1,0:T(8,128)(2,1)S(1)} %slice.11.half), channel_id=1, source_target_pairs={{0,8},{8,0},{16,24},{24,16},{32,40},{40,32},{48,56},{56,48},{64,72... | collective-permute-start | bytes 1572872 | tf_op jit(solution)/shard_map/ppermute | solution.py:312
  37.6 0.0 copy-done.3
  37.6 1.4 %lift_own.1 = (bf16[4,8,2,8,128]{4,3,2,1,0:T(8,128)(2,1)S(1)}, bf16[512,256]{1,0:T(8,128)(2,1)S(1)}) custom-call(s32[32]{0:T(128)S(1)} %copy-done.3, bf16[8,192,256]{2,1,0:T(8,128)(2,1)S(1)} %all-to-all-done.got, f32[8,2048]{1,0:T(8,128)S(1)} %get-tuple-element.20.cosine, f32[8,2048]{1,0:T(8,128)S(1)} %get-tuple-element.21.sine), custom_call_target="tpu_custom_call" | custom-call | tf_op jit(solution)/shard_map/lift_own/pallas_call | solution.py:314
  38.9 0.1 collective-permute-done.3.other
  39.1 0.0 copy-start.2
  39.1 0.8 lift_other.1
  39.9 30.9 %all_to_all.20 = bf16[64,8,384]{2,1,0:T(8,128)(2,1)S(1)} all-to-all(bf16[64,8,384]{2,1,0:T(8,128)(2,1)S(1)} %bitcast.6), channel_id=1, replica_groups=mesh['clus'=64,'samp'=8] {'clus'}, dimensions={0} | all-to-all | bytes 786432 | tf_op jit(solution)/shard_map/all_to_all | solution.py:277
  70.8 2.8 %translate.1 = bf16[32,2,8,256]{3,2,1,0:T(8,128)(2,1)S(1)} custom-call(bf16[32,2,8,384]{3,2,1,0:T(8,128)(2,1)S(1)} %bitcast.7, bf16[64,512]{1,0:T(8,128)(2,1)S(1)} %bitcast.10), custom_call_target="tpu_custom_call" | custom-call | tf_op jit(solution)/shard_map/translate/pallas_call | solution.py:336
  73.5 18.0 %all_to_all.21 = bf16[64,8,256]{2,1,0:T(8,128)(2,1)S(1)} all-to-all(bf16[64,8,256]{2,1,0:T(8,128)(2,1)S(1)} %bitcast.9), channel_id=1, replica_groups=mesh['clus'=64,'samp'=8] {'clus'}, dimensions={0} | all-to-all | bytes 524288 | tf_op jit(solution)/shard_map/all_to_all | solution.py:277
  91.5 1.7 %descend.1 = bf16[8,64,256]{2,1,0:T(8,128)(2,1)S(1)} custom-call(s32[32]{0:T(128)S(1)} %copy-done.3, bf16[4,8,2,8,256]{4,3,2,1,0:T(8,128)(2,1)S(1)} %bitcast.8, bf16[8,128,256]{2,1,0:T(8,128)(2,1)S(1)} %slice.11.half, bf16[8,128,256]{2,1,0:T(8,128)(2,1)S(1)} %collective-permute-done.3.other, f32[8,2048]{1,0:T(8,128)S(1)} %get-tuple-element.20.cosine, ...), custom_call_target="tpu_custom_call" | custom-call | tf_op jit(solution)/shard_map/descend/pallas_call | solution.py:352
  93.3 18.8 %all_to_all.22.got = bf16[8,64,256]{2,1,0:T(8,128)(2,1)S(1)} all-to-all(bf16[8,64,256]{2,1,0:T(8,128)(2,1)S(1)} %descend.1), channel_id=1, replica_groups=mesh['clus'=64,'samp'=8] {'samp'}, dimensions={0} | all-to-all | bytes 524288 | tf_op jit(solution)/shard_map/all_to_all | solution.py:277
  112.0 0.0 copy-done.2
  112.0 1.1 %finish.1 = bf16[4,128,128]{2,1,0:T(8,128)(2,1)} custom-call(bf16[8,64,256]{2,1,0:T(8,128)(2,1)S(1)} %all_to_all.22.got, bf16[4,2,256,128]{3,2,1,0:T(8,128)(2,1)S(1)} %copy-done.2, f32[4,128,128]{2,1,0:T(8,128)S(1)} %near.1), custom_call_target="tpu_custom_call" | custom-call | tf_op jit(solution)/shard_map/finish/pallas_call | solution.py:366
  (5 shorter events, 0.1 us)
Async XLA Ops:
  0.0 11.4 %copy-start = (bf16[32,128,128]{2,1,0:T(8,128)(2,1)S(1)}, bf16[32,128,128]{2,1,0:T(8,128)(2,1)}, u32[]{:S(2)}) copy-start(bf16[32,128,128]{2,1,0:T(8,128)(2,1)} %cur.2) | copy-start | bytes 3145732
  0.0 10.7 %copy-start.9 = (bf16[64,2,256]{2,1,0:T(2,128)(2,1)S(1)}, bf16[64,2,256]{2,1,0:T(2,128)(2,1)}, u32[]{:S(2)}) copy-start(bf16[64,2,256]{2,1,0:T(2,128)(2,1)} %param.21) | copy-start | bytes 196612
  0.0 22.2 %copy-start.8 = (s32[4,16]{1,0:T(4,128)S(1)}, s32[4,16]{1,0:T(4,128)}, u32[]{:S(2)}) copy-start(s32[4,16]{1,0:T(4,128)} %param.20) | copy-start | bytes 772
  0.0 22.2 %copy-start.5 = (f32[8,2048]{1,0:T(8,128)S(1)}, f32[8,2048]{1,0:T(8,128)}, u32[]{:S(2)}) copy-start(f32[8,2048]{1,0:T(8,128)} %param.17) | copy-start | bytes 196612
  0.0 22.5 %copy-start.6 = (s32[4,16]{1,0:T(4,128)S(1)}, s32[4,16]{1,0:T(4,128)}, u32[]{:S(2)}) copy-start(s32[4,16]{1,0:T(4,128)} %param.19) | copy-start | bytes 772
  0.0 22.5 %copy-start.7 = (s32[4,16]{1,0:T(4,128)S(1)}, s32[4,16]{1,0:T(4,128)}, u32[]{:S(2)}) copy-start(s32[4,16]{1,0:T(4,128)} %param.18) | copy-start | bytes 772
  0.0 26.6 %copy-start.4 = (s32[4,10]{1,0:T(4,128)S(1)}, s32[4,10]{1,0:T(4,128)}, u32[]{:S(2)}) copy-start(s32[4,10]{1,0:T(4,128)} %cols.1) | copy-start | bytes 484
  3.0 28.8 %all-to-all-start = ((bf16[8,192,256]{2,1,0:T(8,128)(2,1)}), bf16[8,192,256]{2,1,0:T(8,128)(2,1)S(1)}, u32[]{:S(2)}, u32[]{:S(2)}) async-start(bf16[8,192,256]{2,1,0:T(8,128)(2,1)} %radiate.1), calls=%async_computation | async-start | bytes 1572864 | tf_op jit(solution)/shard_map/all_to_all | solution.py:277
  10.7 11.9 %collective-permute-start.2 = (bf16[64,2,256]{2,1,0:T(2,128)(2,1)S(1)}, bf16[64,2,256]{2,1,0:T(2,128)(2,1)S(1)}, u32[]{:S(2)}, u32[]{:S(2)}) collective-permute-start(bf16[64,2,256]{2,1,0:T(2,128)(2,1)S(1)} %copy-done.9), channel_id=1, source_target_pairs={{0,0},{1,16},{2,32},{3,48},{4,64},{5,80},{6,96},{7,112},{8,8},{9,2... | collective-permute-start | bytes 196616 | tf_op jit(solution)/shard_map/ppermute | solution.py:306
  11.4 13.2 %collective-permute-start.1 = (bf16[8,128,128]{2,1,0:T(8,128)(2,1)S(1)}, bf16[8,128,128]{2,1,0:T(8,128)(2,1)S(1)}, u32[]{:S(2)}, u32[]{:S(2)}) collective-permute-start(bf16[8,128,128]{2,1,0:T(8,128)(2,1)S(1)} %get-tuple-element.27), channel_id=1, source_target_pairs={{8,0},{16,8},{24,16},{32,24},{40,32},{48,40},{56,48},{64,56},{72,6... | collective-permute-start | bytes 786440 | tf_op jit(solution)/shard_map/ppermute | solution.py:246
  16.1 10.6 %collective-permute-start = (bf16[8,128,128]{2,1,0:T(8,128)(2,1)S(1)}, bf16[8,128,128]{2,1,0:T(8,128)(2,1)S(1)}, u32[]{:S(2)}, u32[]{:S(2)}) collective-permute-start(bf16[8,128,128]{2,1,0:T(8,128)(2,1)S(1)} %get-tuple-element.28), channel_id=1, source_target_pairs={{0,8},{8,16},{16,24},{24,32},{32,40},{40,48},{48,56},{56,64},{64,7... | collective-permute-start | bytes 786440 | tf_op jit(solution)/shard_map/ppermute | solution.py:246
  22.6 14.9 %copy-start.3 = (s32[32]{0:T(128)S(1)}, s32[32]{0:T(128)}, u32[]{:S(2)}) copy-start(s32[32]{0:T(128)} %slots.3) | copy-start | bytes 388
  26.7 1.7 %copy-start.1 = (bf16[4,10,2,128,128]{4,3,2,1,0:T(8,128)(2,1)S(1)}, bf16[4,10,2,128,128]{4,3,2,1,0:T(8,128)(2,1)}, u32[]{:S(2)}) copy-start(bf16[4,10,2,128,128]{4,3,2,1,0:T(8,128)(2,1)} %blocks.1) | copy-start | bytes 7864324
  31.9 7.2 %collective-permute-start.3 = (bf16[8,128,256]{2,1,0:T(8,128)(2,1)S(1)}, bf16[8,128,256]{2,1,0:T(8,128)(2,1)S(1)}, u32[]{:S(2)}, u32[]{:S(2)}) collective-permute-start(bf16[8,128,256]{2,1,0:T(8,128)(2,1)S(1)} %slice.11.half), channel_id=1, source_target_pairs={{0,8},{8,0},{16,24},{24,16},{32,40},{40,32},{48,56},{56,48},{64,72... | collective-permute-start | bytes 1572872 | tf_op jit(solution)/shard_map/ppermute | solution.py:312
  39.1 72.9 %copy-start.2 = (bf16[4,2,256,128]{3,2,1,0:T(8,128)(2,1)S(1)}, bf16[4,2,256,128]{3,2,1,0:T(8,128)(2,1)}, u32[]{:S(2)}) copy-start(bf16[4,2,256,128]{3,2,1,0:T(8,128)(2,1)} %rad.1) | copy-start | bytes 1572868
